TPU v7x, 32 devices: a whole 2x2x4 slice. The times are simulated.
32 devices in a mesh: ctx: 8 (over z, x), head: 4 (over y, core).
Axes of the slice: x: 2, y: 2, z: 4, core: 2. Of those that a mesh axis runs over, the one named last changes fastest.
Arguments:
- x_load: bfloat16 [2048, 16384], P(('ctx', 'head')), may hold values from -6 to 6
- z_load: bfloat16 [2048, 16384], P(('ctx', 'head')), may hold values from -6 to 6
- b_load: bfloat16 [2048, 1024], P(('ctx', 'head')), may hold values from -6 to 6
- c_load: bfloat16 [2048, 1024], P(('ctx', 'head')), may hold values from -0.5 to 0.5
- dt_load: bfloat16 [2048, 128], P(('ctx', 'head')), may hold values from -3 to 3
- dt_bias: float32 [128], P('head'), may hold values from -4.5 to -3.5
- a_log: float32 [128], P('head'), may hold values from -12 to 2
- skip_gain: float32 [128], P('head'), may hold values from 0.5 to 2
- norm_gain: bfloat16 [16384], P('head'), may hold values from 0.5 to 1.5
- doc_lengths: int32 [16], replicated, may hold values from 1 to 1024, 2048 in all
- anchor: int32 [2048], P(('ctx', 'head')), may hold values from 0 to 2047, as said below
Outputs:
- mixed: bfloat16 [2048, 16384], P('ctx', 'head')
Inputs may be any that keep to these rules, and one draw needn't show every extreme that they name: `anchor`: a permutation of the positions; each loader shard of 64 rows holds between 4 and 12 rows for each owner's block of 256 positions, and 12 for some owner.
All inputs are finite; a program needn't handle non-finite values.
Results may differ from a plain program's by a relative error of at most 0.0032.
Values may be sent and summed in bfloat16 or wider, within the bound.
No kernel may reach another device: no remote copies, remote signals or barrier semaphores. Data moves between devices by JAX's collectives and lax.ppermute only.
A program may use at most 192 MiB of HBM per device.

v0:
```python
import jax
import jax.numpy as jnp
from jax import lax
from jax.sharding import PartitionSpec as P

STATE = 128
SPAN = 256


def entering(part, axis, combine, identity):
    place = lax.axis_index(axis)
    gathered = jax.tree.map(lambda a: lax.all_gather(a, axis), part)
    state = jax.tree.map(lambda a, e: jnp.zeros_like(a) + jnp.asarray(e, a.dtype), part, identity)

    def one(turn, state):
        return combine(
            state, jax.tree.map(lambda a: lax.dynamic_index_in_dim(a, turn, 0, False), gathered)
        )

    return lax.fori_loop(0, place, one, state)


def doc_index(positions, starts):
    return jnp.sum((starts[None, :] <= positions[:, None]).astype(jnp.int32), axis=1) - 1


def block_parts(x_block, b_block, c_block, dt_block, log_block, doc_ids, doc_before):
    span_len = x_block.shape[0]
    head_count = x_block.shape[1]
    head_width = x_block.shape[2]
    group_count = b_block.shape[1]
    state_width = b_block.shape[2]
    per_group = head_count // group_count
    cum_log = jnp.cumsum(log_block, axis=0)
    lower_mask = jnp.arange(span_len)[:, None] >= jnp.arange(span_len)[None, :]
    keep_mask = lower_mask & (doc_ids[:, None] == doc_ids[None, :])
    cum_heads = cum_log.T
    exponent = jnp.where(keep_mask[None], cum_heads[:, :, None] - cum_heads[:, None, :], -jnp.inf)
    decay = jnp.exp(exponent)
    scores = jnp.einsum("tgn,sgn->gts", c_block, b_block, preferred_element_type=jnp.float32)
    scores = jnp.repeat(scores, per_group, axis=0)
    weights = (scores * decay * dt_block.T[:, None, :]).astype(jnp.bfloat16)
    intra_part = jnp.einsum("hts,shp->thp", weights, x_block, preferred_element_type=jnp.float32)
    tail_weight = (
        jnp.where((doc_ids == doc_ids[-1])[:, None], jnp.exp(cum_log[-1][None, :] - cum_log), 0.0)
        * dt_block
    )
    weighted_b = (
        b_block.astype(jnp.float32)[:, :, None, :]
        * tail_weight.reshape(span_len, group_count, per_group)[:, :, :, None]
    ).astype(jnp.bfloat16)
    local_state = jnp.einsum(
        "sgkn,sgkp->gknp",
        weighted_b,
        x_block.reshape(span_len, group_count, per_group, head_width),
        preferred_element_type=jnp.float32,
    )
    local_state = local_state.reshape(head_count, state_width, head_width)
    entry_decay = jnp.where((doc_ids == doc_before)[:, None], jnp.exp(cum_log), 0.0)
    return (intra_part, local_state, entry_decay)


def cross_term(c_block, state_low, entry_decay):
    span_len, group_count, state_width = c_block.shape
    head_count, _, head_width = state_low.shape
    grouped = state_low.reshape(group_count, head_count // group_count, state_width, head_width)
    cross_part = jnp.einsum("tgn,gknp->tgkp", c_block, grouped, preferred_element_type=jnp.float32)
    return cross_part.reshape(span_len, head_count, head_width) * entry_decay[:, :, None]


def combine_states(earlier, later):
    return (earlier[0] * later[0], later[0][:, None, None] * earlier[1] + later[1])


def place_rows(received, landing, block_rows):
    flattened = received.reshape((-1, received.shape[-1]))
    blank_buffer = jnp.zeros((block_rows, flattened.shape[1]), flattened.dtype)
    return blank_buffer.at[landing].set(flattened, mode="drop")


def body(
    x_load,
    z_load,
    b_load,
    c_load,
    dt_load,
    dt_bias,
    a_log,
    skip_gain,
    norm_gain,
    doc_lengths,
    anchor,
):
    load_rows = anchor.shape[0]
    owners = lax.axis_size("ctx")
    columns = lax.axis_size("head")
    block_rows = load_rows * columns
    capacity = 3 * load_rows // (2 * owners)
    own_index = lax.axis_index("ctx")
    owner_of = anchor // block_rows
    one_hot = (owner_of[:, None] == jnp.arange(owners, dtype=jnp.int32)[None, :]).astype(jnp.int32)
    rank_in = jnp.sum(jnp.cumsum(one_hot, axis=0) * one_hot, axis=1) - 1

    def pack(values):
        split_cols = values.reshape(load_rows, columns, values.shape[1] // columns)
        blank_buffer = jnp.zeros((owners, columns, capacity, split_cols.shape[2]), values.dtype)
        return blank_buffer.at[owner_of, :, rank_in].set(split_cols)

    everyone = lax.all_gather(anchor, ("ctx", "head"), axis=0, tiled=True).reshape(
        owners * columns, load_rows
    )
    is_mine = everyone // block_rows == own_index
    arrival = jnp.cumsum(is_mine.astype(jnp.int32), axis=1) - 1
    loader_ids = jnp.arange(owners * columns, dtype=jnp.int32)[:, None]
    slot_of = jnp.where(is_mine, loader_ids * capacity + arrival, owners * columns * capacity)
    landing = jnp.full((owners * columns * capacity,), block_rows, jnp.int32)
    landing = landing.at[slot_of.reshape(-1)].set(
        (everyone - own_index * block_rows).reshape(-1), mode="drop"
    )
    pack_x = pack(x_load)
    pack_z = pack(z_load)
    pack_b = pack(b_load)
    pack_c = pack(c_load)
    pack_dt = pack(dt_load)
    lead = owners * columns
    arrived = (
        lax.all_to_all(
            pack_x.reshape((lead,) + pack_x.shape[2:]),
            ("ctx", "head"),
            split_axis=0,
            concat_axis=0,
            tiled=True,
        ),
        lax.all_to_all(
            pack_z.reshape((lead,) + pack_z.shape[2:]),
            ("ctx", "head"),
            split_axis=0,
            concat_axis=0,
            tiled=True,
        ),
        lax.all_to_all(
            pack_b.reshape((lead,) + pack_b.shape[2:]),
            ("ctx", "head"),
            split_axis=0,
            concat_axis=0,
            tiled=True,
        ),
        lax.all_to_all(
            pack_c.reshape((lead,) + pack_c.shape[2:]),
            ("ctx", "head"),
            split_axis=0,
            concat_axis=0,
            tiled=True,
        ),
        lax.all_to_all(
            pack_dt.reshape((lead,) + pack_dt.shape[2:]),
            ("ctx", "head"),
            split_axis=0,
            concat_axis=0,
            tiled=True,
        ),
    )
    x_rows = place_rows(arrived[0], landing, block_rows)
    z_rows = place_rows(arrived[1], landing, block_rows)
    b_rows = place_rows(arrived[2], landing, block_rows)
    c_rows = place_rows(arrived[3], landing, block_rows)
    dt_rows = place_rows(arrived[4], landing, block_rows)
    heads_local = dt_bias.shape[0]
    groups_local = b_rows.shape[1] // STATE
    head_width = x_rows.shape[1] // heads_local
    span_count = block_rows // SPAN
    step_size = jax.nn.softplus(dt_rows.astype(jnp.float32) + dt_bias[None, :])
    log_step = -step_size * jnp.exp(a_log)[None, :]
    starts = jnp.cumsum(doc_lengths) - doc_lengths
    positions = own_index * block_rows + jnp.arange(block_rows, dtype=jnp.int32)
    doc_ids = doc_index(positions, starts).reshape(span_count, SPAN)
    first_positions = own_index * block_rows + jnp.arange(span_count, dtype=jnp.int32) * SPAN - 1
    doc_before = doc_index(first_positions, starts)
    x_blocks = x_rows.reshape(span_count, SPAN, heads_local, head_width)
    b_blocks = b_rows.reshape(span_count, SPAN, groups_local, STATE)
    c_blocks = c_rows.reshape(span_count, SPAN, groups_local, STATE)
    intra_part, local_state, entry_decay = jax.vmap(block_parts)(
        x_blocks,
        b_blocks,
        c_blocks,
        step_size.reshape(span_count, SPAN, heads_local),
        log_step.reshape(span_count, SPAN, heads_local),
        doc_ids,
        doc_before,
    )
    carry_factor = entry_decay[:, -1, :]

    def fold_block(running, item):
        running_state, running_factor = running
        block_factor, block_state = item
        return (
            (
                block_factor[:, None, None] * running_state + block_state,
                running_factor * block_factor,
            ),
            (running_state, running_factor),
        )

    zero_state = jnp.zeros((heads_local, STATE, head_width), jnp.float32)
    unit_factor = jnp.ones((heads_local,), jnp.float32)
    (total_state, total_factor), (prefix_states, prefix_factors) = lax.scan(
        fold_block, (zero_state, unit_factor), (carry_factor, local_state)
    )
    incoming = entering(
        (total_factor, total_state), "ctx", combine_states, (unit_factor, zero_state)
    )[1]
    state_in = prefix_factors[:, :, None, None] * incoming[None] + prefix_states
    state_low = state_in.astype(jnp.bfloat16)
    cross_part = jax.vmap(cross_term)(c_blocks, state_low, entry_decay)
    mixed_out = intra_part + cross_part + skip_gain[None, None, :, None] * x_blocks
    gated = mixed_out.reshape(block_rows, -1) * jax.nn.silu(z_rows.astype(jnp.float32))
    grouped = gated.reshape(block_rows, groups_local, -1)
    inv_rms = lax.rsqrt(jnp.mean(grouped * grouped, axis=-1, keepdims=True) + 1e-05)
    result_rows = (grouped * inv_rms).reshape(block_rows, -1) * norm_gain.astype(jnp.float32)[
        None, :
    ]
    return result_rows.astype(jnp.bfloat16)


def solution(mesh):
    in_specs = (
        P(("ctx", "head"), None),
        P(("ctx", "head"), None),
        P(("ctx", "head"), None),
        P(("ctx", "head"), None),
        P(("ctx", "head"), None),
        P("head"),
        P("head"),
        P("head"),
        P("head"),
        P(),
        P(("ctx", "head")),
    )
    out_specs = P("ctx", "head")
    return jax.shard_map(body, mesh=mesh, in_specs=in_specs, out_specs=out_specs, check_vma=False)
```

profile of v0, /device:TPU:27, one launch (start us, length us, event | category | flops | bytes accessed | tf_op | source)
XLA Modules:
  0.0 567.1 jit_solution(9511419967029940728)
XLA Ops:
  9.4 3.1 scatter_fusion.3
  13.3 6.1 %all-to-all-start.3 = ((bf16[32,2,192]{2,1,0:T(2,128)(2,1)}), bf16[32,2,192]{2,1,0:T(2,128)(2,1)S(1)}, u32[]{:S(2)}, u32[]{:S(2)}) async-start(bf16[32,2,192]{2,1,0:T(2,128)(2,1)} %reshape.572), calls=%async_computation.3 | async-start | bytes 65536 | tf_op jit(solution)/shard_map/all_to_all | solution.py:155
  20.5 3.1 scatter_fusion.2
  24.4 5.8 %all-to-all-start.2 = ((bf16[32,12,256]{2,1,0:T(8,128)(2,1)}), bf16[32,12,256]{2,1,0:T(8,128)(2,1)S(1)}, u32[]{:S(2)}, u32[]{:S(2)}) async-start(bf16[32,12,256]{2,1,0:T(8,128)(2,1)} %bitcast.10), calls=%async_computation.2 | async-start | bytes 524288 | tf_op jit(solution)/shard_map/all_to_all | solution.py:141
  30.3 2.8 reshape.480
  33.0 1.5 broadcast.284.clone
  34.6 7.3 %scatter_fusion = bf16[8,4,12,4096]{3,1,2,0:T(4,128)(2,1)S(1)} fusion(bf16[8,4,12,4096]{3,1,2,0:T(4,128)(2,1)S(1)} %broadcast.284.clone, s32[64]{0:T(128)S(1)} %fusion.37, bf16[64,4,4096]{2,1,0:T(4,128)(2,1)} %reshape.480), kind=kCustom, calls=%fused_computation.1 | custom fusion | bytes 6291968 | tf_op jit(solution)/shard_map/scatter | solution.py:107
  41.9 3.9 copy.213
  45.9 5.9 %all-to-all-start = ((bf16[32,12,4096]{2,1,0:T(8,128)(2,1)}), bf16[32,12,4096]{2,1,0:T(8,128)(2,1)}, u32[]{:S(2)}, u32[]{:S(2)}) async-start(bf16[32,12,4096]{2,1,0:T(8,128)(2,1)} %bitcast.112), calls=%async_computation | async-start | bytes 8388608 | tf_op jit(solution)/shard_map/all_to_all | solution.py:127
  52.1 111.7 %all-reduce = s32[2048]{0:T(1024)S(1)} all-reduce(s32[2048]{0:T(1024)S(1)} %dynamic-update-slice), channel_id=1, replica_groups=mesh['ctx'=8,'head'=4] {'ctx','head'}, use_global_device_ids=true, to_apply=%add | all-reduce | flops 2048 | bytes 16384
  166.5 8.0 %scatter_custom_fusion = s32[384]{0:T(512)S(1)} fusion(s32[2048]{0:T(1024)S(1)} %get-tuple-element.95, s32[2048]{0:T(1024)S(1)} %get-tuple-element.94, s32[]{:T(128)} %constant.106.clone.1), kind=kCustom, calls=%fused_computation.88 | custom fusion | bytes 1540 | tf_op jit(solution)/shard_map/scatter | solution.py:117
  175.3 1.7 scatter_custom_fusion.8
  178.5 1.9 scatter_custom_fusion.6
  180.6 5.6 reshape.488
  186.2 6.6 %scatter_custom_fusion.2 = bf16[256,4096]{1,0:T(8,128)(2,1)S(1)} fusion(s32[384]{0:T(512)S(1)} %compare_select_fusion.2, bf16[384,4096]{1,0:T(8,128)(2,1)} %reshape.488, bf16[]{:T(256)} %constant.105.clone.1), kind=kCustom, calls=%fused_computation.34 | custom fusion | bytes 2097664 | tf_op jit(solution)/shard_map/scatter | solution.py:78
  193.3 1.4 fusion.8
  194.7 1.5 bitcast_add_fusion.1
  196.4 3.1 scatter_fusion.1
  200.3 7.8 %all-to-all-start.1 = ((bf16[32,12,256]{2,1,0:T(8,128)(2,1)}), bf16[32,12,256]{2,1,0:T(8,128)(2,1)S(1)}, u32[]{:S(2)}, u32[]{:S(2)}) async-start(bf16[32,12,256]{2,1,0:T(8,128)(2,1)} %bitcast.8), calls=%async_computation.1 | async-start | bytes 524288 | tf_op jit(solution)/shard_map/all_to_all | solution.py:148
  208.1 4.7 reshape.536
  212.8 3.2 broadcast.284.clone.1
  216.1 10.7 %scatter_fusion.4 = bf16[8,4,12,4096]{3,1,2,0:T(4,128)(2,1)} fusion(bf16[8,4,12,4096]{3,1,2,0:T(4,128)(2,1)} %broadcast.284.clone.1, s32[64]{0:T(128)S(1)} %fusion.37, bf16[64,4,4096]{2,1,0:T(4,128)(2,1)} %reshape.536), kind=kCustom, calls=%fused_computation.9 | custom fusion | bytes 6291968 | tf_op jit(solution)/shard_map/scatter | solution.py:107
  226.8 5.8 %copy.220 = bf16[8,4,12,4096]{3,2,1,0:T(8,128)(2,1)} copy(bf16[8,4,12,4096]{3,1,2,0:T(4,128)(2,1)} %scatter_fusion.4) | data formatting | bytes 6291456 | tf_op jit(solution)/shard_map/reshape | solution.py:135
  232.6 5.9 %all-to-all-start.4 = ((bf16[32,12,4096]{2,1,0:T(8,128)(2,1)}), bf16[32,12,4096]{2,1,0:T(8,128)(2,1)}, u32[]{:S(2)}, u32[]{:S(2)}) async-start(bf16[32,12,4096]{2,1,0:T(8,128)(2,1)} %bitcast.113), calls=%async_computation.4 | async-start | bytes 8388608 | tf_op jit(solution)/shard_map/all_to_all | solution.py:134
  238.9 188.5 %all-gather = f32[8,1,32]{2,1,0:T(1,128)S(1)} all-gather(f32[1,1,32]{2,1,0:T(1,128)S(1)} %get-tuple-element.91), channel_id=2, replica_groups=mesh['ctx'=8,'head'=4] {'ctx'}, dimensions={0}, use_global_device_ids=true | all-gather | bytes 1152 | tf_op jit(solution)/shard_map/all_gather | solution.py:12
  427.4 2.4 scatter_custom_fusion.4
  430.2 3.6 fusion.1
  433.8 2.9 copy.203
  436.7 2.5 copy.214
  439.2 4.0 reshape.544
  443.2 6.3 %scatter_custom_fusion.10 = bf16[256,4096]{1,0:T(8,128)(2,1)} fusion(s32[384]{0:T(512)S(1)} %compare_select_fusion.2, bf16[384,4096]{1,0:T(8,128)(2,1)S(1)} %reshape.544, bf16[]{:T(256)} %constant.105.clone.1), kind=kCustom, calls=%fused_computation.32 | custom fusion | bytes 2097154 | tf_op jit(solution)/shard_map/scatter | solution.py:78
  449.4 58.5 %all-gather.3.cloned.1.call-done = f32[8,32,128,128]{3,2,1,0:T(8,128)} async-done(((f32[1,32,128,128]{3,2,1,0:T(8,128)}), f32[8,32,128,128]{3,2,1,0:T(8,128)}) %all-gather.3.cloned.1.call-update) | async-done | bytes 16777232 | tf_op jit(solution)/shard_map/all_gather | solution.py:12
  508.2 14.2 %while.3 = (s32[]{:T(128)}, f32[32,128,128]{2,1,0:T(8,128)S(1)}, s32[]{:T(128)}, f32[8,32]{1,0:T(8,128)S(1)}, f32[8,32,128,128]{3,2,1,0:T(8,128)}, /*index=5*/s32[]{:T(128)}, s32[]{:T(128)}, s32[]{:T(128)}) while((s32[]{:T(128)}, f32[32,128,128]{2,1,0:T(8,128)S(1)}, s32[]{:T(128)}, f32[8,32]{1,0:T(8,128)S(1)}, ...), condition=%wide.region_18.19_spmd, body=%wide.region_17.18_spmd.sunk | while | flops 1048581 | bytes 6291967 | solution.py:20
  508.2 2.0 bitcast_add_fusion.6
  510.3 2.0 bitcast_add_fusion.6
  512.3 2.0 bitcast_add_fusion.6
  514.3 2.0 bitcast_add_fusion.6
  516.4 2.0 bitcast_add_fusion.6
  518.4 2.0 bitcast_add_fusion.6
  520.4 2.0 bitcast_add_fusion.6
  524.6 1.3 copy-done.2
  525.9 5.2 fusion.7
  531.1 5.8 %copy.206 = f32[256,4096]{1,0:T(8,128)} copy(f32[256,4096]{0,1:T(8,128)} %bitcast.117) | data formatting | bytes 8388608 | tf_op jit(solution)/shard_map/reshape | solution.py:216
  536.9 5.3 fusion.38
  542.2 6.6 %mul.197 = f32[256,2,2048]{2,1,0:T(2,128)} reshape(f32[256,4096]{1,0:T(8,128)} %fusion.38) | data formatting | bytes 8388608 | tf_op jit(solution)/shard_map/mul | solution.py:218
  548.7 3.4 reduce_sum.39
  553.3 3.9 copy.227
  557.2 2.9 multiply_convert_fusion
  (109 shorter events, 15.8 us)
Async XLA Ops:
  6.5 23.7 %copy-start.4 = (bf16[64,16384]{1,0:T(8,128)(2,1)S(1)}, bf16[64,16384]{1,0:T(8,128)(2,1)}, u32[]{:S(2)}) copy-start(bf16[64,16384]{1,0:T(8,128)(2,1)} %param.13) | copy-start | bytes 6291460
  13.3 11.1 %all-to-all-start.3 = ((bf16[32,2,192]{2,1,0:T(2,128)(2,1)}), bf16[32,2,192]{2,1,0:T(2,128)(2,1)S(1)}, u32[]{:S(2)}, u32[]{:S(2)}) async-start(bf16[32,2,192]{2,1,0:T(2,128)(2,1)} %reshape.572), calls=%async_computation.3 | async-start | bytes 65536 | tf_op jit(solution)/shard_map/all_to_all | solution.py:155
  24.4 21.5 %all-to-all-start.2 = ((bf16[32,12,256]{2,1,0:T(8,128)(2,1)}), bf16[32,12,256]{2,1,0:T(8,128)(2,1)S(1)}, u32[]{:S(2)}, u32[]{:S(2)}) async-start(bf16[32,12,256]{2,1,0:T(8,128)(2,1)} %bitcast.10), calls=%async_computation.2 | async-start | bytes 524288 | tf_op jit(solution)/shard_map/all_to_all | solution.py:141
  45.9 6.0 %copy-start.10 = (s32[64]{0:T(128)S(1)}, s32[64]{0:T(128)}, u32[]{:S(2)}) copy-start(s32[64]{0:T(128)} %param.23) | copy-start | bytes 772
  45.9 118.4 %copy-start.11 = (f32[32]{0:T(128)S(1)}, f32[32]{0:T(128)}, u32[]{:S(2)}) copy-start(f32[32]{0:T(128)} %param.19) | copy-start | bytes 388
  45.9 118.4 %copy-start.8 = (s32[16]{0:T(128)S(1)}, s32[16]{0:T(128)}, u32[]{:S(2)}) copy-start(s32[16]{0:T(128)} %param.22) | copy-start | bytes 196
  45.9 131.2 %copy-start.7 = (f32[32]{0:T(128)S(1)}, f32[32]{0:T(128)}, u32[]{:S(2)}) copy-start(f32[32]{0:T(128)} %param.18) | copy-start | bytes 388
  45.9 134.7 %all-to-all-start = ((bf16[32,12,4096]{2,1,0:T(8,128)(2,1)}), bf16[32,12,4096]{2,1,0:T(8,128)(2,1)}, u32[]{:S(2)}, u32[]{:S(2)}) async-start(bf16[32,12,4096]{2,1,0:T(8,128)(2,1)} %bitcast.112), calls=%async_computation | async-start | bytes 8388608 | tf_op jit(solution)/shard_map/all_to_all | solution.py:127
  51.8 456.2 %all-gather.3.cloned.1.call-start = ((), (), s32[]{:S(2)}) async-start(), calls=%async_computation.5 | async-start | bytes 18874368 | tf_op jit(solution)/shard_map/all_gather | solution.py:12
  194.7 1.6 copy-start.5
  200.3 32.3 %all-to-all-start.1 = ((bf16[32,12,256]{2,1,0:T(8,128)(2,1)}), bf16[32,12,256]{2,1,0:T(8,128)(2,1)S(1)}, u32[]{:S(2)}, u32[]{:S(2)}) async-start(bf16[32,12,256]{2,1,0:T(8,128)(2,1)} %bitcast.8), calls=%async_computation.1 | async-start | bytes 524288 | tf_op jit(solution)/shard_map/all_to_all | solution.py:148
  232.6 5.9 %copy-start.6 = (bf16[4096]{0:T(1024)(128)(2,1)S(1)}, bf16[4096]{0:T(1024)(128)(2,1)}, u32[]{:S(2)}) copy-start(bf16[4096]{0:T(1024)(128)(2,1)} %param.21) | copy-start | bytes 24580
  232.6 206.6 %all-to-all-start.4 = ((bf16[32,12,4096]{2,1,0:T(8,128)(2,1)}), bf16[32,12,4096]{2,1,0:T(8,128)(2,1)}, u32[]{:S(2)}, u32[]{:S(2)}) async-start(bf16[32,12,4096]{2,1,0:T(8,128)(2,1)} %bitcast.113), calls=%async_computation.4 | async-start | bytes 8388608 | tf_op jit(solution)/shard_map/all_to_all | solution.py:134
  522.4 2.2 copy-start.3
  522.6 3.3 copy-start.2
  522.6 3.3 copy-start.9
  531.1 5.8 %copy-start.1 = (bf16[256,4096]{1,0:T(8,128)(2,1)S(1)}, bf16[256,4096]{1,0:T(8,128)(2,1)}, u32[]{:S(2)}) copy-start(bf16[256,4096]{1,0:T(8,128)(2,1)} %scatter_custom_fusion.10) | copy-start | bytes 6291460
  553.3 3.9 copy-start
Sparse Core Ops, SparseCore 0:
  196.4 311.5 all-gather.2
where the time goes:
time: 576 us; the launch traced here: 567 us
  blocking collectives  300 us (52%)
  local copies, waits for them, and re-layouts  119 us (21%)
  waiting for transfers between devices  58.6 us (10%)
  other arithmetic  35.4 us (6%)
  starting transfers between devices  31.6 us (5%)
  between operations  14.8 us (3%)
  matrix products  7.57 us (1%)
    all_gather x1, blocking collectives, entering(): gathered = jax.tree.map(lambda a: lax.all_gather(a, axis), part)  188 us
    unnamed x1, blocking collectives  112 us
    all_gather x1, waiting for transfers between devices, entering(): gathered = jax.tree.map(lambda a: lax.all_gather(a, axis), part)  58.5 us
    scatter x6, local copies, waits for them, and re-layouts, pack(): return blank_buffer.at[owner_of, :, rank_in].set(split_cols)  27.5 us
    scatter x7, local copies, waits for them, and re-layouts, place_rows(): return blank_buffer.at[landing].set(flattened, mode='drop')  19.1 us
    add x7, other arithmetic, combine_states(): later[0][:, None, None] * earlier[1] + later[1]  13.9 us
  transfers between devices with their start and end apart: 6, of which 1 were waited for; matrix products, arithmetic and copies ran while one was open for 15% of the time, Pallas kernels for 0%

commit v1 on v0

v1 whole, which is shorter than its diff:
```python
import functools

import jax
import jax.numpy as jnp
from jax import lax
from jax.experimental import pallas as pl
from jax.experimental.pallas import tpu as pltpu
from jax.sharding import PartitionSpec as P

SPAN = 256
LANES = 128
ROWS = 8
F32 = jnp.float32
BF16 = jnp.bfloat16
BOTH = ("ctx", "head")
VMEM = pl.BlockSpec(memory_space=pltpu.VMEM)
SMEM = pl.BlockSpec(memory_space=pltpu.SMEM)
PARAMS = pltpu.CompilerParams(vmem_limit_bytes=56 * 1024 * 1024)


def iota(shape, dim):
    return lax.broadcasted_iota(jnp.int32, shape, dim)


def dot(left, right):
    return jnp.dot(left, right, preferred_element_type=F32)


def onehot(mask):
    return jnp.where(mask, 1.0, 0.0).astype(BF16)


def send_onehots(anchor, owners, block_rows, over):
    rows = anchor.shape[1]
    owner = jnp.zeros_like(anchor)
    for k in range(1, owners):
        owner = owner + jnp.where(anchor >= k * block_rows, 1, 0)
    eye = iota((rows, rows), 0) == iota((rows, rows), 1)
    owner_f = owner.astype(F32)
    owner_col = jnp.sum(jnp.where(eye, owner_f, 0.0), axis=1, keepdims=True)
    earlier = (owner_col == owner_f) & (iota((rows, rows), 0) < iota((rows, rows), 1))
    rank = jnp.sum(jnp.where(earlier, 1.0, 0.0), axis=0, keepdims=True).astype(jnp.int32)
    place = (anchor - owner * block_rows + 1).astype(F32)
    place_col = jnp.sum(jnp.where(eye, place, 0.0), axis=1, keepdims=True)
    slot = iota((owners * ROWS, rows), 0)
    first = owner * ROWS + rank
    base = onehot((slot == first) & (rank < ROWS))
    if not over:
        return base, None, None, place_col
    low = onehot((slot == first - ROWS) & (rank >= ROWS))
    high = onehot((slot == first - ROWS // 2) & (rank >= ROWS))
    return base, low, high, place_col


def pack_kernel(owners, block_rows, over, width, heads, small, anchor_ref, wide_ref, *refs):
    out_ref = refs[-1]
    base, low, high, place_col = send_onehots(anchor_ref[...], owners, block_rows, over)

    def put(column, values):
        values = values.astype(BF16).reshape(owners, ROWS, values.shape[1])
        out_ref[:, 0, :, column : column + values.shape[2]] = values

    wide = wide_ref[...]
    put(0, dot(base, wide))
    column = width
    if over:
        half = width // 2
        put(
            column,
            dot(
                jnp.concatenate([low, high], axis=1),
                jnp.concatenate([wide[:, :half], wide[:, half:]], axis=0),
            ),
        )
        column += half
    if small == 0:
        return
    b_part, c_part = refs[0][...], refs[1][...]
    if small == 1:
        put(column, dot(base, jnp.concatenate([b_part, c_part], axis=1)))
        if over:
            put(column + 2 * LANES, dot(low, b_part) + dot(high, c_part))
        return
    turn = pl.program_id(0)
    steps = refs[2][...].astype(F32)
    own = jnp.zeros_like(steps)
    lane = iota(steps.shape, 1)
    for k in range(LANES // heads):
        shifted = steps if k == 0 else pltpu.roll(steps, LANES - k * heads, 1)
        own = own + jnp.where(turn == k, shifted, 0.0)
    meta = jnp.where(lane < heads, own, jnp.where(lane == heads, place_col, 0.0)).astype(BF16)
    put(column, dot(base, jnp.concatenate([b_part, c_part, meta], axis=1)))
    if over:
        pair = dot(low, jnp.concatenate([b_part, c_part], axis=1))
        extra = dot(high, meta)
        put(column + 3 * LANES, pair + jnp.concatenate([extra, jnp.zeros_like(extra)], axis=1))


def pack(anchor, wide, smalls, part, dims, small):
    owners, columns, block_rows, over, width, heads = dims
    load_rows = wide.shape[0]
    parts = wide.shape[1] // (columns * width)
    total = width * 3 // 2 if over else width
    if small == 1:
        total += LANES * (3 if over else 2)
    if small == 2:
        total += LANES * (5 if over else 3)
    narrow = pl.BlockSpec((load_rows, LANES), lambda i: (0, i * parts + part))
    in_specs = [
        pl.BlockSpec((1, load_rows), lambda i: (0, 0)),
        pl.BlockSpec((load_rows, width), lambda i: (0, i * parts + part)),
    ]
    if small:
        in_specs += [narrow, narrow]
    if small == 2:
        in_specs += [pl.BlockSpec((load_rows, LANES), lambda i: (0, 0))]
    packed = pl.pallas_call(
        functools.partial(pack_kernel, owners, block_rows, over, width, heads, small),
        grid=(columns,),
        in_specs=in_specs,
        out_specs=pl.BlockSpec((owners, 1, ROWS, total), lambda i: (0, i, 0, 0)),
        out_shape=jax.ShapeDtypeStruct((owners, columns, ROWS, total), BF16),
        compiler_params=PARAMS,
        name=f"pack{small}",
    )(anchor, wide, *smalls)
    return packed.reshape(owners * columns, ROWS, total)


def exchange(values, axes):
    return lax.all_to_all(values, axes, split_axis=0, concat_axis=0, tiled=True)


def doc_counts(lengths_ref, positions):
    count = jnp.zeros_like(positions)
    start = jnp.int32(0)
    for k in range(lengths_ref.shape[0]):
        count = count + jnp.where(positions >= start, 1, 0)
        start = start + lengths_ref[k]
    return count


def column_of(row):
    size = row.shape[1]
    eye = iota((size, size), 0) == iota((size, size), 1)
    return jnp.sum(jnp.where(eye, row, 0.0), axis=1, keepdims=True)


def placed(q_ref, values_ref, over, start, width, stop):
    slots = values_ref.shape[0]
    own = q_ref[:, 0:slots]
    if not over:
        return dot(own, values_ref[:, start : start + width])
    half = width // 2
    extra = values_ref[:, start + stop : start + stop + half]
    first = dot(own, values_ref[:, start : start + half])
    second = dot(own, values_ref[:, start + half : start + width])
    first = first + dot(q_ref[:, slots : 2 * slots], extra)
    second = second + dot(q_ref[:, 2 * slots : 3 * slots], extra)
    return jnp.concatenate([first, second], axis=1)


def local_states(part, per_group, rows_of, tail_ref, b_placed, x_ref, entry_last, state_ref):
    b_turned = b_placed.T
    for h in range(per_group):
        head = part * per_group + h
        weighted = (b_turned * tail_ref[head : head + 1, :]).astype(BF16)
        state = dot(weighted, x_ref[:, h * LANES : (h + 1) * LANES]).astype(BF16)
        piece = min(rows_of, LANES)
        for k in range(LANES // piece):
            at = h * LANES + k * piece
            state_ref[at // rows_of, at % rows_of : at % rows_of + piece, :] = state[
                k * piece : (k + 1) * piece
            ]
    high = entry_last.astype(BF16).astype(F32)
    middle = (entry_last - high).astype(BF16).astype(F32)
    low = entry_last - high - middle
    sub = iota((ROWS, LANES), 0)
    rows = jnp.where(sub == 0, high, jnp.where(sub == 1, middle, jnp.where(sub == 2, low, 0.0)))
    for k in range(state_ref.shape[0]):
        state_ref[k, rows_of : rows_of + ROWS, :] = rows.astype(BF16)


def first_kernel(
    dims,
    place_ref,
    lengths_ref,
    arrived_ref,
    bias_ref,
    rate_ref,
    q_ref,
    x_ref,
    bc_ref,
    rows_ref,
    columns_ref,
    state_ref,
):
    owners, columns, block_rows, over, width, heads = dims
    slots = arrived_ref.shape[0]
    per_group = width // LANES
    rows_of = state_ref.shape[1] - ROWS
    column = width * 3 // 2 if over else width
    meta = arrived_ref[:, column + 2 * LANES : column + 3 * LANES]
    target = iota((block_rows, slots), 0) + 1
    spot = meta.astype(F32).T[heads : heads + 1, :].astype(jnp.int32)
    own = onehot(target == spot)
    q_ref[:, 0:slots] = own
    b_all = dot(own, arrived_ref[:, column : column + LANES])
    c_all = dot(own, arrived_ref[:, column + LANES : column + 2 * LANES])
    meta_all = dot(own, meta)
    if over:
        extra = arrived_ref[:, column + 3 * LANES : column + 4 * LANES]
        other = arrived_ref[:, column + 4 * LANES : column + 5 * LANES]
        spot = extra.astype(F32).T[heads : heads + 1, :]
        half = ROWS // 2
        inside = iota((1, slots), 1) % ROWS
        high_spot = jnp.where(inside >= half, spot, 0.0)
        low_spot = pltpu.roll(high_spot, slots - half, 1)
        low_spot = jnp.where(inside < half, low_spot, 0.0)
        low = onehot(target == low_spot.astype(jnp.int32))
        high = onehot(target == high_spot.astype(jnp.int32))
        q_ref[:, slots : 2 * slots] = low
        q_ref[:, 2 * slots : 3 * slots] = high
        b_all = b_all + dot(low, extra)
        c_all = c_all + dot(low, other)
        meta_all = meta_all + dot(high, extra)
    x_ref[...] = placed(q_ref, arrived_ref, over, 0, width, width).astype(BF16)
    bc_ref[0] = b_all.astype(BF16)
    bc_ref[1] = c_all.astype(BF16)
    raw = meta_all.T[0:heads, :] + column_of(bias_ref[...])
    small = jnp.exp(-jnp.abs(raw))
    step = jnp.maximum(raw, 0.0) + jnp.log1p(small)
    logs = -step * jnp.exp(column_of(rate_ref[...]))
    upper = jnp.where(
        iota((block_rows, block_rows), 0) <= iota((block_rows, block_rows), 1), 1.0, 0.0
    )
    cum = jnp.dot(logs, upper, preferred_element_type=F32, precision=lax.Precision.HIGHEST)
    start = place_ref[0] * block_rows
    docs = doc_counts(lengths_ref, start + iota((1, block_rows), 1))
    last = doc_counts(lengths_ref, start + block_rows - 1 + jnp.zeros((1, 1), jnp.int32))
    before = doc_counts(lengths_ref, start - 1 + jnp.zeros((1, 1), jnp.int32))
    end = cum[:, block_rows - 1 : block_rows]
    tail = jnp.where(docs == last, jnp.exp(end - cum), 0.0) * step
    entry = jnp.where(docs == before, jnp.exp(cum), 0.0)
    rows_ref[0] = step
    rows_ref[1] = cum
    rows_ref[2] = tail
    blank = jnp.zeros((LANES - heads, block_rows), F32)
    entry_turned = jnp.concatenate([entry, blank], axis=0).T
    columns_ref[0] = jnp.concatenate([cum, blank], axis=0).T
    columns_ref[1] = entry_turned
    local_states(
        0,
        per_group,
        rows_of,
        rows_ref.at[2],
        b_all,
        x_ref,
        entry_turned[block_rows - 1 : block_rows, :],
        state_ref,
    )


def later_kernel(
    dims, part, arrived_ref, q_ref, rows_ref, columns_ref, x_ref, bc_ref, state_ref
):
    owners, columns, block_rows, over, width, heads = dims
    slots = arrived_ref.shape[0]
    per_group = width // LANES
    rows_of = state_ref.shape[1] - ROWS
    column = width * 3 // 2 if over else width
    own = q_ref[:, 0:slots]
    b_all = dot(own, arrived_ref[:, column : column + LANES])
    c_all = dot(own, arrived_ref[:, column + LANES : column + 2 * LANES])
    if over:
        extra = arrived_ref[:, column + 2 * LANES : column + 3 * LANES]
        b_all = b_all + dot(q_ref[:, slots : 2 * slots], extra)
        c_all = c_all + dot(q_ref[:, 2 * slots : 3 * slots], extra)
    x_ref[...] = placed(q_ref, arrived_ref, over, 0, width, width).astype(BF16)
    bc_ref[0] = b_all.astype(BF16)
    bc_ref[1] = c_all.astype(BF16)
    local_states(
        part,
        per_group,
        rows_of,
        rows_ref.at[2],
        b_all,
        x_ref,
        columns_ref[1, block_rows - 1 : block_rows, :],
        state_ref,
    )


def intra_kernel(
    part, place_ref, lengths_ref, skip_ref, x_ref, bc_ref, rows_ref, columns_ref, y_ref
):
    block_rows, width = x_ref.shape
    per_group = width // LANES
    scores = lax.dot_general(
        bc_ref[1], bc_ref[0], (((1,), (1,)), ((), ())), preferred_element_type=F32
    )
    start = place_ref[0] * block_rows
    square = (block_rows, block_rows)
    row_docs = doc_counts(lengths_ref, start + iota((1, block_rows), 1))
    column_docs = doc_counts(lengths_ref, start + iota((block_rows, 1), 0))
    keep = (iota(square, 0) >= iota(square, 1)) & (row_docs == column_docs)
    for h in range(per_group):
        head = part * per_group + h
        across = columns_ref[0, :, head : head + 1] - rows_ref[1, head : head + 1, :]
        decay = jnp.exp(jnp.where(keep, across, -jnp.inf))
        weights = (scores * decay * rows_ref[0, head : head + 1, :]).astype(BF16)
        at = slice(h * LANES, (h + 1) * LANES)
        x_head = x_ref[:, at]
        y_ref[:, at] = dot(weights, x_head) + skip_ref[head] * x_head.astype(F32)


def scan_kernel(part, per_group, place_ref, states_ref, out_ref):
    owners, rows_of, _ = out_ref.shape
    block = min(rows_of, LANES)
    lane = iota((1, LANES), 1)
    for k in range(rows_of // block):
        at = slice(k * block, (k + 1) * block)
        head = part * per_group + (place_ref[0] * rows_of + k * block) // LANES
        state = jnp.zeros((block, LANES), F32)
        for j in range(owners):
            out_ref[j, at, :] = state.astype(BF16)
            parts = states_ref[j, rows_of : rows_of + ROWS, :].astype(F32)
            factors = parts[0:1] + parts[1:2] + parts[2:3]
            factor = jnp.sum(jnp.where(lane == head, factors, 0.0), axis=1, keepdims=True)
            state = factor * state + states_ref[j, at, :].astype(F32)


def final_kernel(
    over, part, arrived_ref, q_ref, y_ref, bc_ref, state_ref, columns_ref, gain_ref, *refs
):
    out_ref, gated_ref = refs[-2:]
    block_rows, width = y_ref.shape
    per_group = width // LANES
    gated_ref[...] = placed(q_ref, arrived_ref, over, 0, width, width)
    squares = jnp.zeros((block_rows, LANES), F32)
    for h in range(per_group):
        head = part * per_group + h
        at = slice(h * LANES, (h + 1) * LANES)
        cross = dot(bc_ref[1], state_ref[at, :])
        value = y_ref[:, at] + columns_ref[1, :, head : head + 1] * cross
        gate = gated_ref[:, at]
        value = value * (gate / (1.0 + jnp.exp(-gate)))
        gated_ref[:, at] = value
        squares = squares + value * value
    mean = jnp.sum(squares, axis=1, keepdims=True) * (1.0 / width)
    scale = lax.rsqrt(mean + 1e-05)
    for h in range(per_group):
        at = slice(h * LANES, (h + 1) * LANES)
        out_ref[:, at] = (gated_ref[:, at] * scale * gain_ref[:, at].astype(F32)).astype(BF16)


def shape(*dims, dtype=BF16):
    return jax.ShapeDtypeStruct(dims, dtype)


def body(
    x_load,
    z_load,
    b_load,
    c_load,
    dt_load,
    dt_bias,
    a_log,
    skip_gain,
    norm_gain,
    doc_lengths,
    anchor,
):
    load_rows = anchor.shape[0]
    owners = lax.axis_size("ctx")
    columns = lax.axis_size("head")
    block_rows = load_rows * columns
    capacity = 3 * load_rows // (2 * owners)
    heads = dt_bias.shape[0]
    groups = b_load.shape[1] // (columns * LANES)
    per_group = heads // groups
    width = per_group * LANES
    over = capacity > ROWS
    dims = (owners, columns, block_rows, over, width, heads)
    slots = owners * columns * ROWS
    finds = 3 if over else 1
    rows_of = width // owners
    anchor = anchor.reshape(1, load_rows)
    place = lax.axis_index("ctx").astype(jnp.int32).reshape(1)

    arrived_x = []
    arrived_z = []
    for part in range(groups):
        smalls = (b_load, c_load, dt_load) if part == 0 else (b_load, c_load)
        sent = pack(anchor, x_load, smalls, part, dims, 2 if part == 0 else 1)
        arrived_x.append(exchange(sent, BOTH).reshape(slots, sent.shape[2]))
    for part in range(groups):
        sent = pack(anchor, z_load, (), part, dims, 0)
        arrived_z.append(exchange(sent, BOTH).reshape(slots, sent.shape[2]))

    rows_x, both, partial, states = [], [], [], []
    per_part = (
        shape(block_rows, width),
        shape(2, block_rows, LANES),
    )
    state_shape = shape(owners, rows_of + ROWS, LANES)
    for part in range(groups):
        if part == 0:
            finder, row_values, both_0, rows_0, columns_0, local = pl.pallas_call(
                lambda p, l, a, b, r, q, x, bc, ro, co, st: first_kernel(
                    dims, p, l, a, b, r, q, x, bc, ro, co, st
                ),
                in_specs=[SMEM, SMEM, VMEM, VMEM, VMEM],
                out_specs=[VMEM] * 6,
                out_shape=(
                    shape(block_rows, finds * slots),
                    per_part[0],
                    per_part[1],
                    shape(3, heads, block_rows, dtype=F32),
                    shape(2, block_rows, LANES, dtype=F32),
                    state_shape,
                ),
                compiler_params=PARAMS,
                name="land_first",
            )(
                place,
                doc_lengths,
                arrived_x[0],
                dt_bias.reshape(1, heads),
                a_log.reshape(1, heads),
            )
        else:
            row_values, both_0, local = pl.pallas_call(
                functools.partial(later_kernel, dims, part),
                in_specs=[VMEM] * 4,
                out_specs=[VMEM] * 3,
                out_shape=(per_part[0], per_part[1], state_shape),
                compiler_params=PARAMS,
                name="land_later",
            )(arrived_x[part], finder, rows_0, columns_0)
        rows_x.append(row_values)
        both.append(both_0)
        gathered = exchange(local, "ctx")
        scanned = pl.pallas_call(
            functools.partial(scan_kernel, part, per_group),
            in_specs=[SMEM, VMEM],
            out_specs=VMEM,
            out_shape=shape(owners, rows_of, LANES),
            compiler_params=PARAMS,
            name="scan",
        )(place, gathered)
        states.append(exchange(scanned, "ctx").reshape(width, LANES))
        partial.append(
            pl.pallas_call(
                functools.partial(intra_kernel, part),
                in_specs=[SMEM, SMEM, SMEM, VMEM, VMEM, VMEM, VMEM],
                out_specs=VMEM,
                out_shape=shape(block_rows, width, dtype=F32),
                compiler_params=PARAMS,
                name="intra",
            )(place, doc_lengths, skip_gain, row_values, both_0, rows_0, columns_0)
        )

    result = None
    gain = norm_gain.reshape(1, groups * width)
    for part in range(groups):
        whole = pl.BlockSpec(memory_space=pltpu.VMEM)
        operands = [arrived_z[part], finder, partial[part], both[part], states[part], columns_0, gain]
        full = lambda a: pl.BlockSpec(a.shape, lambda i, n=a.ndim: (0,) * n)
        in_specs = [full(a) for a in operands[:-1]]
        in_specs.append(pl.BlockSpec((1, width), lambda i, part=part: (0, part)))
        aliases = {}
        if result is not None:
            aliases = {len(operands): 0}
            operands.append(result)
            in_specs.append(pl.BlockSpec(memory_space=pl.ANY))
        result = pl.pallas_call(
            functools.partial(final_kernel, over, part),
            grid=(1,),
            in_specs=in_specs,
            out_specs=pl.BlockSpec((block_rows, width), lambda i, part=part: (0, part)),
            out_shape=shape(block_rows, groups * width),
            scratch_shapes=[pltpu.VMEM((block_rows, width), F32)],
            input_output_aliases=aliases,
            compiler_params=PARAMS,
            name="final",
        )(*operands)
    return result


def solution(mesh):
    in_specs = (
        P(BOTH, None),
        P(BOTH, None),
        P(BOTH, None),
        P(BOTH, None),
        P(BOTH, None),
        P("head"),
        P("head"),
        P("head"),
        P("head"),
        P(),
        P(BOTH),
    )
    out_specs = P("ctx", "head")
    return jax.shard_map(body, mesh=mesh, in_specs=in_specs, out_specs=out_specs, check_vma=False)
```

time: 576 us -> 266 us (0.46); the launches traced: 567 us -> 263 us
  blocking collectives: 300 us -> 0 us
  local copies, waits for them, and re-layouts: 119 us -> 2.6 us
  waiting for transfers between devices: 58.6 us -> 167 us
  Pallas kernels: 0 us -> 47.8 us
  other arithmetic: 35.4 us -> 0 us
  between operations: 14.8 us -> 0.07 us
  starting transfers between devices: 31.6 us -> 45.7 us
  matrix products: 7.57 us -> 0 us
    all_gather x1 -> x0, blocking collectives: 188 us -> none  [entering(): gathered = jax.tree.map(lambda a: lax.all_gather(a, axis), part)]
    all_to_all x5 -> x8, waiting for transfers between devices: 0.01 us -> 167 us  [exchange(): return lax.all_to_all(values, axes, split_axis=0, concat_axis=0, tiled=True)]
    unnamed x1 -> x0, blocking collectives: 112 us -> none
    all_gather x1 -> x0, waiting for transfers between devices: 58.5 us -> none  [entering(): gathered = jax.tree.map(lambda a: lax.all_gather(a, axis), part)]
    scatter x14 -> x0, local copies, waits for them, and re-layouts: 54.6 us -> none  [the longest x6 27.5 us: pack(): return blank_buffer.at[owner_of, :, rank_in].set(split_cols)]
    pallas_call x0 -> x12, Pallas kernels: none -> 47.8 us  [the longest x4 16.9 us: pack(): pl.pallas_call(functools.partial(pack_kernel, owners, block_rows, over, w...]
    reshape x17 -> x1, local copies, waits for them, and re-layouts: 35.5 us -> 0.61 us  [body(): gain = norm_gain.reshape(1, groups * width)]
    add x10 -> x0, other arithmetic: 15.5 us -> none  [the longest x7 13.9 us: combine_states(): later[0][:, None, None] * earlier[1] + later[1]]
  transfers between devices with their start and end apart: 6 -> 8, of which waited for: 1 -> 7; matrix products, arithmetic and copies ran while one was open for 15% -> 0% of each run, Pallas kernels for 0% -> 15%
where the time goes in v1:
time: 266 us; the launch traced here: 263 us
  waiting for transfers between devices  167 us (63%)
  Pallas kernels  47.8 us (18%)
  starting transfers between devices  45.7 us (17%)
    all_to_all x8, waiting for transfers between devices, exchange(): return lax.all_to_all(values, axes, split_axis=0, concat_axis=0, tiled=True)  167 us
    all_to_all x8, starting transfers between devices, exchange(): return lax.all_to_all(values, axes, split_axis=0, concat_axis=0, tiled=True)  45.7 us
    pallas_call x4, Pallas kernels, pack(): pl.pallas_call(functools.partial(pack_kernel, owners, block_rows, over, w...  16.9 us
    pallas_call x2, Pallas kernels, body(): pl.pallas_call(functools.partial(final_kernel, over, part), grid=(1,), in...  10.4 us
    pallas_call x2, Pallas kernels, body(): pl.pallas_call(functools.partial(intra_kernel, part), in_specs=[SMEM, SME...  8.46 us
  transfers between devices with their start and end apart: 8, of which 7 were waited for; matrix products, arithmetic and copies ran while one was open for 0% of the time, Pallas kernels for 15%

profile of v1, /device:TPU:27, one launch (start us, length us, event | category | flops | bytes accessed | tf_op | source)
XLA Modules:
  0.0 262.9 jit_solution(5286928290815518662)
XLA Ops:
  0.0 4.1 %pack0.3 = bf16[8,4,8,3072]{3,2,1,0:T(8,128)(2,1)} custom-call(s32[1,64]{1,0:T(1,128)} %bitcast.23, bf16[64,16384]{1,0:T(8,128)(2,1)} %wide_ref.7), custom_call_target="tpu_custom_call" | custom-call | tf_op jit(solution)/shard_map/pack0/pallas_call | solution.py:117
  4.1 6.2 %all-to-all-start.5 = ((bf16[32,8,3072]{2,1,0:T(8,128)(2,1)}), bf16[32,8,3072]{2,1,0:T(8,128)(2,1)S(1)}, u32[]{:S(2)}, u32[]{:S(2)}) async-start(bf16[32,8,3072]{2,1,0:T(8,128)(2,1)} %bitcast.20), calls=%async_computation.5 | async-start | bytes 3145728 | tf_op jit(solution)/shard_map/all_to_all | solution.py:130
  10.3 4.2 %pack0.2 = bf16[8,4,8,3072]{3,2,1,0:T(8,128)(2,1)} custom-call(s32[1,64]{1,0:T(1,128)} %bitcast.24, bf16[64,16384]{1,0:T(8,128)(2,1)} %wide_ref.7), custom_call_target="tpu_custom_call" | custom-call | tf_op jit(solution)/shard_map/pack0/pallas_call | solution.py:117
  14.5 31.0 %all-to-all-done.5 = bf16[32,8,3072]{2,1,0:T(8,128)(2,1)S(1)} async-done(((bf16[32,8,3072]{2,1,0:T(8,128)(2,1)}), bf16[32,8,3072]{2,1,0:T(8,128)(2,1)S(1)}, u32[]{:S(2)}, u32[]{:S(2)}) %all-to-all-start.5) | async-done | bytes 1572896 | tf_op jit(solution)/shard_map/all_to_all | solution.py:130
  45.5 0.0 copy-start.1
  45.5 5.8 %all-to-all-start = ((bf16[32,8,3072]{2,1,0:T(8,128)(2,1)}), bf16[32,8,3072]{2,1,0:T(8,128)(2,1)S(1)}, u32[]{:S(2)}, u32[]{:S(2)}) async-start(bf16[32,8,3072]{2,1,0:T(8,128)(2,1)} %bitcast.19), calls=%async_computation | async-start | bytes 3145728 | tf_op jit(solution)/shard_map/all_to_all | solution.py:130
  51.3 4.3 %pack2.1 = bf16[8,4,8,3712]{3,2,1,0:T(8,128)(2,1)} custom-call(s32[1,64]{1,0:T(1,128)} %bitcast.25, bf16[64,16384]{1,0:T(8,128)(2,1)} %wide_ref.6, bf16[64,1024]{1,0:T(8,128)(2,1)} %refs_0_.3, bf16[64,1024]{1,0:T(8,128)(2,1)} %refs_1_.3, bf16[64,128]{1,0:T(8,128)(2,1)} %refs_2_.1), custom_call_target="tpu_custom_call" | custom-call | tf_op jit(solution)/shard_map/pack2/pallas_call | solution.py:117
  55.7 0.0 copy-done.1
  55.7 30.9 %all-to-all-done = bf16[32,8,3072]{2,1,0:T(8,128)(2,1)S(1)} async-done(((bf16[32,8,3072]{2,1,0:T(8,128)(2,1)}), bf16[32,8,3072]{2,1,0:T(8,128)(2,1)S(1)}, u32[]{:S(2)}, u32[]{:S(2)}) %all-to-all-start) | async-done | bytes 1572896 | tf_op jit(solution)/shard_map/all_to_all | solution.py:130
  86.6 0.0 copy-start.2
  86.6 1.2 copy-done.2
  87.8 5.8 %all-to-all-start.1 = ((bf16[32,8,3712]{2,1,0:T(8,128)(2,1)}), bf16[32,8,3712]{2,1,0:T(8,128)(2,1)S(1)}, u32[]{:S(2)}, u32[]{:S(2)}) async-start(bf16[32,8,3712]{2,1,0:T(8,128)(2,1)} %bitcast.15), calls=%async_computation.1 | async-start | bytes 3801088 | tf_op jit(solution)/shard_map/all_to_all | solution.py:130
  93.6 4.3 %pack1.1 = bf16[8,4,8,3456]{3,2,1,0:T(8,128)(2,1)} custom-call(s32[1,64]{1,0:T(1,128)} %bitcast.26, bf16[64,16384]{1,0:T(8,128)(2,1)} %wide_ref.6, bf16[64,1024]{1,0:T(8,128)(2,1)} %refs_0_.3, bf16[64,1024]{1,0:T(8,128)(2,1)} %refs_1_.3), custom_call_target="tpu_custom_call" | custom-call | tf_op jit(solution)/shard_map/pack1/pallas_call | solution.py:117
  97.9 37.9 %all-to-all-done.1 = bf16[32,8,3712]{2,1,0:T(8,128)(2,1)S(1)} async-done(((bf16[32,8,3712]{2,1,0:T(8,128)(2,1)}), bf16[32,8,3712]{2,1,0:T(8,128)(2,1)S(1)}, u32[]{:S(2)}, u32[]{:S(2)}) %all-to-all-start.1) | async-done | bytes 1900576 | tf_op jit(solution)/shard_map/all_to_all | solution.py:130
  135.8 0.0 copy-start
  135.8 6.2 %all-to-all-start.2 = ((bf16[32,8,3456]{2,1,0:T(8,128)(2,1)}), bf16[32,8,3456]{2,1,0:T(8,128)(2,1)}, u32[]{:S(2)}, u32[]{:S(2)}) async-start(bf16[32,8,3456]{2,1,0:T(8,128)(2,1)} %bitcast.16), calls=%async_computation.2 | async-start | bytes 3538944 | tf_op jit(solution)/shard_map/all_to_all | solution.py:130
  142.0 0.0 copy-done
  142.0 4.2 %land_first.1 = (bf16[256,768]{1,0:T(8,128)(2,1)}, bf16[256,2048]{1,0:T(8,128)(2,1)}, bf16[2,256,128]{2,1,0:T(8,128)(2,1)}, f32[3,32,256]{2,1,0:T(8,128)}, f32[2...) custom-call(s32[1]{0:T(128)} %bitcast.3.p.place_ref, s32[16]{0:T(128)} %lengths_ref.3, bf16[256,3712]{1,0:T(8,128)(2,1)} %bitcast.14, ...), custom_call_target="tpu_custom_call" | custom-call | tf_op jit(solution)/shard_map/land_first/pallas_call | solution.py:408
  146.2 35.3 %all-to-all-done.2 = bf16[32,8,3456]{2,1,0:T(8,128)(2,1)} async-done(((bf16[32,8,3456]{2,1,0:T(8,128)(2,1)}), bf16[32,8,3456]{2,1,0:T(8,128)(2,1)}, u32[]{:S(2)}, u32[]{:S(2)}) %all-to-all-start.2) | async-done | bytes 1769504 | tf_op jit(solution)/shard_map/all_to_all | solution.py:130
  181.5 5.4 %all-to-all-start.6 = ((bf16[8,264,128]{2,1,0:T(8,128)(2,1)}), bf16[8,264,128]{2,1,0:T(8,128)(2,1)S(1)}, u32[]{:S(2)}, u32[]{:S(2)}) async-start(bf16[8,264,128]{2,1,0:T(8,128)(2,1)} %get-tuple-element.22), calls=%async_computation.6 | async-start | bytes 1081344 | tf_op jit(solution)/shard_map/all_to_all | solution.py:130
  186.9 3.6 %land_later.1 = (bf16[256,2048]{1,0:T(8,128)(2,1)}, bf16[2,256,128]{2,1,0:T(8,128)(2,1)}, bf16[8,264,128]{2,1,0:T(8,128)(2,1)}) custom-call(bf16[256,3456]{1,0:T(8,128)(2,1)} %bitcast.9.arrived_ref, bf16[256,768]{1,0:T(8,128)(2,1)} %get-tuple-element.14.q_ref, f32[3,32,256]{2,1,0:T(8,128)} %get-tuple-element.15.rows_ref, ...), custom_call_target="tpu_custom_call" | custom-call | tf_op jit(solution)/shard_map/land_later/pallas_call | solution.py:432
  190.6 9.6 %all-to-all-done.6.states_ref = bf16[8,264,128]{2,1,0:T(8,128)(2,1)S(1)} async-done(((bf16[8,264,128]{2,1,0:T(8,128)(2,1)}), bf16[8,264,128]{2,1,0:T(8,128)(2,1)S(1)}, u32[]{:S(2)}, u32[]{:S(2)}) %all-to-all-start.6) | async-done | bytes 540704 | tf_op jit(solution)/shard_map/all_to_all | solution.py:130
  200.2 0.0 copy-start.3
  200.2 5.4 %all-to-all-start.3 = ((bf16[8,264,128]{2,1,0:T(8,128)(2,1)}), bf16[8,264,128]{2,1,0:T(8,128)(2,1)S(1)}, u32[]{:S(2)}, u32[]{:S(2)}) async-start(bf16[8,264,128]{2,1,0:T(8,128)(2,1)} %get-tuple-element.19), calls=%async_computation.3 | async-start | bytes 1081344 | tf_op jit(solution)/shard_map/all_to_all | solution.py:130
  205.6 0.0 copy-done.3
  205.6 0.0 copy-start.7
  205.6 2.1 scan.3
  207.7 11.2 %all-to-all-done.3.states_ref = bf16[8,264,128]{2,1,0:T(8,128)(2,1)S(1)} async-done(((bf16[8,264,128]{2,1,0:T(8,128)(2,1)}), bf16[8,264,128]{2,1,0:T(8,128)(2,1)S(1)}, u32[]{:S(2)}, u32[]{:S(2)}) %all-to-all-start.3) | async-done | bytes 540704 | tf_op jit(solution)/shard_map/all_to_all | solution.py:130
  218.8 0.0 copy-start.4
  218.8 5.4 %all-to-all-start.7 = ((bf16[8,256,128]{2,1,0:T(8,128)(2,1)}), bf16[8,256,128]{2,1,0:T(8,128)(2,1)S(1)}, u32[]{:S(2)}, u32[]{:S(2)}) async-start(bf16[8,256,128]{2,1,0:T(8,128)(2,1)} %scan.3), calls=%async_computation.7 | async-start | bytes 1048576 | tf_op jit(solution)/shard_map/all_to_all | solution.py:130
  224.3 0.0 copy-done.4
  224.3 2.1 scan.2
  226.4 10.8 %all-to-all-done.7 = bf16[8,256,128]{2,1,0:T(8,128)(2,1)S(1)} async-done(((bf16[8,256,128]{2,1,0:T(8,128)(2,1)}), bf16[8,256,128]{2,1,0:T(8,128)(2,1)S(1)}, u32[]{:S(2)}, u32[]{:S(2)}) %all-to-all-start.7) | async-done | bytes 524320 | tf_op jit(solution)/shard_map/all_to_all | solution.py:130
  237.1 0.0 copy-start.5
  237.1 5.4 %all-to-all-start.4 = ((bf16[8,256,128]{2,1,0:T(8,128)(2,1)}), bf16[8,256,128]{2,1,0:T(8,128)(2,1)S(1)}, u32[]{:S(2)}, u32[]{:S(2)}) async-start(bf16[8,256,128]{2,1,0:T(8,128)(2,1)} %scan.2), calls=%async_computation.4 | async-start | bytes 1048576 | tf_op jit(solution)/shard_map/all_to_all | solution.py:130
  242.6 0.0 copy-done.7
  242.6 0.6 reshape.56.gain_ref
  243.2 4.2 %intra.3.y_ref = f32[256,2048]{1,0:T(8,128)} custom-call(s32[1]{0:T(128)} %bitcast.3.p.place_ref, s32[16]{0:T(128)} %lengths_ref.3, f32[32]{0:T(128)} %skip_ref.3, bf16[256,2048]{1,0:T(8,128)(2,1)} %get-tuple-element.20.x_ref, bf16[2,256,128]{2,1,0:T(8,128)(2,1)} %get-tuple-element.21.bc_ref, f32[3,32,256]{2,1,0:T(8,128)} %get-tuple-element.15.rows_ref, ...), custom_call_target="tpu_custom_call" | custom-call | tf_op jit(solution)/shard_map/intra/pallas_call | solution.py:453
  247.4 0.0 copy-done.5
  247.4 4.2 %intra.2.y_ref = f32[256,2048]{1,0:T(8,128)} custom-call(s32[1]{0:T(128)} %bitcast.3.p.place_ref, s32[16]{0:T(128)} %lengths_ref.3, f32[32]{0:T(128)} %skip_ref.3, bf16[256,2048]{1,0:T(8,128)(2,1)} %get-tuple-element.17.x_ref, bf16[2,256,128]{2,1,0:T(8,128)(2,1)} %get-tuple-element.18.bc_ref, f32[3,32,256]{2,1,0:T(8,128)} %get-tuple-element.15.rows_ref, ...), custom_call_target="tpu_custom_call" | custom-call | tf_op jit(solution)/shard_map/intra/pallas_call | solution.py:453
  251.6 5.2 %final.2.refs_0_ = bf16[256,4096]{1,0:T(8,128)(2,1)} custom-call(bf16[256,3072]{1,0:T(8,128)(2,1)} %bitcast.17, bf16[256,768]{1,0:T(8,128)(2,1)} %get-tuple-element.14.q_ref, f32[256,2048]{1,0:T(8,128)} %intra.3.y_ref, bf16[2,256,128]{2,1,0:T(8,128)(2,1)} %get-tuple-element.21.bc_ref, bf16[2048,128]{1,0:T(8,128)(2,1)} %bitcast.21, ...), custom_call_target="tpu_custom_call" | custom-call | tf_op jit(solution)/shard_map/final/pallas_call | solution.py:476
  256.9 0.0 all-to-all-done.4
  256.9 0.0 copy-start.6
  256.9 0.8 copy-done.6
  257.7 5.2 %final.3 = bf16[256,4096]{1,0:T(8,128)(2,1)} custom-call(bf16[256,3072]{1,0:T(8,128)(2,1)} %bitcast.18, bf16[256,768]{1,0:T(8,128)(2,1)} %get-tuple-element.14.q_ref, f32[256,2048]{1,0:T(8,128)} %intra.2.y_ref, bf16[2,256,128]{2,1,0:T(8,128)(2,1)} %get-tuple-element.18.bc_ref, bf16[2048,128]{1,0:T(8,128)(2,1)} %bitcast.22, ...), custom_call_target="tpu_custom_call", output_to_operand_aliasing={{}: (7, {})} | custom-call | tf_op jit(solution)/shard_map/final/pallas_call | solution.py:476
Async XLA Ops:
  4.1 41.4 %all-to-all-start.5 = ((bf16[32,8,3072]{2,1,0:T(8,128)(2,1)}), bf16[32,8,3072]{2,1,0:T(8,128)(2,1)S(1)}, u32[]{:S(2)}, u32[]{:S(2)}) async-start(bf16[32,8,3072]{2,1,0:T(8,128)(2,1)} %bitcast.20), calls=%async_computation.5 | async-start | bytes 3145728 | tf_op jit(solution)/shard_map/all_to_all | solution.py:130
  45.5 10.2 %copy-start.1 = (bf16[32,8,3072]{2,1,0:T(8,128)(2,1)}, bf16[32,8,3072]{2,1,0:T(8,128)(2,1)S(1)}, u32[]{:S(2)}) copy-start(bf16[32,8,3072]{2,1,0:T(8,128)(2,1)S(1)} %all-to-all-done.5) | copy-start | bytes 4718596
  45.5 41.1 %all-to-all-start = ((bf16[32,8,3072]{2,1,0:T(8,128)(2,1)}), bf16[32,8,3072]{2,1,0:T(8,128)(2,1)S(1)}, u32[]{:S(2)}, u32[]{:S(2)}) async-start(bf16[32,8,3072]{2,1,0:T(8,128)(2,1)} %bitcast.19), calls=%async_computation | async-start | bytes 3145728 | tf_op jit(solution)/shard_map/all_to_all | solution.py:130
  86.6 1.2 copy-start.2
  87.8 48.1 %all-to-all-start.1 = ((bf16[32,8,3712]{2,1,0:T(8,128)(2,1)}), bf16[32,8,3712]{2,1,0:T(8,128)(2,1)S(1)}, u32[]{:S(2)}, u32[]{:S(2)}) async-start(bf16[32,8,3712]{2,1,0:T(8,128)(2,1)} %bitcast.15), calls=%async_computation.1 | async-start | bytes 3801088 | tf_op jit(solution)/shard_map/all_to_all | solution.py:130
  135.8 6.2 %copy-start = (bf16[32,8,3712]{2,1,0:T(8,128)(2,1)}, bf16[32,8,3712]{2,1,0:T(8,128)(2,1)S(1)}, u32[]{:S(2)}) copy-start(bf16[32,8,3712]{2,1,0:T(8,128)(2,1)S(1)} %all-to-all-done.1) | copy-start | bytes 5701636
  135.8 45.7 %all-to-all-start.2 = ((bf16[32,8,3456]{2,1,0:T(8,128)(2,1)}), bf16[32,8,3456]{2,1,0:T(8,128)(2,1)}, u32[]{:S(2)}, u32[]{:S(2)}) async-start(bf16[32,8,3456]{2,1,0:T(8,128)(2,1)} %bitcast.16), calls=%async_computation.2 | async-start | bytes 3538944 | tf_op jit(solution)/shard_map/all_to_all | solution.py:130
  181.5 18.7 %all-to-all-start.6 = ((bf16[8,264,128]{2,1,0:T(8,128)(2,1)}), bf16[8,264,128]{2,1,0:T(8,128)(2,1)S(1)}, u32[]{:S(2)}, u32[]{:S(2)}) async-start(bf16[8,264,128]{2,1,0:T(8,128)(2,1)} %get-tuple-element.22), calls=%async_computation.6 | async-start | bytes 1081344 | tf_op jit(solution)/shard_map/all_to_all | solution.py:130
  200.2 5.4 %copy-start.3 = (bf16[8,264,128]{2,1,0:T(8,128)(2,1)}, bf16[8,264,128]{2,1,0:T(8,128)(2,1)S(1)}, u32[]{:S(2)}) copy-start(bf16[8,264,128]{2,1,0:T(8,128)(2,1)S(1)} %all-to-all-done.6.states_ref) | copy-start | bytes 1622020
  200.2 18.7 %all-to-all-start.3 = ((bf16[8,264,128]{2,1,0:T(8,128)(2,1)}), bf16[8,264,128]{2,1,0:T(8,128)(2,1)S(1)}, u32[]{:S(2)}, u32[]{:S(2)}) async-start(bf16[8,264,128]{2,1,0:T(8,128)(2,1)} %get-tuple-element.19), calls=%async_computation.3 | async-start | bytes 1081344 | tf_op jit(solution)/shard_map/all_to_all | solution.py:130
  205.6 37.0 %copy-start.7 = (bf16[4096]{0:T(1024)(128)(2,1)S(1)}, bf16[4096]{0:T(1024)(128)(2,1)}, u32[]{:S(2)}) copy-start(bf16[4096]{0:T(1024)(128)(2,1)} %param.19) | copy-start | bytes 24580
  218.8 5.4 %copy-start.4 = (bf16[8,264,128]{2,1,0:T(8,128)(2,1)}, bf16[8,264,128]{2,1,0:T(8,128)(2,1)S(1)}, u32[]{:S(2)}) copy-start(bf16[8,264,128]{2,1,0:T(8,128)(2,1)S(1)} %all-to-all-done.3.states_ref) | copy-start | bytes 1622020
  218.8 18.3 %all-to-all-start.7 = ((bf16[8,256,128]{2,1,0:T(8,128)(2,1)}), bf16[8,256,128]{2,1,0:T(8,128)(2,1)S(1)}, u32[]{:S(2)}, u32[]{:S(2)}) async-start(bf16[8,256,128]{2,1,0:T(8,128)(2,1)} %scan.3), calls=%async_computation.7 | async-start | bytes 1048576 | tf_op jit(solution)/shard_map/all_to_all | solution.py:130
  237.1 10.3 %copy-start.5 = (bf16[8,256,128]{2,1,0:T(8,128)(2,1)}, bf16[8,256,128]{2,1,0:T(8,128)(2,1)S(1)}, u32[]{:S(2)}) copy-start(bf16[8,256,128]{2,1,0:T(8,128)(2,1)S(1)} %all-to-all-done.7) | copy-start | bytes 1572868
  237.1 19.7 %all-to-all-start.4 = ((bf16[8,256,128]{2,1,0:T(8,128)(2,1)}), bf16[8,256,128]{2,1,0:T(8,128)(2,1)S(1)}, u32[]{:S(2)}, u32[]{:S(2)}) async-start(bf16[8,256,128]{2,1,0:T(8,128)(2,1)} %scan.2), calls=%async_computation.4 | async-start | bytes 1048576 | tf_op jit(solution)/shard_map/all_to_all | solution.py:130
  256.9 0.8 copy-start.6

commit v2 on v1

--- a/solution.py
+++ b/solution.py
@@ -7,7 +7,6 @@
 from jax.experimental.pallas import tpu as pltpu
 from jax.sharding import PartitionSpec as P
 
-SPAN = 256
 LANES = 128
 ROWS = 8
 F32 = jnp.float32
@@ -105,25 +104,26 @@
         total += LANES * (3 if over else 2)
     if small == 2:
         total += LANES * (5 if over else 3)
-    narrow = pl.BlockSpec((load_rows, LANES), lambda i: (0, i * parts + part))
+    count = parts if part is None else 1
+    group = (lambda i, k: i * parts + k) if part is None else (lambda i, k: i * parts + part)
+    narrow = pl.BlockSpec((load_rows, LANES), lambda i, k: (0, group(i, k)))
     in_specs = [
-        pl.BlockSpec((1, load_rows), lambda i: (0, 0)),
-        pl.BlockSpec((load_rows, width), lambda i: (0, i * parts + part)),
+        pl.BlockSpec((1, load_rows), lambda i, k: (0, 0)),
+        pl.BlockSpec((load_rows, width), lambda i, k: (0, group(i, k))),
     ]
     if small:
         in_specs += [narrow, narrow]
     if small == 2:
-        in_specs += [pl.BlockSpec((load_rows, LANES), lambda i: (0, 0))]
+        in_specs += [pl.BlockSpec((load_rows, LANES), lambda i, k: (0, 0))]
     packed = pl.pallas_call(
         functools.partial(pack_kernel, owners, block_rows, over, width, heads, small),
-        grid=(columns,),
+        grid=(columns, count),
         in_specs=in_specs,
-        out_specs=pl.BlockSpec((owners, 1, ROWS, total), lambda i: (0, i, 0, 0)),
-        out_shape=jax.ShapeDtypeStruct((owners, columns, ROWS, total), BF16),
+        out_specs=pl.BlockSpec((owners, 1, ROWS, total), lambda i, k: (0, i, 0, k)),
+        out_shape=jax.ShapeDtypeStruct((owners, columns, ROWS, total * count), BF16),
         compiler_params=PARAMS,
-        name=f"pack{small}",
     )(anchor, wide, *smalls)
-    return packed.reshape(owners * columns, ROWS, total)
+    return packed.reshape(owners * columns, ROWS, total * count)
 
 
 def exchange(values, axes):
@@ -159,25 +159,19 @@
     return jnp.concatenate([first, second], axis=1)
 
 
-def local_states(part, per_group, rows_of, tail_ref, b_placed, x_ref, entry_last, state_ref):
+def local_states(part, per_group, tail_ref, b_placed, x_ref, entry_last, state_ref):
     b_turned = b_placed.T
     for h in range(per_group):
         head = part * per_group + h
         weighted = (b_turned * tail_ref[head : head + 1, :]).astype(BF16)
-        state = dot(weighted, x_ref[:, h * LANES : (h + 1) * LANES]).astype(BF16)
-        piece = min(rows_of, LANES)
-        for k in range(LANES // piece):
-            at = h * LANES + k * piece
-            state_ref[at // rows_of, at % rows_of : at % rows_of + piece, :] = state[
-                k * piece : (k + 1) * piece
-            ]
+        at = slice(h * LANES, (h + 1) * LANES)
+        state_ref[at, :] = dot(weighted, x_ref[:, at]).astype(BF16)
     high = entry_last.astype(BF16).astype(F32)
     middle = (entry_last - high).astype(BF16).astype(F32)
     low = entry_last - high - middle
     sub = iota((ROWS, LANES), 0)
     rows = jnp.where(sub == 0, high, jnp.where(sub == 1, middle, jnp.where(sub == 2, low, 0.0)))
-    for k in range(state_ref.shape[0]):
-        state_ref[k, rows_of : rows_of + ROWS, :] = rows.astype(BF16)
+    state_ref[per_group * LANES :, :] = rows.astype(BF16)
 
 
 def first_kernel(
@@ -194,10 +188,9 @@
     columns_ref,
     state_ref,
 ):
-    owners, columns, block_rows, over, width, heads = dims
+    _, _, block_rows, over, width, heads = dims
     slots = arrived_ref.shape[0]
     per_group = width // LANES
-    rows_of = state_ref.shape[1] - ROWS
     column = width * 3 // 2 if over else width
     meta = arrived_ref[:, column + 2 * LANES : column + 3 * LANES]
     target = iota((block_rows, slots), 0) + 1
@@ -251,7 +244,6 @@
     local_states(
         0,
         per_group,
-        rows_of,
         rows_ref.at[2],
         b_all,
         x_ref,
@@ -263,10 +255,9 @@
 def later_kernel(
     dims, part, arrived_ref, q_ref, rows_ref, columns_ref, x_ref, bc_ref, state_ref
 ):
-    owners, columns, block_rows, over, width, heads = dims
+    _, _, block_rows, over, width, _ = dims
     slots = arrived_ref.shape[0]
     per_group = width // LANES
-    rows_of = state_ref.shape[1] - ROWS
     column = width * 3 // 2 if over else width
     own = q_ref[:, 0:slots]
     b_all = dot(own, arrived_ref[:, column : column + LANES])
@@ -281,7 +272,6 @@
     local_states(
         part,
         per_group,
-        rows_of,
         rows_ref.at[2],
         b_all,
         x_ref,
@@ -313,44 +303,144 @@
         y_ref[:, at] = dot(weights, x_head) + skip_ref[head] * x_head.astype(F32)
 
 
-def scan_kernel(part, per_group, place_ref, states_ref, out_ref):
-    owners, rows_of, _ = out_ref.shape
-    block = min(rows_of, LANES)
-    lane = iota((1, LANES), 1)
-    for k in range(rows_of // block):
-        at = slice(k * block, (k + 1) * block)
-        head = part * per_group + (place_ref[0] * rows_of + k * block) // LANES
-        state = jnp.zeros((block, LANES), F32)
-        for j in range(owners):
-            out_ref[j, at, :] = state.astype(BF16)
-            parts = states_ref[j, rows_of : rows_of + ROWS, :].astype(F32)
-            factors = parts[0:1] + parts[1:2] + parts[2:3]
-            factor = jnp.sum(jnp.where(lane == head, factors, 0.0), axis=1, keepdims=True)
-            state = factor * state + states_ref[j, at, :].astype(F32)
-
-
-def final_kernel(
-    over, part, arrived_ref, q_ref, y_ref, bc_ref, state_ref, columns_ref, gain_ref, *refs
-):
+def decays(rows):
+    parts = rows.astype(F32)
+    return parts[0:1] + parts[1:2] + parts[2:3]
+
+
+def one_lane(row, index):
+    return jnp.sum(jnp.where(iota((1, LANES), 1) == index, row, 0.0), axis=1, keepdims=True)
+
+
+def offer_kernel(place_ref, state_ref, send_ref):
+    half = send_ref.shape[0] - ROWS
+    side = place_ref[0] % 2
+    send_ref[0:half, :] = jnp.where(side == 0, state_ref[half : 2 * half], state_ref[0:half])
+    send_ref[half:, :] = state_ref[2 * half :, :]
+
+
+def meet_kernel(part, place_ref, state_ref, got_ref, total_ref, sent_ref, decay_ref):
+    half = got_ref.shape[0] - ROWS
+    side = place_ref[0] % 2
+    own = decays(state_ref[2 * half :, :])
+    other = decays(got_ref[half:, :])
+    decay_ref[...] = jnp.broadcast_to(own * other, decay_ref.shape)
+    second = jnp.where(side == 0, other, own)
+    for q in range(half // LANES):
+        at = slice(q * LANES, (q + 1) * LANES)
+        below = slice(half + q * LANES, half + (q + 1) * LANES)
+        kept = jnp.where(side == 0, state_ref[at, :], state_ref[below, :]).astype(F32)
+        got = got_ref[at, :].astype(F32)
+        index = (2 * part + side) * (half // LANES) + q
+        fresh = jnp.where(side == 0, got, kept)
+        total = one_lane(second, index) * jnp.where(side == 0, kept, got) + fresh
+        total_ref[at, :] = total
+        sent_ref[at, :] = total.astype(BF16)
+
+
+def step_kernel(part, place_ref, total_ref, decay_ref, got_ref, sent_ref):
+    half = got_ref.shape[0]
+    side = place_ref[0] % 2
+    for q in range(half // LANES):
+        at = slice(q * LANES, (q + 1) * LANES)
+        index = (2 * part + side) * (half // LANES) + q
+        decay = one_lane(decay_ref[0:1, :], index)
+        sent_ref[at, :] = (decay * got_ref[at, :].astype(F32) + total_ref[at, :]).astype(BF16)
+
+
+def split_kernel(part, place_ref, state_ref, got_ref, *refs):
+    keep_ref, send_ref = refs[-2:]
+    half = got_ref.shape[0] - ROWS
+    side = place_ref[0] % 2
+    first = jnp.where(side == 0, decays(state_ref[2 * half :, :]), decays(got_ref[half:, :]))
+    for q in range(half // LANES):
+        at = slice(q * LANES, (q + 1) * LANES)
+        index = (2 * part + side) * (half // LANES) + q
+        entering = refs[0][at, :].astype(F32)
+        for ref in refs[1:-2]:
+            entering = entering + ref[at, :].astype(F32)
+        earlier = jnp.where(side == 0, state_ref[at, :], got_ref[at, :]).astype(F32)
+        after = one_lane(first, index) * entering + earlier
+        keep_ref[at, :] = jnp.where(side == 0, entering, after).astype(BF16)
+        send_ref[at, :] = jnp.where(side == 0, after, entering).astype(BF16)
+
+
+def enter(part, place, state):
+    blocks = lax.axis_size("ctx")
+    half = (state.shape[0] - ROWS) // 2
+    pairs = [(i, i ^ 1) for i in range(blocks)]
+    call = functools.partial(pl.pallas_call, compiler_params=PARAMS)
+    shared = dict(out_specs=VMEM, out_shape=shape(half, LANES))
+    offered = call(
+        offer_kernel,
+        in_specs=[SMEM, VMEM],
+        out_specs=VMEM,
+        out_shape=shape(half + ROWS, LANES),
+        name="offer",
+    )(place, state)
+    got = lax.ppermute(offered, "ctx", pairs)
+    total, sent, decay = call(
+        functools.partial(meet_kernel, part),
+        in_specs=[SMEM, VMEM, VMEM],
+        out_specs=[VMEM] * 3,
+        out_shape=(
+            shape(half, LANES, dtype=F32),
+            shape(half, LANES),
+            shape(ROWS, LANES, dtype=F32),
+        ),
+        name="meet",
+    )(place, state, got)
+    received = []
+    for k in range(blocks // 2 - 1):
+        if k > 0:
+            sent = call(
+                functools.partial(step_kernel, part),
+                in_specs=[SMEM, VMEM, VMEM, VMEM],
+                name="step",
+                **shared,
+            )(place, total, decay, received[-1])
+        hops = [(2 * k + side, 2 * k + 2 + side) for side in range(2)]
+        received.append(lax.ppermute(sent, "ctx", hops))
+    keep, send = call(
+      functools.partial(split_kernel, part),
+      in_specs=[SMEM] + [VMEM] * (2 + len(received)),
+      out_specs=[VMEM] * 2,
+      out_shape=(shape(half, LANES),) * 2,
+      name="split",
+    )(place, state, got, *received)
+    return keep, lax.ppermute(send, "ctx", pairs)
+
+
+def final_kernel(over, groups, place_ref, arrived_ref, q_ref, columns_ref, gain_ref, *refs):
     out_ref, gated_ref = refs[-2:]
-    block_rows, width = y_ref.shape
+    block_rows = out_ref.shape[0]
+    width = out_ref.shape[1] // groups
     per_group = width // LANES
-    gated_ref[...] = placed(q_ref, arrived_ref, over, 0, width, width)
-    squares = jnp.zeros((block_rows, LANES), F32)
-    for h in range(per_group):
-        head = part * per_group + h
-        at = slice(h * LANES, (h + 1) * LANES)
-        cross = dot(bc_ref[1], state_ref[at, :])
-        value = y_ref[:, at] + columns_ref[1, :, head : head + 1] * cross
-        gate = gated_ref[:, at]
-        value = value * (gate / (1.0 + jnp.exp(-gate)))
-        gated_ref[:, at] = value
-        squares = squares + value * value
-    mean = jnp.sum(squares, axis=1, keepdims=True) * (1.0 / width)
-    scale = lax.rsqrt(mean + 1e-05)
-    for h in range(per_group):
-        at = slice(h * LANES, (h + 1) * LANES)
-        out_ref[:, at] = (gated_ref[:, at] * scale * gain_ref[:, at].astype(F32)).astype(BF16)
+    stride = arrived_ref.shape[1] // groups
+    side = place_ref[0] % 2
+    for part in range(groups):
+        y_ref, bc_ref, keep_ref, got_ref = refs[4 * part : 4 * part + 4]
+        gated_ref[...] = placed(q_ref, arrived_ref.at[:, part * stride : (part + 1) * stride], over, 0, width, width)
+        c_rows = bc_ref[0]
+        squares = jnp.zeros((block_rows, LANES), F32)
+        for h in range(per_group):
+            head = part * per_group + h
+            at = slice(h * LANES, (h + 1) * LANES)
+            low = h < per_group // 2
+            of = slice((h % (per_group // 2)) * LANES, (h % (per_group // 2) + 1) * LANES)
+            state = jnp.where((side == 0) == low, keep_ref[of, :], got_ref[of, :])
+            cross = dot(c_rows, state)
+            value = y_ref[:, at] + columns_ref[0, :, head : head + 1] * cross
+            gate = 0.5 * gated_ref[:, at]
+            value = value * (gate * jnp.tanh(gate) + gate)
+            gated_ref[:, at] = value
+            squares = squares + value * value
+        mean = jnp.sum(squares, axis=1, keepdims=True) * (1.0 / width)
+        scale = lax.rsqrt(mean + 1e-05)
+        for h in range(per_group):
+            at = slice(h * LANES, (h + 1) * LANES)
+            to = slice((part * per_group + h) * LANES, (part * per_group + h + 1) * LANES)
+            out_ref[:, to] = (gated_ref[:, at] * scale * gain_ref[:, to].astype(F32)).astype(BF16)
 
 
 def shape(*dims, dtype=BF16):
@@ -383,32 +473,27 @@
     dims = (owners, columns, block_rows, over, width, heads)
     slots = owners * columns * ROWS
     finds = 3 if over else 1
-    rows_of = width // owners
     anchor = anchor.reshape(1, load_rows)
     place = lax.axis_index("ctx").astype(jnp.int32).reshape(1)
 
     arrived_x = []
-    arrived_z = []
     for part in range(groups):
         smalls = (b_load, c_load, dt_load) if part == 0 else (b_load, c_load)
         sent = pack(anchor, x_load, smalls, part, dims, 2 if part == 0 else 1)
         arrived_x.append(exchange(sent, BOTH).reshape(slots, sent.shape[2]))
-    for part in range(groups):
-        sent = pack(anchor, z_load, (), part, dims, 0)
-        arrived_z.append(exchange(sent, BOTH).reshape(slots, sent.shape[2]))
-
-    rows_x, both, partial, states = [], [], [], []
+    sent = pack(anchor, z_load, (), None, dims, 0)
+    arrived_z = exchange(sent, BOTH).reshape(slots, sent.shape[2])
+
+    finals = []
     per_part = (
         shape(block_rows, width),
         shape(2, block_rows, LANES),
     )
-    state_shape = shape(owners, rows_of + ROWS, LANES)
+    state_shape = shape(width + ROWS, LANES)
     for part in range(groups):
         if part == 0:
-            finder, row_values, both_0, rows_0, columns_0, local = pl.pallas_call(
-                lambda p, l, a, b, r, q, x, bc, ro, co, st: first_kernel(
-                    dims, p, l, a, b, r, q, x, bc, ro, co, st
-                ),
+            finder, row_values, both, rows_0, columns_0, local = pl.pallas_call(
+                functools.partial(first_kernel, dims),
                 in_specs=[SMEM, SMEM, VMEM, VMEM, VMEM],
                 out_specs=[VMEM] * 6,
                 out_shape=(
@@ -421,15 +506,9 @@
                 ),
                 compiler_params=PARAMS,
                 name="land_first",
-            )(
-                place,
-                doc_lengths,
-                arrived_x[0],
-                dt_bias.reshape(1, heads),
-                a_log.reshape(1, heads),
-            )
+            )(place, doc_lengths, arrived_x[0], dt_bias.reshape(1, heads), a_log.reshape(1, heads))
         else:
-            row_values, both_0, local = pl.pallas_call(
+            row_values, both, local = pl.pallas_call(
                 functools.partial(later_kernel, dims, part),
                 in_specs=[VMEM] * 4,
                 out_specs=[VMEM] * 3,
@@ -437,54 +516,45 @@
                 compiler_params=PARAMS,
                 name="land_later",
             )(arrived_x[part], finder, rows_0, columns_0)
-        rows_x.append(row_values)
-        both.append(both_0)
-        gathered = exchange(local, "ctx")
-        scanned = pl.pallas_call(
-            functools.partial(scan_kernel, part, per_group),
-            in_specs=[SMEM, VMEM],
+        keep, got = enter(part, place, local)
+        partial = pl.pallas_call(
+            functools.partial(intra_kernel, part),
+            in_specs=[SMEM, SMEM, SMEM, VMEM, VMEM, VMEM, VMEM],
             out_specs=VMEM,
-            out_shape=shape(owners, rows_of, LANES),
+            out_shape=shape(block_rows, width, dtype=F32),
             compiler_params=PARAMS,
-            name="scan",
-        )(place, gathered)
-        states.append(exchange(scanned, "ctx").reshape(width, LANES))
-        partial.append(
-            pl.pallas_call(
-                functools.partial(intra_kernel, part),
-                in_specs=[SMEM, SMEM, SMEM, VMEM, VMEM, VMEM, VMEM],
-                out_specs=VMEM,
-                out_shape=shape(block_rows, width, dtype=F32),
-                compiler_params=PARAMS,
-                name="intra",
-            )(place, doc_lengths, skip_gain, row_values, both_0, rows_0, columns_0)
-        )
-
-    result = None
+            name="intra",
+        )(place, doc_lengths, skip_gain, row_values, both, rows_0, columns_0)
+        finals += [partial, both, keep, got]
+
+    tile = block_rows // 4
+    full = lambda a: pl.BlockSpec(a.shape, lambda i, n=a.ndim: (0,) * n)
     gain = norm_gain.reshape(1, groups * width)
+    in_specs = [
+        SMEM,
+        full(arrived_z),
+        pl.BlockSpec((tile, finds * slots), lambda i: (i, 0)),
+        pl.BlockSpec((1, tile, LANES), lambda i: (1, i, 0)),
+        full(gain),
+    ]
     for part in range(groups):
-        whole = pl.BlockSpec(memory_space=pltpu.VMEM)
-        operands = [arrived_z[part], finder, partial[part], both[part], states[part], columns_0, gain]
-        full = lambda a: pl.BlockSpec(a.shape, lambda i, n=a.ndim: (0,) * n)
-        in_specs = [full(a) for a in operands[:-1]]
-        in_specs.append(pl.BlockSpec((1, width), lambda i, part=part: (0, part)))
-        aliases = {}
-        if result is not None:
-            aliases = {len(operands): 0}
-            operands.append(result)
-            in_specs.append(pl.BlockSpec(memory_space=pl.ANY))
-        result = pl.pallas_call(
-            functools.partial(final_kernel, over, part),
-            grid=(1,),
-            in_specs=in_specs,
-            out_specs=pl.BlockSpec((block_rows, width), lambda i, part=part: (0, part)),
-            out_shape=shape(block_rows, groups * width),
-            scratch_shapes=[pltpu.VMEM((block_rows, width), F32)],
-            input_output_aliases=aliases,
-            compiler_params=PARAMS,
-            name="final",
-        )(*operands)
-    return result
+        keep = finals[4 * part + 2]
+        in_specs += [
+            pl.BlockSpec((tile, width), lambda i: (i, 0)),
+            pl.BlockSpec((1, tile, LANES), lambda i: (1, i, 0)),
+            full(keep),
+            full(keep),
+        ]
+    return pl.pallas_call(
+        functools.partial(final_kernel, over, groups),
+        grid=(block_rows // tile,),
+        in_specs=in_specs,
+        out_specs=pl.BlockSpec((tile, groups * width), lambda i: (i, 0)),
+        out_shape=shape(block_rows, groups * width),
+        scratch_shapes=[pltpu.VMEM((tile, width), F32)],
+        compiler_params=PARAMS,
+        name="final",
+    )(place, arrived_z, finder, columns_0, gain, *finals)
 
 
 def solution(mesh):
@@ -502,4 +572,5 @@
         P(BOTH),
     )
     out_specs = P("ctx", "head")
+
     return jax.shard_map(body, mesh=mesh, in_specs=in_specs, out_specs=out_specs, check_vma=False)

time: 266 us -> 225 us (0.85)
  waiting for transfers between devices: 167 us -> 123 us
  starting transfers between devices: 45.7 us -> 25.8 us
  Pallas kernels: 47.8 us -> 62.1 us
  local copies, waits for them, and re-layouts: 2.6 us -> 10.4 us
    all_to_all x8 -> x3, waiting for transfers between devices: 167 us -> 70.2 us  [exchange(): return lax.all_to_all(values, axes, split_axis=0, concat_axis=0, tiled=True)]
    ppermute x0 -> x10, waiting for transfers between devices: none -> 52.9 us  [the longest x6 29.3 us: enter(): received.append(lax.ppermute(sent, 'ctx', hops))]
    all_to_all x8 -> x3, starting transfers between devices: 45.7 us -> 18.3 us  [exchange(): return lax.all_to_all(values, axes, split_axis=0, concat_axis=0, tiled=True)]
    pallas_call x5 -> x12, Pallas kernels: 18.8 us -> 34.3 us  [the longest x1 9.48 us: body(): pl.pallas_call(functools.partial(final_kernel, over, groups), grid=(block...]
    unnamed x16 -> x26, local copies, waits for them, and re-layouts: 1.99 us -> 9.78 us
    ppermute x0 -> x10, starting transfers between devices: none -> 7.49 us  [the longest x6 5.35 us: enter(): received.append(lax.ppermute(sent, 'ctx', hops))]
    pallas_call x4 -> x3, Pallas kernels: 16.9 us -> 15.7 us  [pack(): pl.pallas_call(functools.partial(pack_kernel, owners, block_rows, over, w...]
  transfers between devices with their start and end apart: 8 -> 13, of which waited for: 7 -> 6; matrix products, arithmetic and copies ran while one was open for 0% -> 0% of each run, Pallas kernels for 15% -> 22%
where the time goes in v2:
time: 225 us; the launch traced here: 222 us
  waiting for transfers between devices  123 us (55%)
  Pallas kernels  62.1 us (28%)
  starting transfers between devices  25.8 us (11%)
  local copies, waits for them, and re-layouts  10.4 us (5%)
    all_to_all x3, waiting for transfers between devices, exchange(): return lax.all_to_all(values, axes, split_axis=0, concat_axis=0, tiled=True)  70.2 us
    ppermute x6, waiting for transfers between devices, enter(): received.append(lax.ppermute(sent, 'ctx', hops))  29.3 us
    ppermute x2, waiting for transfers between devices, enter(): got = lax.ppermute(offered, 'ctx', pairs)  23.6 us
    all_to_all x3, starting transfers between devices, exchange(): return lax.all_to_all(values, axes, split_axis=0, concat_axis=0, tiled=True)  18.3 us
    pallas_call x3, Pallas kernels, pack(): pl.pallas_call(functools.partial(pack_kernel, owners, block_rows, over, w...  15.7 us
    unnamed x26, local copies, waits for them, and re-layouts  9.78 us
    pallas_call x1, Pallas kernels, body(): pl.pallas_call(functools.partial(final_kernel, over, groups), grid=(block...  9.48 us
    pallas_call x2, Pallas kernels, body(): pl.pallas_call(functools.partial(intra_kernel, part), in_specs=[SMEM, SME...  8.5 us
  transfers between devices with their start and end apart: 13, of which 6 were waited for; matrix products, arithmetic and copies ran while one was open for 0% of the time, Pallas kernels for 22%

profile of v2, /device:TPU:27, one launch (start us, length us, event | category | flops | bytes accessed | tf_op | source)
XLA Modules:
  0.0 221.5 jit_solution(9511791430567715892)
XLA Ops:
  0.0 4.2 %shard_map.111 = bf16[8,4,8,3456]{3,2,1,0:T(8,128)(2,1)} custom-call(s32[1,64]{1,0:T(1,128)} %bitcast.16, bf16[64,16384]{1,0:T(8,128)(2,1)} %wide_ref.5, bf16[64,1024]{1,0:T(8,128)(2,1)} %refs_0_.3, bf16[64,1024]{1,0:T(8,128)(2,1)} %refs_1_.3), custom_call_target="tpu_custom_call" | custom-call | tf_op jit(solution)/shard_map/pallas_call | solution.py:118
  4.2 6.2 %all-to-all-start.2 = ((bf16[32,8,3456]{2,1,0:T(8,128)(2,1)}), bf16[32,8,3456]{2,1,0:T(8,128)(2,1)S(1)}, u32[]{:S(2)}, u32[]{:S(2)}) async-start(bf16[32,8,3456]{2,1,0:T(8,128)(2,1)} %bitcast.15), calls=%async_computation.2 | async-start | bytes 3538944 | tf_op jit(solution)/shard_map/all_to_all | solution.py:130
  10.4 4.3 %shard_map.110 = bf16[8,4,8,3712]{3,2,1,0:T(8,128)(2,1)} custom-call(s32[1,64]{1,0:T(1,128)} %bitcast.17, bf16[64,16384]{1,0:T(8,128)(2,1)} %wide_ref.5, bf16[64,1024]{1,0:T(8,128)(2,1)} %refs_0_.3, bf16[64,1024]{1,0:T(8,128)(2,1)} %refs_1_.3, bf16[64,128]{1,0:T(8,128)(2,1)} %refs_2_.1), custom_call_target="tpu_custom_call" | custom-call | tf_op jit(solution)/shard_map/pallas_call | solution.py:118
  14.7 35.1 %all-to-all-done.2 = bf16[32,8,3456]{2,1,0:T(8,128)(2,1)S(1)} async-done(((bf16[32,8,3456]{2,1,0:T(8,128)(2,1)}), bf16[32,8,3456]{2,1,0:T(8,128)(2,1)S(1)}, u32[]{:S(2)}, u32[]{:S(2)}) %all-to-all-start.2) | async-done | bytes 1769504 | tf_op jit(solution)/shard_map/all_to_all | solution.py:130
  49.8 1.2 copy-done.2
  51.1 6.0 %all-to-all-start.1 = ((bf16[32,8,3712]{2,1,0:T(8,128)(2,1)}), bf16[32,8,3712]{2,1,0:T(8,128)(2,1)S(1)}, u32[]{:S(2)}, u32[]{:S(2)}) async-start(bf16[32,8,3712]{2,1,0:T(8,128)(2,1)} %bitcast.13), calls=%async_computation.1 | async-start | bytes 3801088 | tf_op jit(solution)/shard_map/all_to_all | solution.py:130
  57.1 7.1 %shard_map.109 = bf16[8,4,8,6144]{3,2,1,0:T(8,128)(2,1)} custom-call(s32[1,64]{1,0:T(1,128)} %bitcast.18, bf16[64,16384]{1,0:T(8,128)(2,1)} %wide_ref.3), custom_call_target="tpu_custom_call" | custom-call | tf_op jit(solution)/shard_map/pallas_call | solution.py:118
  64.2 35.1 %all-to-all-done.1 = bf16[32,8,3712]{2,1,0:T(8,128)(2,1)S(1)} async-done(((bf16[32,8,3712]{2,1,0:T(8,128)(2,1)}), bf16[32,8,3712]{2,1,0:T(8,128)(2,1)S(1)}, u32[]{:S(2)}, u32[]{:S(2)}) %all-to-all-start.1) | async-done | bytes 1900576 | tf_op jit(solution)/shard_map/all_to_all | solution.py:130
  99.3 1.2 copy-done.1
  100.6 6.1 %all-to-all-start = ((bf16[32,8,6144]{2,1,0:T(8,128)(2,1)}), bf16[32,8,6144]{2,1,0:T(8,128)(2,1)S(1)}, u32[]{:S(2)}, u32[]{:S(2)}) async-start(bf16[32,8,6144]{2,1,0:T(8,128)(2,1)} %bitcast.11), calls=%async_computation | async-start | bytes 6291456 | tf_op jit(solution)/shard_map/all_to_all | solution.py:130
  106.7 4.2 %land_first.1 = (bf16[256,768]{1,0:T(8,128)(2,1)}, bf16[256,2048]{1,0:T(8,128)(2,1)}, bf16[2,256,128]{2,1,0:T(8,128)(2,1)}, f32[3,32,256]{2,1,0:T(8,128)}, f32[2...) custom-call(s32[1]{0:T(128)} %bitcast.place_ref, s32[16]{0:T(128)} %lengths_ref.5, bf16[256,3712]{1,0:T(8,128)(2,1)} %bitcast.12, ...), custom_call_target="tpu_custom_call" | custom-call | tf_op jit(solution)/shard_map/land_first/pallas_call | solution.py:495
  110.8 1.8 offer.2
  112.9 3.6 %land_later.1 = (bf16[256,2048]{1,0:T(8,128)(2,1)}, bf16[2,256,128]{2,1,0:T(8,128)(2,1)}, bf16[2056,128]{1,0:T(8,128)(2,1)}) custom-call(bf16[256,3456]{1,0:T(8,128)(2,1)} %bitcast.14, bf16[256,768]{1,0:T(8,128)(2,1)} %get-tuple-element.24.q_ref, f32[3,32,256]{2,1,0:T(8,128)} %get-tuple-element.28.rows_ref, f32[2,256,128]{2,1,0:T(8,128)} %get-tuple-element.25.columns_ref), custom_call_target="tpu_custom_call" | custom-call | tf_op jit(solution)/shard_map/land_later/pallas_call | solution.py:511
  116.6 1.8 offer.3
  118.4 1.2 collective-permute-start.5
  119.6 19.8 %collective-permute-done.got_ref = bf16[1032,128]{1,0:T(8,128)(2,1)S(1)} collective-permute-done((bf16[1032,128]{1,0:T(8,128)(2,1)}, bf16[1032,128]{1,0:T(8,128)(2,1)S(1)}, u32[]{:S(2)}, u32[]{:S(2)}) %collective-permute-start) | collective-permute-done | bytes 264224 | tf_op jit(solution)/shard_map/ppermute | solution.py:381
  139.4 0.7 copy-done.4
  140.1 2.2 meet.2
  142.3 0.7 collective-permute-start.1
  143.0 3.7 %collective-permute-done.5.got_ref = bf16[1032,128]{1,0:T(8,128)(2,1)S(1)} collective-permute-done((bf16[1032,128]{1,0:T(8,128)(2,1)}, bf16[1032,128]{1,0:T(8,128)(2,1)S(1)}, u32[]{:S(2)}, u32[]{:S(2)}) %collective-permute-start.5) | collective-permute-done | bytes 264224 | tf_op jit(solution)/shard_map/ppermute | solution.py:381
  146.7 0.7 copy-done.3
  147.4 2.2 meet.3
  149.6 0.7 collective-permute-start.6
  150.3 0.7 copy-done.6
  151.0 2.0 step.4
  152.9 0.7 collective-permute-start.2
  153.6 0.7 copy-done.5
  154.3 2.0 step.6
  156.3 0.7 collective-permute-start.7
  157.0 0.7 copy-done.8
  157.7 2.0 step.5
  159.7 1.4 collective-permute-start.3
  161.1 0.7 copy-done.7
  161.8 2.0 step.7
  163.8 1.3 collective-permute-start.8
  165.1 26.9 %collective-permute-done.3.refs_2_ = bf16[1024,128]{1,0:T(8,128)(2,1)S(1)} collective-permute-done((bf16[1024,128]{1,0:T(8,128)(2,1)}, bf16[1024,128]{1,0:T(8,128)(2,1)S(1)}, u32[]{:S(2)}, u32[]{:S(2)}) %collective-permute-start.3) | collective-permute-done | bytes 262176 | tf_op jit(solution)/shard_map/ppermute | solution.py:403
  192.0 0.7 copy-done.11
  192.7 2.4 %split.2 = (bf16[1024,128]{1,0:T(8,128)(2,1)}, bf16[1024,128]{1,0:T(8,128)(2,1)}) custom-call(s32[1]{0:T(128)} %bitcast.place_ref, bf16[2056,128]{1,0:T(8,128)(2,1)} %get-tuple-element.29.state_ref, bf16[1032,128]{1,0:T(8,128)(2,1)} %copy-done.4, bf16[1024,128]{1,0:T(8,128)(2,1)} %copy-done.6, bf16[1024,128]{1,0:T(8,128)(2,1)} %copy-done.8, ...), custom_call_target="tpu_custom_call" | custom-call | tf_op jit(solution)/shard_map/split/pallas_call | solution.py:404
  195.1 0.3 collective-permute-start.4
  195.4 2.4 %collective-permute-done.8.refs_2_ = bf16[1024,128]{1,0:T(8,128)(2,1)S(1)} collective-permute-done((bf16[1024,128]{1,0:T(8,128)(2,1)}, bf16[1024,128]{1,0:T(8,128)(2,1)S(1)}, u32[]{:S(2)}, u32[]{:S(2)}) %collective-permute-start.8) | collective-permute-done | bytes 262176 | tf_op jit(solution)/shard_map/ppermute | solution.py:403
  197.8 0.7 copy-done.10
  198.5 2.4 %split.3 = (bf16[1024,128]{1,0:T(8,128)(2,1)}, bf16[1024,128]{1,0:T(8,128)(2,1)}) custom-call(s32[1]{0:T(128)} %bitcast.place_ref, bf16[2056,128]{1,0:T(8,128)(2,1)} %get-tuple-element.37.state_ref, bf16[1032,128]{1,0:T(8,128)(2,1)} %copy-done.3, bf16[1024,128]{1,0:T(8,128)(2,1)} %copy-done.5, bf16[1024,128]{1,0:T(8,128)(2,1)} %copy-done.7, ...), custom_call_target="tpu_custom_call" | custom-call | tf_op jit(solution)/shard_map/split/pallas_call | solution.py:404
  201.2 0.6 reshape.41.gain_ref
  201.8 4.3 %intra.2.refs_0_ = f32[256,2048]{1,0:T(8,128)} custom-call(s32[1]{0:T(128)} %bitcast.place_ref, s32[16]{0:T(128)} %lengths_ref.5, f32[32]{0:T(128)} %skip_ref.3, bf16[256,2048]{1,0:T(8,128)(2,1)} %get-tuple-element.26.x_ref, bf16[2,256,128]{2,1,0:T(8,128)(2,1)} %get-tuple-element.27.bc_ref.refs_1_, f32[3,32,256]{2,1,0:T(8,128)} %get-tuple-element.28.rows_ref, ...), custom_call_target="tpu_custom_call" | custom-call | tf_op jit(solution)/shard_map/intra/pallas_call | solution.py:520
  206.1 4.2 %intra.3.refs_4_ = f32[256,2048]{1,0:T(8,128)} custom-call(s32[1]{0:T(128)} %bitcast.place_ref, s32[16]{0:T(128)} %lengths_ref.5, f32[32]{0:T(128)} %skip_ref.3, bf16[256,2048]{1,0:T(8,128)(2,1)} %get-tuple-element.35.x_ref, bf16[2,256,128]{2,1,0:T(8,128)(2,1)} %get-tuple-element.36.bc_ref.refs_5_, f32[3,32,256]{2,1,0:T(8,128)} %get-tuple-element.28.rows_ref, ...), custom_call_target="tpu_custom_call" | custom-call | tf_op jit(solution)/shard_map/intra/pallas_call | solution.py:520
  210.4 0.7 copy-done.9
  211.1 1.0 copy-done
  212.1 9.5 %final.1 = bf16[256,4096]{1,0:T(8,128)(2,1)} custom-call(s32[1]{0:T(128)} %bitcast.place_ref, bf16[256,6144]{1,0:T(8,128)(2,1)} %bitcast.10, bf16[256,768]{1,0:T(8,128)(2,1)} %get-tuple-element.24.q_ref, f32[2,256,128]{2,1,0:T(8,128)} %get-tuple-element.25.columns_ref, bf16[1,4096]{1,0:T(2,128)(2,1)} %reshape.41.gain_ref, f32[256,2048]{1,0:T(8,128)} %intra.2.refs_0_, ...), custom_call_target="tpu_custom_call" | custom-call | tf_op jit(solution)/shard_map/final/pallas_call | solution.py:548
  (23 shorter events, 0.6 us)
Async XLA Ops:
  4.2 45.6 %all-to-all-start.2 = ((bf16[32,8,3456]{2,1,0:T(8,128)(2,1)}), bf16[32,8,3456]{2,1,0:T(8,128)(2,1)S(1)}, u32[]{:S(2)}, u32[]{:S(2)}) async-start(bf16[32,8,3456]{2,1,0:T(8,128)(2,1)} %bitcast.15), calls=%async_computation.2 | async-start | bytes 3538944 | tf_op jit(solution)/shard_map/all_to_all | solution.py:130
  49.8 1.2 copy-start.2
  51.1 48.2 %all-to-all-start.1 = ((bf16[32,8,3712]{2,1,0:T(8,128)(2,1)}), bf16[32,8,3712]{2,1,0:T(8,128)(2,1)S(1)}, u32[]{:S(2)}, u32[]{:S(2)}) async-start(bf16[32,8,3712]{2,1,0:T(8,128)(2,1)} %bitcast.13), calls=%async_computation.1 | async-start | bytes 3801088 | tf_op jit(solution)/shard_map/all_to_all | solution.py:130
  99.3 1.2 copy-start.1
  100.6 109.8 %all-to-all-start = ((bf16[32,8,6144]{2,1,0:T(8,128)(2,1)}), bf16[32,8,6144]{2,1,0:T(8,128)(2,1)S(1)}, u32[]{:S(2)}, u32[]{:S(2)}) async-start(bf16[32,8,6144]{2,1,0:T(8,128)(2,1)} %bitcast.11), calls=%async_computation | async-start | bytes 6291456 | tf_op jit(solution)/shard_map/all_to_all | solution.py:130
  112.7 26.7 %collective-permute-start = (bf16[1032,128]{1,0:T(8,128)(2,1)}, bf16[1032,128]{1,0:T(8,128)(2,1)S(1)}, u32[]{:S(2)}, u32[]{:S(2)}) collective-permute-start(bf16[1032,128]{1,0:T(8,128)(2,1)} %offer.2), channel_id=1, source_target_pairs={{0,4},{4,0},{8,12},{12,8},{16,20},{20,16},{24,28},{28,24},{1,5},{5... | collective-permute-start | bytes 792584 | tf_op jit(solution)/shard_map/ppermute | solution.py:381
  118.4 28.4 %collective-permute-start.5 = (bf16[1032,128]{1,0:T(8,128)(2,1)}, bf16[1032,128]{1,0:T(8,128)(2,1)S(1)}, u32[]{:S(2)}, u32[]{:S(2)}) collective-permute-start(bf16[1032,128]{1,0:T(8,128)(2,1)} %offer.3), channel_id=1, source_target_pairs={{0,4},{4,0},{8,12},{12,8},{16,20},{20,16},{24,28},{28,24},{1,5},{5... | collective-permute-start | bytes 792584 | tf_op jit(solution)/shard_map/ppermute | solution.py:381
  139.4 0.7 copy-start.4
  142.3 7.9 %collective-permute-start.1 = (bf16[1024,128]{1,0:T(8,128)(2,1)}, bf16[1024,128]{1,0:T(8,128)(2,1)S(1)}, u32[]{:S(2)}, u32[]{:S(2)}) collective-permute-start(bf16[1024,128]{1,0:T(8,128)(2,1)} %get-tuple-element.30), channel_id=1, source_target_pairs={{0,8},{4,12},{1,9},{5,13},{2,10},{6,14},{3,11},{7,15}} | collective-permute-start | bytes 786440 | tf_op jit(solution)/shard_map/ppermute | solution.py:403
  146.7 0.7 copy-start.3
  149.6 4.1 %collective-permute-start.6 = (bf16[1024,128]{1,0:T(8,128)(2,1)}, bf16[1024,128]{1,0:T(8,128)(2,1)S(1)}, u32[]{:S(2)}, u32[]{:S(2)}) collective-permute-start(bf16[1024,128]{1,0:T(8,128)(2,1)} %get-tuple-element.38), channel_id=1, source_target_pairs={{0,8},{4,12},{1,9},{5,13},{2,10},{6,14},{3,11},{7,15}} | collective-permute-start | bytes 786440 | tf_op jit(solution)/shard_map/ppermute | solution.py:403
  150.2 0.7 copy-start.6
  152.9 4.0 %collective-permute-start.2 = (bf16[1024,128]{1,0:T(8,128)(2,1)}, bf16[1024,128]{1,0:T(8,128)(2,1)S(1)}, u32[]{:S(2)}, u32[]{:S(2)}) collective-permute-start(bf16[1024,128]{1,0:T(8,128)(2,1)} %step.4), channel_id=1, source_target_pairs={{8,16},{12,20},{9,17},{13,21},{10,18},{14,22},{11,19},{15,23}} | collective-permute-start | bytes 786440 | tf_op jit(solution)/shard_map/ppermute | solution.py:403
  153.6 0.7 copy-start.5
  156.3 4.8 %collective-permute-start.7 = (bf16[1024,128]{1,0:T(8,128)(2,1)}, bf16[1024,128]{1,0:T(8,128)(2,1)S(1)}, u32[]{:S(2)}, u32[]{:S(2)}) collective-permute-start(bf16[1024,128]{1,0:T(8,128)(2,1)} %step.6), channel_id=1, source_target_pairs={{8,16},{12,20},{9,17},{13,21},{10,18},{14,22},{11,19},{15,23}} | collective-permute-start | bytes 786440 | tf_op jit(solution)/shard_map/ppermute | solution.py:403
  157.0 0.7 copy-start.8
  159.7 41.5 %copy-start.12 = (bf16[4096]{0:T(1024)(128)(2,1)S(1)}, bf16[4096]{0:T(1024)(128)(2,1)}, u32[]{:S(2)}) copy-start(bf16[4096]{0:T(1024)(128)(2,1)} %param.19) | copy-start | bytes 24580
  159.7 32.3 %collective-permute-start.3 = (bf16[1024,128]{1,0:T(8,128)(2,1)}, bf16[1024,128]{1,0:T(8,128)(2,1)S(1)}, u32[]{:S(2)}, u32[]{:S(2)}) collective-permute-start(bf16[1024,128]{1,0:T(8,128)(2,1)} %step.5), channel_id=1, source_target_pairs={{16,24},{20,28},{17,25},{21,29},{18,26},{22,30},{19,27},{23,31}} | collective-permute-start | bytes 786440 | tf_op jit(solution)/shard_map/ppermute | solution.py:403
  161.1 0.7 copy-start.7
  163.8 34.0 %collective-permute-start.8 = (bf16[1024,128]{1,0:T(8,128)(2,1)}, bf16[1024,128]{1,0:T(8,128)(2,1)S(1)}, u32[]{:S(2)}, u32[]{:S(2)}) collective-permute-start(bf16[1024,128]{1,0:T(8,128)(2,1)} %step.7), channel_id=1, source_target_pairs={{16,24},{20,28},{17,25},{21,29},{18,26},{22,30},{19,27},{23,31}} | collective-permute-start | bytes 786440 | tf_op jit(solution)/shard_map/ppermute | solution.py:403
  192.0 0.7 copy-start.11
  195.1 15.3 %collective-permute-start.4 = (bf16[1024,128]{1,0:T(8,128)(2,1)}, bf16[1024,128]{1,0:T(8,128)(2,1)S(1)}, u32[]{:S(2)}, u32[]{:S(2)}) collective-permute-start(bf16[1024,128]{1,0:T(8,128)(2,1)} %get-tuple-element.34), channel_id=1, source_target_pairs={{0,4},{4,0},{8,12},{12,8},{16,20},{20,16},{24,28},{28,24},{1,5},{5... | collective-permute-start | bytes 786440 | tf_op jit(solution)/shard_map/ppermute | solution.py:411
  197.8 0.7 copy-start.10
  200.9 9.5 %collective-permute-start.9 = (bf16[1024,128]{1,0:T(8,128)(2,1)}, bf16[1024,128]{1,0:T(8,128)(2,1)}, u32[]{:S(2)}, u32[]{:S(2)}) collective-permute-start(bf16[1024,128]{1,0:T(8,128)(2,1)} %get-tuple-element.42), channel_id=1, source_target_pairs={{0,4},{4,0},{8,12},{12,8},{16,20},{20,16},{24,28},{28,24},{1,5},{5... | collective-permute-start | bytes 786440 | tf_op jit(solution)/shard_map/ppermute | solution.py:411
  210.3 0.7 copy-start.9
  210.4 1.7 copy-start

commit v3 on v1

v3 whole, which is shorter than its diff:
```python
import functools

import jax
import jax.numpy as jnp
from jax import lax
from jax.experimental import pallas as pl
from jax.experimental.pallas import tpu as pltpu
from jax.sharding import PartitionSpec as P

LANES = 128
ROWS = 8
F32 = jnp.float32
BF16 = jnp.bfloat16
BOTH = ("ctx", "head")
VMEM = pl.BlockSpec(memory_space=pltpu.VMEM)
SMEM = pl.BlockSpec(memory_space=pltpu.SMEM)
PARAMS = pltpu.CompilerParams(vmem_limit_bytes=56 * 1024 * 1024)


def iota(shape, dim):
    return lax.broadcasted_iota(jnp.int32, shape, dim)


def dot(left, right):
    return jnp.dot(left, right, preferred_element_type=F32)


def onehot(mask):
    return jnp.where(mask, 1.0, 0.0).astype(BF16)


def send_onehots(anchor, owners, block_rows, over):
    rows = anchor.shape[1]
    owner = jnp.zeros_like(anchor)
    for k in range(1, owners):
        owner = owner + jnp.where(anchor >= k * block_rows, 1, 0)
    eye = iota((rows, rows), 0) == iota((rows, rows), 1)
    owner_f = owner.astype(F32)
    owner_col = jnp.sum(jnp.where(eye, owner_f, 0.0), axis=1, keepdims=True)
    earlier = (owner_col == owner_f) & (iota((rows, rows), 0) < iota((rows, rows), 1))
    rank = jnp.sum(jnp.where(earlier, 1.0, 0.0), axis=0, keepdims=True).astype(jnp.int32)
    place = (anchor - owner * block_rows + 1).astype(F32)
    place_col = jnp.sum(jnp.where(eye, place, 0.0), axis=1, keepdims=True)
    slot = iota((owners * ROWS, rows), 0)
    first = owner * ROWS + rank
    base = onehot((slot == first) & (rank < ROWS))
    if not over:
        return base, None, None, place_col
    low = onehot((slot == first - ROWS) & (rank >= ROWS))
    high = onehot((slot == first - ROWS // 2) & (rank >= ROWS))
    return base, low, high, place_col


def pack_kernel(dims, small, anchor_ref, wide_ref, *refs):
    owners, _, block_rows, over, groups, width, heads = dims
    out_ref, base_ref, extra_ref, place_ref = refs[-4:]
    load_rows = wide_ref.shape[0]

    @pl.when(pl.program_id(0) == 0)
    def _():
        base, low, high, place_col = send_onehots(anchor_ref[...], owners, block_rows, over)
        base_ref[...] = base
        place_ref[...] = jnp.broadcast_to(place_col, place_ref.shape)
        if over:
            extra_ref[:, 0:load_rows] = low
            extra_ref[:, load_rows:] = high

    def put(column, values):
        values = values.astype(BF16).reshape(owners, ROWS, values.shape[1])
        out_ref[:, 0, :, column : column + values.shape[2]] = values

    def folded(low, high):
        return dot(extra_ref[...], jnp.concatenate([low, high], axis=0))

    column = 0
    for part in range(groups):
        at = part * width
        put(column, dot(base_ref[...], wide_ref[:, at : at + width]))
        column += width
        if over:
            half = width // 2
            put(column, folded(wide_ref[:, at : at + half], wide_ref[:, at + half : at + width]))
            column += half
    if not small:
        return
    b_part, c_part, dt_part = refs[0][...], refs[1][...], refs[2][...]
    steps = dt_part.astype(F32)
    own = jnp.zeros_like(steps)
    lane = iota(steps.shape, 1)
    for k in range(LANES // heads):
        shifted = steps if k == 0 else pltpu.roll(steps, LANES - k * heads, 1)
        own = own + jnp.where(pl.program_id(0) == k, shifted, 0.0)
    meta = jnp.where(lane < heads, own, jnp.where(lane == heads, place_ref[...], 0.0))
    put(column, dot(base_ref[...], jnp.concatenate([b_part, c_part], axis=1)))
    column += 2 * b_part.shape[1]
    tile = dot(base_ref[...], meta.astype(BF16))
    if over:
        turned = pltpu.roll(meta, LANES // 2, 1).astype(BF16)
        tile = tile + dot(extra_ref[:, 0:load_rows], turned)
    put(column, tile)
    if over:
        put(column + LANES, folded(b_part, c_part))


def pack(anchor, wide, smalls, dims):
    owners, columns, _, over, groups, width, _ = dims
    load_rows = wide.shape[0]
    total = groups * (width * 3 // 2 if over else width)
    if smalls:
        total += LANES * (groups * (3 if over else 2) + 1)
    in_specs = [
        pl.BlockSpec((1, load_rows), lambda i: (0, 0)),
        pl.BlockSpec((load_rows, groups * width), lambda i: (0, i)),
    ]
    if smalls:
        in_specs += [pl.BlockSpec((load_rows, groups * LANES), lambda i: (0, i))] * 2
        in_specs += [pl.BlockSpec((load_rows, LANES), lambda i: (0, 0))]
    packed = pl.pallas_call(
        functools.partial(pack_kernel, dims, bool(smalls)),
        grid=(columns,),
        in_specs=in_specs,
        out_specs=pl.BlockSpec((owners, 1, ROWS, total), lambda i: (0, i, 0, 0)),
        out_shape=shape(owners, columns, ROWS, total),
        scratch_shapes=[
            pltpu.VMEM((owners * ROWS, load_rows), BF16),
            pltpu.VMEM((owners * ROWS, 2 * load_rows), BF16),
            pltpu.VMEM((load_rows, LANES), F32),
        ],
        compiler_params=PARAMS,
        name="pack",
    )(anchor, wide, *smalls)
    return packed.reshape(owners * columns, ROWS, total)


def exchange(values, axes):
    return lax.all_to_all(values, axes, split_axis=0, concat_axis=0, tiled=True)


def doc_counts(lengths_ref, positions):
    count = jnp.zeros_like(positions)
    start = jnp.int32(0)
    for k in range(lengths_ref.shape[0]):
        count = count + jnp.where(positions >= start, 1, 0)
        start = start + lengths_ref[k]
    return count


def column_of(row):
    size = row.shape[1]
    eye = iota((size, size), 0) == iota((size, size), 1)
    return jnp.sum(jnp.where(eye, row, 0.0), axis=1, keepdims=True)


def placed(q_ref, values_ref, over, width):
    slots = values_ref.shape[0]
    half = width // 2
    if not over:
        return dot(q_ref[...], values_ref[:, 0:half]), dot(q_ref[...], values_ref[:, half:width])
    extra = values_ref[:, width : width + half]
    first = jnp.concatenate([extra, values_ref[:, 0:half]], axis=0)
    second = jnp.concatenate([values_ref[:, half:width], extra], axis=0)
    return dot(q_ref[:, 0 : 2 * slots], first), dot(q_ref[:, slots : 3 * slots], second)


def land(dims, part, side, q_ref, wide_ref, small_ref, rows_ref, decay_ref, refs):
    _, _, _, over, groups, width, _ = dims
    x_ref, bc_ref, keep_ref, offer_ref = refs
    slots = wide_ref.shape[0]
    per_group = width // LANES
    b_slots = small_ref[:, part * LANES : (part + 1) * LANES]
    c_slots = small_ref[:, (groups + part) * LANES : (groups + part + 1) * LANES]
    if over:
        at = (2 * groups + 1 + part) * LANES
        extra = small_ref[:, at : at + LANES]
        b_all = dot(q_ref[:, 0 : 2 * slots], jnp.concatenate([extra, b_slots], axis=0))
        c_all = dot(q_ref[:, slots : 3 * slots], jnp.concatenate([c_slots, extra], axis=0))
    else:
        b_all = dot(q_ref[...], b_slots)
        c_all = dot(q_ref[...], c_slots)
    bc_ref[0] = b_all.astype(BF16)
    bc_ref[1] = c_all.astype(BF16)
    first, second = placed(q_ref, wide_ref, over, width)
    x_ref[:, 0 : width // 2] = first.astype(BF16)
    x_ref[:, width // 2 :] = second.astype(BF16)
    b_turned = b_all.T

    def state_of(h):
        head = part * per_group + h
        weighted = (b_turned * rows_ref[2, head : head + 1, :]).astype(BF16)
        return dot(weighted, x_ref[:, h * LANES : (h + 1) * LANES])

    half = per_group // 2
    for q in range(half):
        low, high = state_of(q), state_of(half + q)
        at = slice(q * LANES, (q + 1) * LANES)
        keep_ref[at, :] = jnp.where(side == 0, low, high).astype(BF16)
        offer_ref[at, :] = jnp.where(side == 0, high, low).astype(BF16)
    decay = decay_ref[part * per_group : (part + 1) * per_group, :]
    top = decay.astype(BF16).astype(F32)
    middle = (decay - top).astype(BF16).astype(F32)
    for k, piece in enumerate((top, middle, decay - top - middle)):
        at = slice(half * (LANES + k), half * (LANES + k + 1))
        keep_ref[at, :] = jnp.where(side == 0, piece[0:half], piece[half:]).astype(BF16)
        offer_ref[at, :] = jnp.where(side == 0, piece[half:], piece[0:half]).astype(BF16)


def fetch(arrived_ref, stride, part, dims, wide_ref, small_ref, sems):
    start = dims[4] * stride
    wide = pltpu.make_async_copy(
        arrived_ref.at[:, part * stride : (part + 1) * stride], wide_ref, sems.at[0]
    )
    small = pltpu.make_async_copy(
        arrived_ref.at[:, start : start + small_ref.shape[1]], small_ref, sems.at[1]
    )
    small.start()
    wide.start()
    small.wait()
    return wide


def first_kernel(
    dims,
    place_ref,
    lengths_ref,
    arrived_ref,
    bias_ref,
    rate_ref,
    q_ref,
    rows_ref,
    columns_ref,
    decay_ref,
    x_ref,
    bc_ref,
    keep_ref,
    offer_ref,
    wide_ref,
    small_ref,
    sems,
):
    _, _, block_rows, over, groups, _, heads = dims
    slots = arrived_ref.shape[0]
    wide = fetch(arrived_ref, wide_ref.shape[1], 0, dims, wide_ref, small_ref, sems)
    meta = small_ref[:, 2 * groups * LANES : (2 * groups + 1) * LANES]
    turned = meta.astype(F32).T
    target = iota((block_rows, slots), 0) + 1
    own = onehot(target == turned[heads : heads + 1, :].astype(jnp.int32))
    raw = dot(own, meta).T[0:heads, :]
    if over:
        half = ROWS // 2
        inside = iota((1, slots), 1) % ROWS
        spot = jnp.where(inside < half, turned[LANES // 2 + heads : LANES // 2 + heads + 1, :], 0.0)
        low = onehot(target == spot.astype(jnp.int32))
        high = onehot(target == pltpu.roll(spot, half, 1).astype(jnp.int32))
        q_ref[:, 0:slots] = low
        q_ref[:, slots : 2 * slots] = own
        q_ref[:, 2 * slots :] = high
        raw = raw + dot(low, meta).T[LANES // 2 : LANES // 2 + heads, :]
    else:
        q_ref[...] = own
    raw = raw + column_of(bias_ref[...])
    step = jnp.maximum(raw, 0.0) + jnp.log1p(jnp.exp(-jnp.abs(raw)))
    logs = -step * jnp.exp(column_of(rate_ref[...]))
    upper = jnp.where(
        iota((block_rows, block_rows), 0) <= iota((block_rows, block_rows), 1), 1.0, 0.0
    )
    cum = jnp.dot(logs, upper, preferred_element_type=F32, precision=lax.Precision.HIGHEST)
    start = place_ref[0] * block_rows
    docs = doc_counts(lengths_ref, start + iota((1, block_rows), 1))
    last = doc_counts(lengths_ref, start + block_rows - 1 + jnp.zeros((1, 1), jnp.int32))
    before = doc_counts(lengths_ref, start - 1 + jnp.zeros((1, 1), jnp.int32))
    end = cum[:, block_rows - 1 : block_rows]
    entry = jnp.where(docs == before, jnp.exp(cum), 0.0)
    rows_ref[0] = step
    rows_ref[1] = cum
    rows_ref[2] = jnp.where(docs == last, jnp.exp(end - cum), 0.0) * step
    blank = jnp.zeros((LANES - heads, block_rows), F32)
    columns_ref[0] = jnp.concatenate([cum, blank], axis=0).T
    columns_ref[1] = jnp.concatenate([entry, blank], axis=0).T
    decay_ref[...] = jnp.broadcast_to(entry[:, block_rows - 1 : block_rows], decay_ref.shape)
    wide.wait()
    refs = (x_ref, bc_ref, keep_ref, offer_ref)
    land(dims, 0, place_ref[0] % 2, q_ref, wide_ref, small_ref, rows_ref, decay_ref, refs)


def later_kernel(
    dims,
    part,
    place_ref,
    arrived_ref,
    q_ref,
    rows_ref,
    decay_ref,
    x_ref,
    bc_ref,
    keep_ref,
    offer_ref,
    wide_ref,
    small_ref,
    sems,
):
    fetch(arrived_ref, wide_ref.shape[1], part, dims, wide_ref, small_ref, sems).wait()
    refs = (x_ref, bc_ref, keep_ref, offer_ref)
    land(dims, part, place_ref[0] % 2, q_ref, wide_ref, small_ref, rows_ref, decay_ref, refs)


def intra_kernel(groups, place_ref, lengths_ref, skip_ref, rows_ref, columns_ref, *refs):
    y_ref = refs[-1]
    block_rows, width = refs[0].shape
    per_group = width // LANES
    start = place_ref[0] * block_rows
    square = (block_rows, block_rows)
    row_docs = doc_counts(lengths_ref, start + iota((1, block_rows), 1))
    column_docs = doc_counts(lengths_ref, start + iota((block_rows, 1), 0))
    keep = (iota(square, 0) >= iota(square, 1)) & (row_docs == column_docs)
    for part in range(groups):
        x_ref, bc_ref = refs[2 * part : 2 * part + 2]
        scores = lax.dot_general(
            bc_ref[1], bc_ref[0], (((1,), (1,)), ((), ())), preferred_element_type=F32
        )
        for h in range(per_group):
            head = part * per_group + h
            across = columns_ref[0, :, head : head + 1] - rows_ref[1, head : head + 1, :]
            decay = jnp.exp(jnp.where(keep, across, -jnp.inf))
            weights = (scores * decay * rows_ref[0, head : head + 1, :]).astype(BF16)
            x_head = x_ref[:, h * LANES : (h + 1) * LANES]
            y_ref[:, head * LANES : (head + 1) * LANES] = dot(weights, x_head) + skip_ref[
                head
            ] * x_head.astype(F32)


def enter(place, keep, offer):
    blocks = lax.axis_size("ctx")
    half = keep.shape[0] // (LANES + 3)
    pairs = [(i, i ^ 1) for i in range(blocks)]
    even = place % 2 == 0

    def parts(values):
        state = values[: half * LANES].reshape(half, LANES, LANES).astype(F32)
        decay = values[half * LANES :].reshape(3, half, 1, LANES).astype(F32)
        return state, decay[0] + decay[1] + decay[2]

    got = lax.ppermute(offer, "ctx", pairs)
    own_state, own_decay = parts(keep)
    got_state, got_decay = parts(got)
    first = jnp.where(even, own_state, got_state)
    first_decay = jnp.where(even, own_decay, got_decay)
    second = jnp.where(even, got_state, own_state)
    second_decay = jnp.where(even, got_decay, own_decay)
    total = second_decay * first + second
    decay = own_decay * got_decay
    sent = total.astype(BF16)
    entering = jnp.zeros_like(total)
    for k in range(blocks // 2 - 1):
        hops = [(2 * k + side, 2 * k + 2 + side) for side in range(2)]
        come = lax.ppermute(sent, "ctx", hops).astype(F32)
        sent = (decay * come + total).astype(BF16)
        entering = entering + come
    after = first_decay * entering + first
    kept = jnp.where(even, entering, after).astype(BF16)
    other = jnp.where(even, after, entering).astype(BF16)
    other = lax.ppermute(other, "ctx", pairs)
    return kept.reshape(half * LANES, LANES), other.reshape(half * LANES, LANES)


def final_kernel(over, groups, place_ref, arrived_ref, q_ref, columns_ref, y_ref, gain_ref, *refs):
    out_ref, gated_ref = refs[-2:]
    block_rows, width = out_ref.shape
    per_group = width // LANES
    side = place_ref[0] % 2

    def one(part):
        bc_ref, keep_ref, got_ref = refs[3 * part : 3 * part + 3]
        first, second = placed(q_ref, arrived_ref, over, width)
        gated_ref[:, 0 : width // 2] = first
        gated_ref[:, width // 2 :] = second
        c_rows = bc_ref[0]
        squares = jnp.zeros((block_rows, LANES), F32)
        for h in range(per_group):
            head = part * per_group + h
            at = slice(h * LANES, (h + 1) * LANES)
            low = h < per_group // 2
            of = slice((h % (per_group // 2)) * LANES, (h % (per_group // 2) + 1) * LANES)
            state = jnp.where((side == 0) == low, keep_ref[of, :], got_ref[of, :])
            cross = dot(c_rows, state)
            value = y_ref[:, at] + columns_ref[0, :, head : head + 1] * cross
            gate = 0.5 * gated_ref[:, at]
            value = value * (gate * jnp.tanh(gate) + gate)
            gated_ref[:, at] = value
            squares = squares + value * value
        mean = jnp.sum(squares, axis=1, keepdims=True) * (1.0 / width)
        scale = lax.rsqrt(mean + 1e-05)
        for h in range(per_group):
            at = slice(h * LANES, (h + 1) * LANES)
            out_ref[:, at] = (gated_ref[:, at] * scale * gain_ref[:, at].astype(F32)).astype(BF16)

    for part in range(groups):
        pl.when(pl.program_id(0) == part)(functools.partial(one, part))


def shape(*dims, dtype=BF16):
    return jax.ShapeDtypeStruct(dims, dtype)


def body(
    x_load,
    z_load,
    b_load,
    c_load,
    dt_load,
    dt_bias,
    a_log,
    skip_gain,
    norm_gain,
    doc_lengths,
    anchor,
):
    load_rows = anchor.shape[0]
    owners = lax.axis_size("ctx")
    columns = lax.axis_size("head")
    block_rows = load_rows * columns
    capacity = 3 * load_rows // (2 * owners)
    heads = dt_bias.shape[0]
    groups = b_load.shape[1] // (columns * LANES)
    per_group = heads // groups
    width = per_group * LANES
    over = capacity > ROWS
    dims = (owners, columns, block_rows, over, groups, width, heads)
    slots = owners * columns * ROWS
    finds = 3 if over else 1
    anchor = anchor.reshape(1, load_rows)
    number = lax.axis_index("ctx").astype(jnp.int32)
    place = number.reshape(1)

    sent = pack(anchor, x_load, (b_load, c_load, dt_load), dims)
    arrived_x = exchange(sent, BOTH).reshape(slots, sent.shape[2])
    sent_z = pack(anchor, z_load, (), dims)
    arrived_z = exchange(sent_z, BOTH).reshape(slots, sent_z.shape[2])

    stride = width * 3 // 2 if over else width
    carried = (per_group // 2) * (LANES + 3)
    per_part = (
        shape(block_rows, width),
        shape(2, block_rows, LANES),
        shape(carried, LANES),
        shape(carried, LANES),
    )
    scratch = [
        pltpu.VMEM((slots, stride), BF16),
        pltpu.VMEM((slots, arrived_x.shape[1] - groups * stride), BF16),
        pltpu.SemaphoreType.DMA((2,)),
    ]
    anywhere = pl.BlockSpec(memory_space=pl.ANY)
    blocks, states = [], []
    for part in range(groups):
        if part == 0:
            finder, rows, turned, decay, x_block, both, keep, offer = pl.pallas_call(
                functools.partial(first_kernel, dims),
                in_specs=[SMEM, SMEM, anywhere, VMEM, VMEM],
                out_specs=[VMEM] * 8,
                out_shape=(
                    shape(block_rows, finds * slots),
                    shape(3, heads, block_rows, dtype=F32),
                    shape(2, block_rows, LANES, dtype=F32),
                    shape(heads, LANES, dtype=F32),
                )
                + per_part,
                scratch_shapes=scratch,
                compiler_params=PARAMS,
                name="land_first",
            )(
                place,
                doc_lengths,
                arrived_x,
                dt_bias.reshape(1, heads),
                a_log.reshape(1, heads),
            )
        else:
            x_block, both, keep, offer = pl.pallas_call(
                functools.partial(later_kernel, dims, part),
                in_specs=[SMEM, anywhere, VMEM, VMEM, VMEM],
                out_specs=[VMEM] * 4,
                out_shape=per_part,
                scratch_shapes=scratch,
                compiler_params=PARAMS,
                name="land_later",
            )(place, arrived_x, finder, rows, decay)
        blocks += [x_block, both]
        states.append(enter(number, keep, offer))
    y = pl.pallas_call(
        functools.partial(intra_kernel, groups),
        in_specs=[SMEM, SMEM, SMEM] + [VMEM] * (2 + len(blocks)),
        out_specs=VMEM,
        out_shape=shape(block_rows, groups * width, dtype=F32),
        compiler_params=PARAMS,
        name="intra",
    )(place, doc_lengths, skip_gain, rows, turned, *blocks)

    full = lambda a: pl.BlockSpec(a.shape, lambda i, n=a.ndim: (0,) * n)
    second = pl.BlockSpec((1, block_rows, LANES), lambda i: (1, 0, 0))
    in_specs = [
        SMEM,
        pl.BlockSpec((slots, stride), lambda i: (0, i)),
        full(finder),
        second,
        pl.BlockSpec((block_rows, width), lambda i: (0, i)),
        pl.BlockSpec((1, width), lambda i: (0, i)),
    ]
    operands = []
    for part in range(groups):
        operands += [blocks[2 * part + 1], *states[part]]
        in_specs += [second, full(states[part][0]), full(states[part][1])]
    return pl.pallas_call(
        functools.partial(final_kernel, over, groups),
        grid=(groups,),
        in_specs=in_specs,
        out_specs=pl.BlockSpec((block_rows, width), lambda i: (0, i)),
        out_shape=shape(block_rows, groups * width),
        scratch_shapes=[pltpu.VMEM((block_rows, width), F32)],
        compiler_params=PARAMS,
        name="final",
    )(place, arrived_z, finder, turned, y, norm_gain.reshape(1, groups * width), *operands)


def solution(mesh):
    in_specs = (
        P(BOTH, None),
        P(BOTH, None),
        P(BOTH, None),
        P(BOTH, None),
        P(BOTH, None),
        P("head"),
        P("head"),
        P("head"),
        P("head"),
        P(),
        P(BOTH),
    )
    out_specs = P("ctx", "head")

    return jax.shard_map(body, mesh=mesh, in_specs=in_specs, out_specs=out_specs, check_vma=False)
```

time: 266 us -> 207 us (0.78)
  starting transfers between devices: 45.7 us -> 21.6 us
  waiting for transfers between devices: 167 us -> 143 us
  Pallas kernels: 47.8 us -> 33.2 us
  other arithmetic: 0 us -> 3.47 us
    all_to_all x8 -> x2, waiting for transfers between devices: 167 us -> 74 us  [exchange(): return lax.all_to_all(values, axes, split_axis=0, concat_axis=0, tiled=True)]
    ppermute x0 -> x10, waiting for transfers between devices: none -> 68.5 us  [the longest x6 41 us: enter(): come = lax.ppermute(sent, 'ctx', hops).astype(F32)]
    all_to_all x8 -> x2, starting transfers between devices: 45.7 us -> 14 us  [exchange(): return lax.all_to_all(values, axes, split_axis=0, concat_axis=0, tiled=True)]
    pallas_call x12 -> x6, Pallas kernels: 47.8 us -> 33.2 us  [the longest x2 9.8 us: pack(): pl.pallas_call(functools.partial(pack_kernel, dims, bool(smalls)), grid=(...]
    ppermute x0 -> x10, starting transfers between devices: none -> 7.67 us  [the longest x6 5.47 us: enter(): come = lax.ppermute(sent, 'ctx', hops).astype(F32)]
    convert_element_type x0 -> x12, other arithmetic: none -> 3.3 us  [the longest x2 2.07 us: enter(): other = jnp.where(even, after, entering).astype(BF16)]
  transfers between devices with their start and end apart: 8 -> 12, of which waited for: 7 -> 5; matrix products, arithmetic and copies ran while one was open for 0% -> 2% of each run, Pallas kernels for 15% -> 10%
where the time goes in v3:
time: 207 us; the launch traced here: 203 us
  waiting for transfers between devices  143 us (69%)
  Pallas kernels  33.2 us (16%)
  starting transfers between devices  21.6 us (10%)
  other arithmetic  3.47 us (2%)
  local copies, waits for them, and re-layouts  2.33 us (1%)
    all_to_all x2, waiting for transfers between devices, exchange(): return lax.all_to_all(values, axes, split_axis=0, concat_axis=0, tiled=True)  74 us
    ppermute x6, waiting for transfers between devices, enter(): come = lax.ppermute(sent, 'ctx', hops).astype(F32)  41 us
    ppermute x2, waiting for transfers between devices, enter(): got = lax.ppermute(offer, 'ctx', pairs)  27.5 us
    all_to_all x2, starting transfers between devices, exchange(): return lax.all_to_all(values, axes, split_axis=0, concat_axis=0, tiled=True)  14 us
    pallas_call x2, Pallas kernels, pack(): pl.pallas_call(functools.partial(pack_kernel, dims, bool(smalls)), grid=(...  9.8 us
    pallas_call x1, Pallas kernels, body(): pl.pallas_call(functools.partial(final_kernel, over, groups), grid=(group...  7.38 us
    pallas_call x1, Pallas kernels, body(): pl.pallas_call(functools.partial(intra_kernel, groups), in_specs=[SMEM, S...  6.49 us
    ppermute x6, starting transfers between devices, enter(): come = lax.ppermute(sent, 'ctx', hops).astype(F32)  5.47 us
  transfers between devices with their start and end apart: 12, of which 5 were waited for; matrix products, arithmetic and copies ran while one was open for 2% of the time, Pallas kernels for 10%

profile of v3, /device:TPU:27, one launch (start us, length us, event | category | flops | bytes accessed | tf_op | source)
XLA Modules:
  0.0 203.4 jit_solution(12197101570421742421)
XLA Ops:
  0.0 5.0 %pack.3 = bf16[8,4,8,7040]{3,2,1,0:T(8,128)(2,1)} custom-call(s32[1,64]{1,0:T(1,128)} %bitcast.28, bf16[64,16384]{1,0:T(8,128)(2,1)} %wide_ref.3, bf16[64,1024]{1,0:T(8,128)(2,1)} %refs_0_.1, bf16[64,1024]{1,0:T(8,128)(2,1)} %refs_1_.1, bf16[64,128]{1,0:T(8,128)(2,1)} %refs_2_.1), custom_call_target="tpu_custom_call" | custom-call | tf_op jit(solution)/shard_map/pack/pallas_call | solution.py:118
  5.0 6.2 %all-to-all-start.1 = ((bf16[32,8,7040]{2,1,0:T(8,128)(2,1)}), bf16[32,8,7040]{2,1,0:T(8,128)(2,1)}, u32[]{:S(2)}, u32[]{:S(2)}) async-start(bf16[32,8,7040]{2,1,0:T(8,128)(2,1)} %bitcast.16), calls=%async_computation.1 | async-start | bytes 7208960 | tf_op jit(solution)/shard_map/all_to_all | solution.py:136
  11.2 4.8 %pack.2 = bf16[8,4,8,6144]{3,2,1,0:T(8,128)(2,1)} custom-call(s32[1,64]{1,0:T(1,128)} %bitcast.29, bf16[64,16384]{1,0:T(8,128)(2,1)} %wide_ref.2), custom_call_target="tpu_custom_call" | custom-call | tf_op jit(solution)/shard_map/pack/pallas_call | solution.py:118
  16.0 74.0 %all-to-all-done.1 = bf16[32,8,7040]{2,1,0:T(8,128)(2,1)} async-done(((bf16[32,8,7040]{2,1,0:T(8,128)(2,1)}), bf16[32,8,7040]{2,1,0:T(8,128)(2,1)}, u32[]{:S(2)}, u32[]{:S(2)}) %all-to-all-start.1) | async-done | bytes 3604512 | tf_op jit(solution)/shard_map/all_to_all | solution.py:136
  90.0 7.8 %all-to-all-start = ((bf16[32,8,6144]{2,1,0:T(8,128)(2,1)}), bf16[32,8,6144]{2,1,0:T(8,128)(2,1)S(1)}, u32[]{:S(2)}, u32[]{:S(2)}) async-start(bf16[32,8,6144]{2,1,0:T(8,128)(2,1)} %bitcast.18), calls=%async_computation | async-start | bytes 6291456 | tf_op jit(solution)/shard_map/all_to_all | solution.py:136
  97.8 4.8 %land_first.1 = (bf16[256,768]{1,0:T(8,128)(2,1)}, f32[3,32,256]{2,1,0:T(8,128)}, f32[2,256,128]{2,1,0:T(8,128)}, f32[32,128]{1,0:T(8,128)}, bf16[256,2048]{1,0:...) custom-call(s32[1]{0:T(128)} %bitcast.place_ref, ...), custom_call_target="tpu_custom_call" | custom-call | tf_op jit(solution)/shard_map/land_first/pallas_call | solution.py:456
  102.6 0.0 copy-start.2
  102.6 0.3 collective-permute-start
  103.0 4.7 %land_later.1 = (bf16[256,2048]{1,0:T(8,128)(2,1)}, bf16[2,256,128]{2,1,0:T(8,128)(2,1)}, bf16[1048,128]{1,0:T(8,128)(2,1)}, bf16[1048,128]{1,0:T(8,128)(2,1)}) custom-call(s32[1]{0:T(128)} %bitcast.place_ref, bf16[256,7040]{1,0:T(8,128)(2,1)} %bitcast.5.arrived_ref, bf16[256,768]{1,0:T(8,128)(2,1)} %get-tuple-element.17.q_ref, ...), custom_call_target="tpu_custom_call" | custom-call | tf_op jit(solution)/shard_map/land_later/pallas_call | solution.py:478
  107.7 0.8 slice_convert_fusion.2
  108.5 1.2 collective-permute-start.5
  109.6 21.1 %collective-permute-done = bf16[1048,128]{1,0:T(8,128)(2,1)S(1)} collective-permute-done((bf16[1048,128]{1,0:T(8,128)(2,1)}, bf16[1048,128]{1,0:T(8,128)(2,1)S(1)}, u32[]{:S(2)}, u32[]{:S(2)}) %collective-permute-start) | collective-permute-done | bytes 268320 | tf_op jit(solution)/shard_map/ppermute | solution.py:342
  130.7 0.1 convert_select_fusion.2
  130.8 0.1 fusion.11
  130.9 0.7 collective-permute-start.1
  131.6 6.4 %collective-permute-done.5 = bf16[1048,128]{1,0:T(8,128)(2,1)S(1)} collective-permute-done((bf16[1048,128]{1,0:T(8,128)(2,1)}, bf16[1048,128]{1,0:T(8,128)(2,1)S(1)}, u32[]{:S(2)}, u32[]{:S(2)}) %collective-permute-start.5) | collective-permute-done | bytes 268320 | tf_op jit(solution)/shard_map/ppermute | solution.py:342
  138.0 0.0 copy-done.1
  138.0 0.1 convert_select_fusion
  138.1 0.1 fusion.10
  138.2 0.7 collective-permute-start.6
  138.9 0.0 collective-permute-done.1
  138.9 0.1 fusion.1
  139.0 0.7 collective-permute-start.2
  139.7 0.0 collective-permute-done.6
  139.7 0.1 fusion.6
  139.8 0.0 copy-start.4
  139.8 0.7 collective-permute-start.7
  140.5 0.0 collective-permute-done.2
  140.5 0.1 fusion.4
  140.6 1.3 collective-permute-start.3
  141.9 0.0 collective-permute-done.7
  141.9 0.1 fusion.9
  141.9 1.5 collective-permute-start.8
  143.4 36.7 %collective-permute-done.3 = bf16[8,128,128]{2,1,0:T(8,128)(2,1)S(1)} collective-permute-done((bf16[8,128,128]{2,1,0:T(8,128)(2,1)S(1)}, bf16[8,128,128]{2,1,0:T(8,128)(2,1)S(1)}, u32[]{:S(2)}, u32[]{:S(2)}) %collective-permute-start.3) | collective-permute-done | bytes 262176 | tf_op jit(solution)/shard_map/ppermute | solution.py:355
  180.1 1.0 select_convert_fusion.2
  181.1 0.3 collective-permute-start.4
  181.5 4.3 %collective-permute-done.8 = bf16[8,128,128]{2,1,0:T(8,128)(2,1)S(1)} collective-permute-done((bf16[8,128,128]{2,1,0:T(8,128)(2,1)S(1)}, bf16[8,128,128]{2,1,0:T(8,128)(2,1)S(1)}, u32[]{:S(2)}, u32[]{:S(2)}) %collective-permute-start.8) | collective-permute-done | bytes 262176 | tf_op jit(solution)/shard_map/ppermute | solution.py:355
  185.8 1.1 select_convert_fusion
  186.9 0.3 collective-permute-start.9
  187.2 0.6 reshape.307.gain_ref
  187.8 6.5 %intra.1.y_ref = f32[256,4096]{1,0:T(8,128)} custom-call(s32[1]{0:T(128)} %bitcast.place_ref, s32[16]{0:T(128)} %lengths_ref.3, f32[32]{0:T(128)} %skip_ref.1, f32[3,32,256]{2,1,0:T(8,128)} %get-tuple-element.19.rows_ref, f32[2,256,128]{2,1,0:T(8,128)} %get-tuple-element.18.columns_ref, bf16[256,2048]{1,0:T(8,128)(2,1)} %get-tuple-element.20.refs_0_, ...), custom_call_target="tpu_custom_call" | custom-call | tf_op jit(solution)/shard_map/intra/pallas_call | solution.py:489
  194.3 0.0 all-to-all-done
  194.3 0.0 collective-permute-done.4
  194.3 0.0 copy-start.3
  194.3 0.0 collective-permute-done.9
  194.3 1.6 copy-done
  195.9 0.1 copy-done.3
  196.0 7.4 %final.1 = bf16[256,4096]{1,0:T(8,128)(2,1)} custom-call(s32[1]{0:T(128)} %bitcast.place_ref, bf16[256,6144]{1,0:T(8,128)(2,1)} %bitcast.17, bf16[256,768]{1,0:T(8,128)(2,1)} %get-tuple-element.17.q_ref, f32[2,256,128]{2,1,0:T(8,128)} %get-tuple-element.18.columns_ref, f32[256,4096]{1,0:T(8,128)} %intra.1.y_ref, bf16[1,4096]{1,0:T(2,128)(2,1)} %reshape.307.gain_ref, ...), custom_call_target="tpu_custom_call" | custom-call | tf_op jit(solution)/shard_map/final/pallas_call | solution.py:512
  (11 shorter events, 0.0 us)
Async XLA Ops:
  5.0 85.0 %all-to-all-start.1 = ((bf16[32,8,7040]{2,1,0:T(8,128)(2,1)}), bf16[32,8,7040]{2,1,0:T(8,128)(2,1)}, u32[]{:S(2)}, u32[]{:S(2)}) async-start(bf16[32,8,7040]{2,1,0:T(8,128)(2,1)} %bitcast.16), calls=%async_computation.1 | async-start | bytes 7208960 | tf_op jit(solution)/shard_map/all_to_all | solution.py:136
  90.0 104.3 %all-to-all-start = ((bf16[32,8,6144]{2,1,0:T(8,128)(2,1)}), bf16[32,8,6144]{2,1,0:T(8,128)(2,1)S(1)}, u32[]{:S(2)}, u32[]{:S(2)}) async-start(bf16[32,8,6144]{2,1,0:T(8,128)(2,1)} %bitcast.18), calls=%async_computation | async-start | bytes 6291456 | tf_op jit(solution)/shard_map/all_to_all | solution.py:136
  102.6 7.0 %copy-start.2 = (bf16[1048,128]{1,0:T(8,128)(2,1)S(1)}, bf16[1048,128]{1,0:T(8,128)(2,1)}, u32[]{:S(2)}) copy-start(bf16[1048,128]{1,0:T(8,128)(2,1)} %get-tuple-element.26) | copy-start | bytes 804868
  102.6 28.1 %collective-permute-start = (bf16[1048,128]{1,0:T(8,128)(2,1)}, bf16[1048,128]{1,0:T(8,128)(2,1)S(1)}, u32[]{:S(2)}, u32[]{:S(2)}) collective-permute-start(bf16[1048,128]{1,0:T(8,128)(2,1)} %get-tuple-element.25), channel_id=1, source_target_pairs={{0,4},{4,0},{8,12},{12,8},{16,20},{20,16},{24,28},{28,24},{1,5},{5... | collective-permute-start | bytes 804872 | tf_op jit(solution)/shard_map/ppermute | solution.py:342
  107.7 30.3 %copy-start.1 = (bf16[1048,128]{1,0:T(8,128)(2,1)S(1)}, bf16[1048,128]{1,0:T(8,128)(2,1)}, u32[]{:S(2)}) copy-start(bf16[1048,128]{1,0:T(8,128)(2,1)} %get-tuple-element.28) | copy-start | bytes 804868
  108.5 29.5 %collective-permute-start.5 = (bf16[1048,128]{1,0:T(8,128)(2,1)}, bf16[1048,128]{1,0:T(8,128)(2,1)S(1)}, u32[]{:S(2)}, u32[]{:S(2)}) collective-permute-start(bf16[1048,128]{1,0:T(8,128)(2,1)} %get-tuple-element.27), channel_id=1, source_target_pairs={{0,4},{4,0},{8,12},{12,8},{16,20},{20,16},{24,28},{28,24},{1,5},{5... | collective-permute-start | bytes 804872 | tf_op jit(solution)/shard_map/ppermute | solution.py:342
  130.9 8.0 %collective-permute-start.1 = (bf16[8,128,128]{2,1,0:T(8,128)(2,1)S(1)}, bf16[8,128,128]{2,1,0:T(8,128)(2,1)S(1)}, u32[]{:S(2)}, u32[]{:S(2)}) collective-permute-start(bf16[8,128,128]{2,1,0:T(8,128)(2,1)S(1)} %get-tuple-element.37), channel_id=1, source_target_pairs={{0,8},{4,12},{1,9},{5,13},{2,10},{6,14},{3,11},{7,15}} | collective-permute-start | bytes 786440 | tf_op jit(solution)/shard_map/ppermute | solution.py:355
  138.2 1.5 collective-permute-start.6
  139.0 1.5 collective-permute-start.2
  139.8 47.4 %copy-start.4 = (bf16[4096]{0:T(1024)(128)(2,1)S(1)}, bf16[4096]{0:T(1024)(128)(2,1)}, u32[]{:S(2)}) copy-start(bf16[4096]{0:T(1024)(128)(2,1)} %param.19) | copy-start | bytes 24580
  139.8 2.1 %collective-permute-start.7 = (bf16[8,128,128]{2,1,0:T(8,128)(2,1)S(1)}, bf16[8,128,128]{2,1,0:T(8,128)(2,1)S(1)}, u32[]{:S(2)}, u32[]{:S(2)}) collective-permute-start(bf16[8,128,128]{2,1,0:T(8,128)(2,1)S(1)} %fusion.6), channel_id=1, source_target_pairs={{8,16},{12,20},{9,17},{13,21},{10,18},{14,22},{11,19},{15,23}} | collective-permute-start | bytes 786440 | tf_op jit(solution)/shard_map/ppermute | solution.py:355
  140.6 39.6 %collective-permute-start.3 = (bf16[8,128,128]{2,1,0:T(8,128)(2,1)S(1)}, bf16[8,128,128]{2,1,0:T(8,128)(2,1)S(1)}, u32[]{:S(2)}, u32[]{:S(2)}) collective-permute-start(bf16[8,128,128]{2,1,0:T(8,128)(2,1)S(1)} %fusion.4), channel_id=1, source_target_pairs={{16,24},{20,28},{17,25},{21,29},{18,26},{22,30},{19,27},{23,31}} | collective-permute-start | bytes 786440 | tf_op jit(solution)/shard_map/ppermute | solution.py:355
  141.9 43.9 %collective-permute-start.8 = (bf16[8,128,128]{2,1,0:T(8,128)(2,1)S(1)}, bf16[8,128,128]{2,1,0:T(8,128)(2,1)S(1)}, u32[]{:S(2)}, u32[]{:S(2)}) collective-permute-start(bf16[8,128,128]{2,1,0:T(8,128)(2,1)S(1)} %fusion.9), channel_id=1, source_target_pairs={{16,24},{20,28},{17,25},{21,29},{18,26},{22,30},{19,27},{23,31}} | collective-permute-start | bytes 786440 | tf_op jit(solution)/shard_map/ppermute | solution.py:355
  181.1 13.2 %collective-permute-start.4 = (bf16[8,128,128]{2,1,0:T(8,128)(2,1)}, bf16[8,128,128]{2,1,0:T(8,128)(2,1)S(1)}, u32[]{:S(2)}, u32[]{:S(2)}) collective-permute-start(bf16[8,128,128]{2,1,0:T(8,128)(2,1)} %get-tuple-element.41), channel_id=1, source_target_pairs={{0,4},{4,0},{8,12},{12,8},{16,20},{20,16},{24,28},{28,24},{1,5},{5... | collective-permute-start | bytes 786440 | tf_op jit(solution)/shard_map/ppermute | solution.py:361
  186.9 7.5 %collective-permute-start.9 = (bf16[8,128,128]{2,1,0:T(8,128)(2,1)}, bf16[8,128,128]{2,1,0:T(8,128)(2,1)}, u32[]{:S(2)}, u32[]{:S(2)}) collective-permute-start(bf16[8,128,128]{2,1,0:T(8,128)(2,1)} %get-tuple-element.39), channel_id=1, source_target_pairs={{0,4},{4,0},{8,12},{12,8},{16,20},{20,16},{24,28},{28,24},{1,5},{5... | collective-permute-start | bytes 786440 | tf_op jit(solution)/shard_map/ppermute | solution.py:361
  194.3 1.6 copy-start
  194.3 1.7 copy-start.3

commit v4 on v3

--- a/solution.py
+++ b/solution.py
@@ -29,7 +29,7 @@
     return jnp.where(mask, 1.0, 0.0).astype(BF16)
 
 
-def send_onehots(anchor, owners, block_rows, over):
+def send_onehots(anchor, turn, owners, block_rows, over):
     rows = anchor.shape[1]
     owner = jnp.zeros_like(anchor)
     for k in range(1, owners):
@@ -42,7 +42,7 @@
     place = (anchor - owner * block_rows + 1).astype(F32)
     place_col = jnp.sum(jnp.where(eye, place, 0.0), axis=1, keepdims=True)
     slot = iota((owners * ROWS, rows), 0)
-    first = owner * ROWS + rank
+    first = (owner ^ turn) * ROWS + rank
     base = onehot((slot == first) & (rank < ROWS))
     if not over:
         return base, None, None, place_col
@@ -51,23 +51,30 @@
     return base, low, high, place_col
 
 
-def pack_kernel(dims, small, anchor_ref, wide_ref, *refs):
+def pack_kernel(dims, small, *refs):
     owners, _, block_rows, over, groups, width, heads = dims
-    out_ref, base_ref, extra_ref, place_ref = refs[-4:]
+    place_ref = None if small else refs[0]
+    anchor_ref, wide_ref, *refs = refs if small else refs[1:]
+    out_ref, base_ref, extra_ref, spot_ref = refs[-4:]
     load_rows = wide_ref.shape[0]
 
     @pl.when(pl.program_id(0) == 0)
     def _():
-        base, low, high, place_col = send_onehots(anchor_ref[...], owners, block_rows, over)
+        turn = jnp.int32(0) if small else place_ref[0]
+        base, low, high, place_col = send_onehots(anchor_ref[...], turn, owners, block_rows, over)
         base_ref[...] = base
-        place_ref[...] = jnp.broadcast_to(place_col, place_ref.shape)
+        spot_ref[...] = jnp.broadcast_to(place_col, spot_ref.shape)
         if over:
             extra_ref[:, 0:load_rows] = low
             extra_ref[:, load_rows:] = high
 
     def put(column, values):
         values = values.astype(BF16).reshape(owners, ROWS, values.shape[1])
-        out_ref[:, 0, :, column : column + values.shape[2]] = values
+        to = slice(column, column + values.shape[2])
+        if small:
+            out_ref[:, 0, :, to] = values
+        else:
+            out_ref[0, :, :, to] = values
 
     def folded(low, high):
         return dot(extra_ref[...], jnp.concatenate([low, high], axis=0))
@@ -90,7 +97,7 @@
     for k in range(LANES // heads):
         shifted = steps if k == 0 else pltpu.roll(steps, LANES - k * heads, 1)
         own = own + jnp.where(pl.program_id(0) == k, shifted, 0.0)
-    meta = jnp.where(lane < heads, own, jnp.where(lane == heads, place_ref[...], 0.0))
+    meta = jnp.where(lane < heads, own, jnp.where(lane == heads, spot_ref[...], 0.0))
     put(column, dot(base_ref[...], jnp.concatenate([b_part, c_part], axis=1)))
     column += 2 * b_part.shape[1]
     tile = dot(base_ref[...], meta.astype(BF16))
@@ -102,34 +109,41 @@
         put(column + LANES, folded(b_part, c_part))
 
 
-def pack(anchor, wide, smalls, dims):
+def pack(place, anchor, wide, smalls, dims):
     owners, columns, _, over, groups, width, _ = dims
     load_rows = wide.shape[0]
     total = groups * (width * 3 // 2 if over else width)
     if smalls:
         total += LANES * (groups * (3 if over else 2) + 1)
+        grouped, block, index = (owners, columns), (owners, 1), lambda i, *p: (0, i, 0, 0)
+        column = lambda i, *p: (0, i)
+    else:
+        grouped, block, index = (columns, owners), (1, owners), lambda i, p: (i, 0, 0, 0)
+        column = lambda i, p: (0, i ^ p[1])
     in_specs = [
-        pl.BlockSpec((1, load_rows), lambda i: (0, 0)),
-        pl.BlockSpec((load_rows, groups * width), lambda i: (0, i)),
+        pl.BlockSpec((1, load_rows), lambda i, *p: (0, 0)),
+        pl.BlockSpec((load_rows, groups * width), column),
     ]
     if smalls:
-        in_specs += [pl.BlockSpec((load_rows, groups * LANES), lambda i: (0, i))] * 2
-        in_specs += [pl.BlockSpec((load_rows, LANES), lambda i: (0, 0))]
-    packed = pl.pallas_call(
+        in_specs += [pl.BlockSpec((load_rows, groups * LANES), column)] * 2
+        in_specs += [pl.BlockSpec((load_rows, LANES), lambda i, *p: (0, 0))]
+    return pl.pallas_call(
         functools.partial(pack_kernel, dims, bool(smalls)),
-        grid=(columns,),
-        in_specs=in_specs,
-        out_specs=pl.BlockSpec((owners, 1, ROWS, total), lambda i: (0, i, 0, 0)),
-        out_shape=shape(owners, columns, ROWS, total),
-        scratch_shapes=[
-            pltpu.VMEM((owners * ROWS, load_rows), BF16),
-            pltpu.VMEM((owners * ROWS, 2 * load_rows), BF16),
-            pltpu.VMEM((load_rows, LANES), F32),
-        ],
+        grid_spec=pltpu.PrefetchScalarGridSpec(
+            num_scalar_prefetch=len(place),
+            grid=(columns,),
+            in_specs=in_specs,
+            out_specs=pl.BlockSpec(block + (ROWS, total), index),
+            scratch_shapes=[
+                pltpu.VMEM((owners * ROWS, load_rows), BF16),
+                pltpu.VMEM((owners * ROWS, 2 * load_rows), BF16),
+                pltpu.VMEM((load_rows, LANES), F32),
+            ],
+        ),
+        out_shape=shape(*grouped, ROWS, total),
         compiler_params=PARAMS,
         name="pack",
-    )(anchor, wide, *smalls)
-    return packed.reshape(owners * columns, ROWS, total)
+    )(*place, anchor, wide, *smalls)
 
 
 def exchange(values, axes):
@@ -151,15 +165,36 @@
     return jnp.sum(jnp.where(eye, row, 0.0), axis=1, keepdims=True)
 
 
-def placed(q_ref, values_ref, over, width):
-    slots = values_ref.shape[0]
+def placed(q_ref, values_refs, over, width):
+    slots = sum(ref.shape[0] for ref in values_refs)
     half = width // 2
+
+    def part(k):
+        pieces = [ref[:, k * half : (k + 1) * half] for ref in values_refs]
+        return pieces[0] if len(pieces) == 1 else jnp.concatenate(pieces, axis=0)
+
     if not over:
-        return dot(q_ref[...], values_ref[:, 0:half]), dot(q_ref[...], values_ref[:, half:width])
-    extra = values_ref[:, width : width + half]
-    first = jnp.concatenate([extra, values_ref[:, 0:half]], axis=0)
-    second = jnp.concatenate([values_ref[:, half:width], extra], axis=0)
+        return dot(q_ref[...], part(0)), dot(q_ref[...], part(1))
+    extra = part(2)
+    first = jnp.concatenate([extra, part(0)], axis=0)
+    second = jnp.concatenate([part(1), extra], axis=0)
     return dot(q_ref[:, 0 : 2 * slots], first), dot(q_ref[:, slots : 3 * slots], second)
+
+
+def find(q_ref, meta, block_rows, over, heads):
+    slots = meta.shape[0]
+    turned = meta.T
+    target = iota((block_rows, slots), 0) + 1
+    own = onehot(target == turned[heads : heads + 1, :].astype(jnp.int32))
+    if not over:
+        q_ref[...] = own
+        return
+    half = ROWS // 2
+    inside = iota((1, slots), 1) % ROWS
+    spot = jnp.where(inside < half, turned[LANES // 2 + heads : LANES // 2 + heads + 1, :], 0.0)
+    q_ref[:, 0:slots] = onehot(target == spot.astype(jnp.int32))
+    q_ref[:, slots : 2 * slots] = own
+    q_ref[:, 2 * slots :] = onehot(target == pltpu.roll(spot, half, 1).astype(jnp.int32))
 
 
 def land(dims, part, side, q_ref, wide_ref, small_ref, rows_ref, decay_ref, refs):
@@ -179,7 +214,7 @@
         c_all = dot(q_ref[...], c_slots)
     bc_ref[0] = b_all.astype(BF16)
     bc_ref[1] = c_all.astype(BF16)
-    first, second = placed(q_ref, wide_ref, over, width)
+    first, second = placed(q_ref, [wide_ref], over, width)
     x_ref[:, 0 : width // 2] = first.astype(BF16)
     x_ref[:, width // 2 :] = second.astype(BF16)
     b_turned = b_all.T
@@ -226,6 +261,7 @@
     bias_ref,
     rate_ref,
     q_ref,
+    turned_q_ref,
     rows_ref,
     columns_ref,
     decay_ref,
@@ -235,28 +271,29 @@
     offer_ref,
     wide_ref,
     small_ref,
+    meta_ref,
     sems,
 ):
-    _, _, block_rows, over, groups, _, heads = dims
+    owners, columns, block_rows, over, groups, _, heads = dims
     slots = arrived_ref.shape[0]
     wide = fetch(arrived_ref, wide_ref.shape[1], 0, dims, wide_ref, small_ref, sems)
     meta = small_ref[:, 2 * groups * LANES : (2 * groups + 1) * LANES]
-    turned = meta.astype(F32).T
-    target = iota((block_rows, slots), 0) + 1
-    own = onehot(target == turned[heads : heads + 1, :].astype(jnp.int32))
-    raw = dot(own, meta).T[0:heads, :]
+    meta_ref[0] = meta.astype(F32)
+    find(q_ref, meta_ref[0], block_rows, over, heads)
+
+    def move(i, carry):
+        loader = (place_ref[0] ^ (i // columns)) * columns + (place_ref[1] ^ (i % columns))
+        to = pl.multiple_of(i * ROWS, ROWS)
+        meta_ref[1, pl.ds(to, ROWS), :] = meta_ref[0, pl.ds(pl.multiple_of(loader * ROWS, ROWS), ROWS), :]
+        return carry
+
+    lax.fori_loop(0, owners * columns, move, 0)
+    find(turned_q_ref, meta_ref[1], block_rows, over, heads)
     if over:
-        half = ROWS // 2
-        inside = iota((1, slots), 1) % ROWS
-        spot = jnp.where(inside < half, turned[LANES // 2 + heads : LANES // 2 + heads + 1, :], 0.0)
-        low = onehot(target == spot.astype(jnp.int32))
-        high = onehot(target == pltpu.roll(spot, half, 1).astype(jnp.int32))
-        q_ref[:, 0:slots] = low
-        q_ref[:, slots : 2 * slots] = own
-        q_ref[:, 2 * slots :] = high
-        raw = raw + dot(low, meta).T[LANES // 2 : LANES // 2 + heads, :]
+        raw = dot(q_ref[:, slots : 2 * slots], meta).T[0:heads, :]
+        raw = raw + dot(q_ref[:, 0:slots], meta).T[LANES // 2 : LANES // 2 + heads, :]
     else:
-        q_ref[...] = own
+        raw = dot(q_ref[...], meta).T[0:heads, :]
     raw = raw + column_of(bias_ref[...])
     step = jnp.maximum(raw, 0.0) + jnp.log1p(jnp.exp(-jnp.abs(raw)))
     logs = -step * jnp.exp(column_of(rate_ref[...]))
@@ -362,7 +399,8 @@
     return kept.reshape(half * LANES, LANES), other.reshape(half * LANES, LANES)
 
 
-def final_kernel(over, groups, place_ref, arrived_ref, q_ref, columns_ref, y_ref, gain_ref, *refs):
+def final_kernel(over, groups, place_ref, q_ref, columns_ref, y_ref, gain_ref, *refs):
+    arrived_refs = refs[3 * groups : -2]
     out_ref, gated_ref = refs[-2:]
     block_rows, width = out_ref.shape
     per_group = width // LANES
@@ -370,7 +408,7 @@
 
     def one(part):
         bc_ref, keep_ref, got_ref = refs[3 * part : 3 * part + 3]
-        first, second = placed(q_ref, arrived_ref, over, width)
+        first, second = placed(q_ref, arrived_refs, over, width)
         gated_ref[:, 0 : width // 2] = first
         gated_ref[:, width // 2 :] = second
         c_rows = bc_ref[0]
@@ -429,12 +467,22 @@
     finds = 3 if over else 1
     anchor = anchor.reshape(1, load_rows)
     number = lax.axis_index("ctx").astype(jnp.int32)
-    place = number.reshape(1)
-
-    sent = pack(anchor, x_load, (b_load, c_load, dt_load), dims)
+    place = jnp.stack([number, lax.axis_index("head").astype(jnp.int32)])
+
+    sent = pack((), anchor, x_load, (b_load, c_load, dt_load), dims)
+    sent = sent.reshape(owners * columns, ROWS, sent.shape[3])
     arrived_x = exchange(sent, BOTH).reshape(slots, sent.shape[2])
-    sent_z = pack(anchor, z_load, (), dims)
-    arrived_z = exchange(sent_z, BOTH).reshape(slots, sent_z.shape[2])
+    sent_z = pack((place,), anchor, z_load, (), dims)
+    gathered = [sent_z[0]]
+    for k in range(1, columns):
+        hops = [(i, i ^ k) for i in range(columns)]
+        gathered.append(lax.ppermute(sent_z[k], "head", hops))
+    arrived_z = []
+    for k in range(owners):
+        piece = jnp.concatenate([a[k] for a in gathered], axis=0)
+        if k > 0:
+            piece = lax.ppermute(piece, "ctx", [(i, i ^ k) for i in range(owners)])
+        arrived_z.append(piece)
 
     stride = width * 3 // 2 if over else width
     carried = (per_group // 2) * (LANES + 3)
@@ -453,18 +501,19 @@
     blocks, states = [], []
     for part in range(groups):
         if part == 0:
-            finder, rows, turned, decay, x_block, both, keep, offer = pl.pallas_call(
+            (finder, finder_z, rows, turned, decay, x_block, both, keep, offer) = pl.pallas_call(
                 functools.partial(first_kernel, dims),
                 in_specs=[SMEM, SMEM, anywhere, VMEM, VMEM],
-                out_specs=[VMEM] * 8,
+                out_specs=[VMEM] * 9,
                 out_shape=(
+                    shape(block_rows, finds * slots),
                     shape(block_rows, finds * slots),
                     shape(3, heads, block_rows, dtype=F32),
                     shape(2, block_rows, LANES, dtype=F32),
                     shape(heads, LANES, dtype=F32),
                 )
                 + per_part,
-                scratch_shapes=scratch,
+                scratch_shapes=scratch[:2] + [pltpu.VMEM((2, slots, LANES), F32)] + scratch[2:],
                 compiler_params=PARAMS,
                 name="land_first",
             )(
@@ -499,8 +548,7 @@
     second = pl.BlockSpec((1, block_rows, LANES), lambda i: (1, 0, 0))
     in_specs = [
         SMEM,
-        pl.BlockSpec((slots, stride), lambda i: (0, i)),
-        full(finder),
+        full(finder_z),
         second,
         pl.BlockSpec((block_rows, width), lambda i: (0, i)),
         pl.BlockSpec((1, width), lambda i: (0, i)),
@@ -509,6 +557,9 @@
     for part in range(groups):
         operands += [blocks[2 * part + 1], *states[part]]
         in_specs += [second, full(states[part][0]), full(states[part][1])]
+    for piece in arrived_z:
+        operands.append(piece)
+        in_specs.append(pl.BlockSpec((piece.shape[0], stride), lambda i: (0, i)))
     return pl.pallas_call(
         functools.partial(final_kernel, over, groups),
         grid=(groups,),
@@ -518,7 +569,7 @@
         scratch_shapes=[pltpu.VMEM((block_rows, width), F32)],
         compiler_params=PARAMS,
         name="final",
-    )(place, arrived_z, finder, turned, y, norm_gain.reshape(1, groups * width), *operands)
+    )(place, finder_z, turned, y, norm_gain.reshape(1, groups * width), *operands)
 
 
 def solution(mesh):

time: 207 us -> 217 us (1.048)
  the two profiles are of different devices: /device:TPU:27 before, /device:TPU:13 now
where the time goes in v4:
time: 217 us; the launch traced here: 216 us
  waiting for transfers between devices  131 us (60%)
  starting transfers between devices  35.8 us (16%)
  Pallas kernels  34.2 us (16%)
  local copies, waits for them, and re-layouts  7.17 us (3%)
  other arithmetic  7.11 us (3%)
    ppermute x3, waiting for transfers between devices, body(): gathered.append(lax.ppermute(sent_z[k], 'head', hops))  47 us
    ppermute x7, waiting for transfers between devices, body(): piece = lax.ppermute(piece, 'ctx', [(i, i ^ k) for i in range(owners)])  46.9 us
    all_to_all x1, waiting for transfers between devices, exchange(): return lax.all_to_all(values, axes, split_axis=0, concat_axis=0, tiled=True)  23.5 us
    ppermute x7, starting transfers between devices, body(): piece = lax.ppermute(piece, 'ctx', [(i, i ^ k) for i in range(owners)])  14.9 us
    pallas_call x2, Pallas kernels, pack(): pl.pallas_call(functools.partial(pack_kernel, dims, bool(smalls)), grid_s...  10.6 us
    ppermute x6, waiting for transfers between devices, enter(): come = lax.ppermute(sent, 'ctx', hops).astype(F32)  7.92 us
    pallas_call x1, Pallas kernels, body(): pl.pallas_call(functools.partial(final_kernel, over, groups), grid=(group...  7.18 us
    ppermute x6, starting transfers between devices, enter(): come = lax.ppermute(sent, 'ctx', hops).astype(F32)  6.73 us
  transfers between devices with their start and end apart: 21, of which 11 were waited for; matrix products, arithmetic and copies ran while one was open for 5% of the time, Pallas kernels for 10%

profile of v4, /device:TPU:13, one launch (start us, length us, event | category | flops | bytes accessed | tf_op | source)
XLA Modules:
  0.0 216.1 jit_solution(11448984775000827230)
XLA Ops:
  0.0 0.6 pad_add_fusion.place_ref.refs_0_
  0.6 5.6 %pack.3 = bf16[4,8,8,6144]{3,2,1,0:T(8,128)(2,1)} custom-call(s32[2]{0:T(128)} %pad_add_fusion.place_ref.refs_0_, s32[1,64]{1,0:T(1,128)} %bitcast.96, bf16[64,16384]{1,0:T(8,128)(2,1)} %refs_2_.3), custom_call_target="tpu_custom_call" | custom-call | tf_op jit(solution)/shard_map/pack/pallas_call | solution.py:130
  6.2 1.8 slice_bitcast_fusion.2
  7.9 0.7 collective-permute-start.10
  8.7 0.2 collective-permute-start.12
  8.9 1.2 collective-permute-start.11
  10.1 5.0 %pack.2 = bf16[8,4,8,7040]{3,2,1,0:T(8,128)(2,1)} custom-call(s32[1,64]{1,0:T(1,128)} %bitcast.97, bf16[64,16384]{1,0:T(8,128)(2,1)} %refs_1_.1, bf16[64,1024]{1,0:T(8,128)(2,1)} %refs_2_.2, bf16[64,1024]{1,0:T(8,128)(2,1)} %refs_3_.1, bf16[64,128]{1,0:T(8,128)(2,1)} %refs_4_.1), custom_call_target="tpu_custom_call" | custom-call | tf_op jit(solution)/shard_map/pack/pallas_call | solution.py:130
  15.1 6.3 %all-to-all-start = ((bf16[32,8,7040]{2,1,0:T(8,128)(2,1)}), bf16[32,8,7040]{2,1,0:T(8,128)(2,1)}, u32[]{:S(2)}, u32[]{:S(2)}) async-start(bf16[32,8,7040]{2,1,0:T(8,128)(2,1)} %bitcast.85), calls=%async_computation | async-start | bytes 7208960 | tf_op jit(solution)/shard_map/all_to_all | solution.py:150
  21.5 0.6 reshape.311.gain_ref
  22.1 1.3 slice_bitcast_fusion.6
  23.4 1.3 slice_bitcast_fusion.5
  24.7 17.5 %collective-permute-done.12 = bf16[8,8,6144]{2,1,0:T(8,128)(2,1)} collective-permute-done((bf16[8,8,6144]{2,1,0:T(8,128)(2,1)S(1)}, bf16[8,8,6144]{2,1,0:T(8,128)(2,1)}, u32[]{:S(2)}, u32[]{:S(2)}) %collective-permute-start.12) | collective-permute-done | bytes 786464 | tf_op jit(solution)/shard_map/ppermute | solution.py:479
  42.2 1.3 slice_bitcast_fusion.3
  43.5 29.5 %collective-permute-done.11 = bf16[8,8,6144]{2,1,0:T(8,128)(2,1)S(1)} collective-permute-done((bf16[8,8,6144]{2,1,0:T(8,128)(2,1)S(1)}, bf16[8,8,6144]{2,1,0:T(8,128)(2,1)S(1)}, u32[]{:S(2)}, u32[]{:S(2)}) %collective-permute-start.11) | collective-permute-done | bytes 786464 | tf_op jit(solution)/shard_map/ppermute | solution.py:479
  73.0 0.8 pad_maximum_fusion.1
  73.8 0.5 collective-permute-start.13
  74.3 0.8 pad_maximum_fusion.2
  75.1 0.9 collective-permute-start.14
  76.1 0.8 pad_maximum_fusion.3
  76.9 1.2 collective-permute-start.15
  78.2 23.5 %all-to-all-done = bf16[32,8,7040]{2,1,0:T(8,128)(2,1)} async-done(((bf16[32,8,7040]{2,1,0:T(8,128)(2,1)}), bf16[32,8,7040]{2,1,0:T(8,128)(2,1)}, u32[]{:S(2)}, u32[]{:S(2)}) %all-to-all-start) | async-done | bytes 3604512 | tf_op jit(solution)/shard_map/all_to_all | solution.py:150
  101.7 5.3 %land_first.1 = (bf16[256,768]{1,0:T(8,128)(2,1)}, bf16[256,768]{1,0:T(8,128)(2,1)}, f32[3,32,256]{2,1,0:T(8,128)}, f32[2,256,128]{2,1,0:T(8,128)}, f32[32,128]{...) custom-call(s32[2]{0:T(128)} %pad_add_fusion.place_ref.refs_0_, ...), custom_call_target="tpu_custom_call" | custom-call | tf_op jit(solution)/shard_map/land_first/pallas_call | solution.py:504
  107.0 2.4 %collective-permute-start = (bf16[1048,128]{1,0:T(8,128)(2,1)}, bf16[1048,128]{1,0:T(8,128)(2,1)S(1)}, u32[]{:S(2)}, u32[]{:S(2)}) collective-permute-start(bf16[1048,128]{1,0:T(8,128)(2,1)} %get-tuple-element.27), channel_id=1, source_target_pairs={{0,4},{4,0},{8,12},{12,8},{16,20},{20,16},{24,28},{28,24},{1,5},{5... | collective-permute-start | bytes 804872 | tf_op jit(solution)/shard_map/ppermute | solution.py:379
  109.4 4.7 %land_later.1 = (bf16[256,2048]{1,0:T(8,128)(2,1)}, bf16[2,256,128]{2,1,0:T(8,128)(2,1)}, bf16[1048,128]{1,0:T(8,128)(2,1)}, bf16[1048,128]{1,0:T(8,128)(2,1)}) custom-call(s32[2]{0:T(128)} %pad_add_fusion.place_ref.refs_0_, bf16[256,7040]{1,0:T(8,128)(2,1)} %bitcast.4.arrived_ref, bf16[256,768]{1,0:T(8,128)(2,1)} %get-tuple-element.23.q_ref, ...), custom_call_target="tpu_custom_call" | custom-call | tf_op jit(solution)/shard_map/land_later/pallas_call | solution.py:527
  114.1 0.8 slice_convert_fusion.2
  114.9 1.1 collective-permute-done
  116.2 1.3 collective-permute-start.1
  117.5 4.9 %collective-permute-done.5 = bf16[1048,128]{1,0:T(8,128)(2,1)S(1)} collective-permute-done((bf16[1048,128]{1,0:T(8,128)(2,1)}, bf16[1048,128]{1,0:T(8,128)(2,1)S(1)}, u32[]{:S(2)}, u32[]{:S(2)}) %collective-permute-start.5) | collective-permute-done | bytes 268320 | tf_op jit(solution)/shard_map/ppermute | solution.py:379
  122.5 1.3 collective-permute-start.6
  123.8 1.1 collective-permute-done.1
  125.0 1.3 collective-permute-start.2
  126.3 4.4 %collective-permute-done.6 = bf16[8,128,128]{2,1,0:T(8,128)(2,1)S(1)} collective-permute-done((bf16[8,128,128]{2,1,0:T(8,128)(2,1)S(1)}, bf16[8,128,128]{2,1,0:T(8,128)(2,1)S(1)}, u32[]{:S(2)}, u32[]{:S(2)}) %collective-permute-start.6) | collective-permute-done | bytes 262176 | tf_op jit(solution)/shard_map/ppermute | solution.py:392
  130.8 1.3 collective-permute-start.7
  132.2 0.7 collective-permute-start.3
  132.9 2.5 %collective-permute-done.7 = bf16[8,128,128]{2,1,0:T(8,128)(2,1)S(1)} collective-permute-done((bf16[8,128,128]{2,1,0:T(8,128)(2,1)S(1)}, bf16[8,128,128]{2,1,0:T(8,128)(2,1)S(1)}, u32[]{:S(2)}, u32[]{:S(2)}) %collective-permute-start.7) | collective-permute-done | bytes 262176 | tf_op jit(solution)/shard_map/ppermute | solution.py:392
  135.4 0.9 collective-permute-start.8
  136.3 0.9 select_convert_fusion.2
  137.2 9.6 %collective-permute-start.17 = (bf16[32,6144]{1,0:T(8,128)(2,1)S(1)}, bf16[32,6144]{1,0:T(8,128)(2,1)S(1)}, u32[]{:S(2)}, u32[]{:S(2)}) collective-permute-start(bf16[32,6144]{1,0:T(8,128)(2,1)S(1)} %pad_maximum_fusion.5), channel_id=1, source_target_pairs={{0,20},{4,16},{8,28},{12,24},{16,4},{20,0},{24,12},{28,8},{1,21},{... | collective-permute-start | bytes 1179656 | tf_op jit(solution)/shard_map/ppermute | solution.py:484
  146.8 0.9 select_convert_fusion
  147.7 2.6 %collective-permute-start.19 = (bf16[32,6144]{1,0:T(8,128)(2,1)S(1)}, bf16[32,6144]{1,0:T(8,128)(2,1)S(1)}, u32[]{:S(2)}, u32[]{:S(2)}) collective-permute-start(bf16[32,6144]{1,0:T(8,128)(2,1)S(1)} %pad_maximum_fusion.7), channel_id=1, source_target_pairs={{0,28},{4,24},{8,20},{12,16},{16,12},{20,8},{24,4},{28,0},{1,29},{... | collective-permute-start | bytes 1179656 | tf_op jit(solution)/shard_map/ppermute | solution.py:484
  150.4 26.4 %collective-permute-done.16.refs_10_ = bf16[32,6144]{1,0:T(8,128)(2,1)S(1)} collective-permute-done((bf16[32,6144]{1,0:T(8,128)(2,1)S(1)}, bf16[32,6144]{1,0:T(8,128)(2,1)S(1)}, u32[]{:S(2)}, u32[]{:S(2)}) %collective-permute-start.16) | collective-permute-done | bytes 393248 | tf_op jit(solution)/shard_map/ppermute | solution.py:484
  176.8 3.3 %collective-permute-start.9 = (bf16[8,128,128]{2,1,0:T(8,128)(2,1)S(1)}, bf16[8,128,128]{2,1,0:T(8,128)(2,1)S(1)}, u32[]{:S(2)}, u32[]{:S(2)}) collective-permute-start(bf16[8,128,128]{2,1,0:T(8,128)(2,1)S(1)} %get-tuple-element.52), channel_id=1, source_target_pairs={{0,4},{4,0},{8,12},{12,8},{16,20},{20,16},{24,28},{28,24},{1,5},{5... | collective-permute-start | bytes 786440 | tf_op jit(solution)/shard_map/ppermute | solution.py:398
  180.1 0.8 pad_maximum_fusion.refs_6_
  180.8 6.4 %intra.1.y_ref = f32[256,4096]{1,0:T(8,128)} custom-call(s32[2]{0:T(128)} %pad_add_fusion.place_ref.refs_0_, s32[16]{0:T(128)} %lengths_ref.3, f32[32]{0:T(128)} %skip_ref.1, f32[3,32,256]{2,1,0:T(8,128)} %get-tuple-element.20.rows_ref, f32[2,256,128]{2,1,0:T(8,128)} %get-tuple-element.19.columns_ref, bf16[256,2048]{1,0:T(8,128)(2,1)} %get-tuple-element.21.refs_0_, ...), custom_call_target="tpu_custom_call" | custom-call | tf_op jit(solution)/shard_map/intra/pallas_call | solution.py:538
  187.3 6.4 %collective-permute-done.18.refs_12_ = bf16[32,6144]{1,0:T(8,128)(2,1)S(1)} collective-permute-done((bf16[32,6144]{1,0:T(8,128)(2,1)S(1)}, bf16[32,6144]{1,0:T(8,128)(2,1)S(1)}, u32[]{:S(2)}, u32[]{:S(2)}) %collective-permute-start.18) | collective-permute-done | bytes 393248 | tf_op jit(solution)/shard_map/ppermute | solution.py:484
  193.8 14.1 %collective-permute-done.19.refs_13_ = bf16[32,6144]{1,0:T(8,128)(2,1)S(1)} collective-permute-done((bf16[32,6144]{1,0:T(8,128)(2,1)S(1)}, bf16[32,6144]{1,0:T(8,128)(2,1)S(1)}, u32[]{:S(2)}, u32[]{:S(2)}) %collective-permute-start.19) | collective-permute-done | bytes 393248 | tf_op jit(solution)/shard_map/ppermute | solution.py:484
  207.9 0.8 copy-done.6
  208.8 7.2 %final.1 = bf16[256,4096]{1,0:T(8,128)(2,1)} custom-call(s32[2]{0:T(128)} %pad_add_fusion.place_ref.refs_0_, bf16[256,768]{1,0:T(8,128)(2,1)} %get-tuple-element.18.q_ref, f32[2,256,128]{2,1,0:T(8,128)} %get-tuple-element.19.columns_ref, f32[256,4096]{1,0:T(8,128)} %intra.1.y_ref, bf16[1,4096]{1,0:T(2,128)(2,1)} %reshape.311.gain_ref, ...), custom_call_target="tpu_custom_call" | custom-call | tf_op jit(solution)/shard_map/final/pallas_call | solution.py:563
  (57 shorter events, 1.1 us)
Async XLA Ops:
  7.9 15.4 %collective-permute-start.10 = (bf16[8,8,6144]{2,1,0:T(8,128)(2,1)S(1)}, bf16[8,8,6144]{2,1,0:T(8,128)(2,1)}, u32[]{:S(2)}, u32[]{:S(2)}) collective-permute-start(bf16[8,8,6144]{2,1,0:T(8,128)(2,1)S(1)} %get-tuple-element.49), channel_id=1, source_target_pairs={{0,1},{1,0},{2,3},{3,2},{4,5},{5,4},{6,7},{7,6},{8,9},{9,8},{10,11... | collective-permute-start | bytes 2359304 | tf_op jit(solution)/shard_map/ppermute | solution.py:479
  8.7 33.5 %collective-permute-start.12 = (bf16[8,8,6144]{2,1,0:T(8,128)(2,1)S(1)}, bf16[8,8,6144]{2,1,0:T(8,128)(2,1)}, u32[]{:S(2)}, u32[]{:S(2)}) collective-permute-start(bf16[8,8,6144]{2,1,0:T(8,128)(2,1)S(1)} %get-tuple-element.50), channel_id=1, source_target_pairs={{0,3},{1,2},{2,1},{3,0},{4,7},{5,6},{6,5},{7,4},{8,11},{9,10},{10,... | collective-permute-start | bytes 2359304 | tf_op jit(solution)/shard_map/ppermute | solution.py:479
  8.9 64.1 %collective-permute-start.11 = (bf16[8,8,6144]{2,1,0:T(8,128)(2,1)S(1)}, bf16[8,8,6144]{2,1,0:T(8,128)(2,1)S(1)}, u32[]{:S(2)}, u32[]{:S(2)}) collective-permute-start(bf16[8,8,6144]{2,1,0:T(8,128)(2,1)S(1)} %get-tuple-element.51), channel_id=1, source_target_pairs={{0,2},{1,3},{2,0},{3,1},{4,6},{5,7},{6,4},{7,5},{8,10},{9,11},{10,... | collective-permute-start | bytes 2359304 | tf_op jit(solution)/shard_map/ppermute | solution.py:479
  15.1 6.4 %copy-start.11 = (bf16[4096]{0:T(1024)(128)(2,1)S(1)}, bf16[4096]{0:T(1024)(128)(2,1)}, u32[]{:S(2)}) copy-start(bf16[4096]{0:T(1024)(128)(2,1)} %param.19) | copy-start | bytes 24580
  15.1 86.5 %all-to-all-start = ((bf16[32,8,7040]{2,1,0:T(8,128)(2,1)}), bf16[32,8,7040]{2,1,0:T(8,128)(2,1)}, u32[]{:S(2)}, u32[]{:S(2)}) async-start(bf16[32,8,7040]{2,1,0:T(8,128)(2,1)} %bitcast.85), calls=%async_computation | async-start | bytes 7208960 | tf_op jit(solution)/shard_map/all_to_all | solution.py:150
  73.8 73.9 %collective-permute-start.13 = (bf16[32,6144]{1,0:T(8,128)(2,1)}, bf16[32,6144]{1,0:T(8,128)(2,1)S(1)}, u32[]{:S(2)}, u32[]{:S(2)}) collective-permute-start(bf16[32,6144]{1,0:T(8,128)(2,1)} %pad_maximum_fusion.1), channel_id=1, source_target_pairs={{0,4},{4,0},{8,12},{12,8},{16,20},{20,16},{24,28},{28,24},{1,5},{5... | collective-permute-start | bytes 1179656 | tf_op jit(solution)/shard_map/ppermute | solution.py:484
  75.1 72.6 %collective-permute-start.14 = (bf16[32,6144]{1,0:T(8,128)(2,1)}, bf16[32,6144]{1,0:T(8,128)(2,1)S(1)}, u32[]{:S(2)}, u32[]{:S(2)}) collective-permute-start(bf16[32,6144]{1,0:T(8,128)(2,1)} %pad_maximum_fusion.2), channel_id=1, source_target_pairs={{0,8},{4,12},{8,0},{12,4},{16,24},{20,28},{24,16},{28,20},{1,9},{5... | collective-permute-start | bytes 1179656 | tf_op jit(solution)/shard_map/ppermute | solution.py:484
  76.9 73.5 %collective-permute-start.15 = (bf16[32,6144]{1,0:T(8,128)(2,1)}, bf16[32,6144]{1,0:T(8,128)(2,1)S(1)}, u32[]{:S(2)}, u32[]{:S(2)}) collective-permute-start(bf16[32,6144]{1,0:T(8,128)(2,1)} %pad_maximum_fusion.3), channel_id=1, source_target_pairs={{0,12},{4,8},{8,4},{12,0},{16,28},{20,24},{24,20},{28,16},{1,13},{... | collective-permute-start | bytes 1179656 | tf_op jit(solution)/shard_map/ppermute | solution.py:484
  107.0 7.9 %copy-start.8 = (bf16[1048,128]{1,0:T(8,128)(2,1)S(1)}, bf16[1048,128]{1,0:T(8,128)(2,1)}, u32[]{:S(2)}) copy-start(bf16[1048,128]{1,0:T(8,128)(2,1)} %get-tuple-element.28) | copy-start | bytes 804868
  107.0 8.9 %collective-permute-start = (bf16[1048,128]{1,0:T(8,128)(2,1)}, bf16[1048,128]{1,0:T(8,128)(2,1)S(1)}, u32[]{:S(2)}, u32[]{:S(2)}) collective-permute-start(bf16[1048,128]{1,0:T(8,128)(2,1)} %get-tuple-element.27), channel_id=1, source_target_pairs={{0,4},{4,0},{8,12},{12,8},{16,20},{20,16},{24,28},{28,24},{1,5},{5... | collective-permute-start | bytes 804872 | tf_op jit(solution)/shard_map/ppermute | solution.py:379
  114.1 8.3 %copy-start.7 = (bf16[1048,128]{1,0:T(8,128)(2,1)S(1)}, bf16[1048,128]{1,0:T(8,128)(2,1)}, u32[]{:S(2)}) copy-start(bf16[1048,128]{1,0:T(8,128)(2,1)} %get-tuple-element.30) | copy-start | bytes 804868
  114.8 7.5 %collective-permute-start.5 = (bf16[1048,128]{1,0:T(8,128)(2,1)}, bf16[1048,128]{1,0:T(8,128)(2,1)S(1)}, u32[]{:S(2)}, u32[]{:S(2)}) collective-permute-start(bf16[1048,128]{1,0:T(8,128)(2,1)} %get-tuple-element.29), channel_id=1, source_target_pairs={{0,4},{4,0},{8,12},{12,8},{16,20},{20,16},{24,28},{28,24},{1,5},{5... | collective-permute-start | bytes 804872 | tf_op jit(solution)/shard_map/ppermute | solution.py:379
  116.2 8.7 %collective-permute-start.1 = (bf16[8,128,128]{2,1,0:T(8,128)(2,1)S(1)}, bf16[8,128,128]{2,1,0:T(8,128)(2,1)S(1)}, u32[]{:S(2)}, u32[]{:S(2)}) collective-permute-start(bf16[8,128,128]{2,1,0:T(8,128)(2,1)S(1)} %get-tuple-element.39), channel_id=1, source_target_pairs={{0,8},{4,12},{1,9},{5,13},{2,10},{6,14},{3,11},{7,15}} | collective-permute-start | bytes 786440 | tf_op jit(solution)/shard_map/ppermute | solution.py:392
  122.5 8.2 %collective-permute-start.6 = (bf16[8,128,128]{2,1,0:T(8,128)(2,1)S(1)}, bf16[8,128,128]{2,1,0:T(8,128)(2,1)S(1)}, u32[]{:S(2)}, u32[]{:S(2)}) collective-permute-start(bf16[8,128,128]{2,1,0:T(8,128)(2,1)S(1)} %get-tuple-element.34), channel_id=1, source_target_pairs={{0,8},{4,12},{1,9},{5,13},{2,10},{6,14},{3,11},{7,15}} | collective-permute-start | bytes 786440 | tf_op jit(solution)/shard_map/ppermute | solution.py:392
  125.0 7.1 %collective-permute-start.2 = (bf16[8,128,128]{2,1,0:T(8,128)(2,1)S(1)}, bf16[8,128,128]{2,1,0:T(8,128)(2,1)S(1)}, u32[]{:S(2)}, u32[]{:S(2)}) collective-permute-start(bf16[8,128,128]{2,1,0:T(8,128)(2,1)S(1)} %fusion.1), channel_id=1, source_target_pairs={{8,16},{12,20},{9,17},{13,21},{10,18},{14,22},{11,19},{15,23}} | collective-permute-start | bytes 786440 | tf_op jit(solution)/shard_map/ppermute | solution.py:392
  130.8 4.6 %collective-permute-start.7 = (bf16[8,128,128]{2,1,0:T(8,128)(2,1)S(1)}, bf16[8,128,128]{2,1,0:T(8,128)(2,1)S(1)}, u32[]{:S(2)}, u32[]{:S(2)}) collective-permute-start(bf16[8,128,128]{2,1,0:T(8,128)(2,1)S(1)} %fusion.6), channel_id=1, source_target_pairs={{8,16},{12,20},{9,17},{13,21},{10,18},{14,22},{11,19},{15,23}} | collective-permute-start | bytes 786440 | tf_op jit(solution)/shard_map/ppermute | solution.py:392
  132.2 3.3 %collective-permute-start.3 = (bf16[8,128,128]{2,1,0:T(8,128)(2,1)S(1)}, bf16[8,128,128]{2,1,0:T(8,128)(2,1)S(1)}, u32[]{:S(2)}, u32[]{:S(2)}) collective-permute-start(bf16[8,128,128]{2,1,0:T(8,128)(2,1)S(1)} %fusion.4), channel_id=1, source_target_pairs={{16,24},{20,28},{17,25},{21,29},{18,26},{22,30},{19,27},{23,31}} | collective-permute-start | bytes 786440 | tf_op jit(solution)/shard_map/ppermute | solution.py:392
  135.4 41.4 %collective-permute-start.16 = (bf16[32,6144]{1,0:T(8,128)(2,1)S(1)}, bf16[32,6144]{1,0:T(8,128)(2,1)S(1)}, u32[]{:S(2)}, u32[]{:S(2)}) collective-permute-start(bf16[32,6144]{1,0:T(8,128)(2,1)S(1)} %pad_maximum_fusion.4), channel_id=1, source_target_pairs={{0,16},{4,20},{8,24},{12,28},{16,0},{20,4},{24,8},{28,12},{1,17},{... | collective-permute-start | bytes 1179656 | tf_op jit(solution)/shard_map/ppermute | solution.py:484
  135.4 1.8 collective-permute-start.8
  137.2 50.1 %collective-permute-start.17 = (bf16[32,6144]{1,0:T(8,128)(2,1)S(1)}, bf16[32,6144]{1,0:T(8,128)(2,1)S(1)}, u32[]{:S(2)}, u32[]{:S(2)}) collective-permute-start(bf16[32,6144]{1,0:T(8,128)(2,1)S(1)} %pad_maximum_fusion.5), channel_id=1, source_target_pairs={{0,20},{4,16},{8,28},{12,24},{16,4},{20,0},{24,12},{28,8},{1,21},{... | collective-permute-start | bytes 1179656 | tf_op jit(solution)/shard_map/ppermute | solution.py:484
  147.7 39.6 %copy-start = (bf16[32,6144]{1,0:T(8,128)(2,1)}, bf16[32,6144]{1,0:T(8,128)(2,1)S(1)}, u32[]{:S(2)}) copy-start(bf16[32,6144]{1,0:T(8,128)(2,1)S(1)} %collective-permute-done.13.refs_7_) | copy-start | bytes 1179652
  147.7 46.1 %collective-permute-start.18 = (bf16[32,6144]{1,0:T(8,128)(2,1)S(1)}, bf16[32,6144]{1,0:T(8,128)(2,1)S(1)}, u32[]{:S(2)}, u32[]{:S(2)}) collective-permute-start(bf16[32,6144]{1,0:T(8,128)(2,1)S(1)} %pad_maximum_fusion.6), channel_id=1, source_target_pairs={{0,24},{4,28},{8,16},{12,20},{16,8},{20,12},{24,0},{28,4},{1,25},{... | collective-permute-start | bytes 1179656 | tf_op jit(solution)/shard_map/ppermute | solution.py:484
  147.7 39.6 %copy-start.1 = (bf16[32,6144]{1,0:T(8,128)(2,1)}, bf16[32,6144]{1,0:T(8,128)(2,1)S(1)}, u32[]{:S(2)}) copy-start(bf16[32,6144]{1,0:T(8,128)(2,1)S(1)} %collective-permute-done.14.refs_8_) | copy-start | bytes 1179652
  147.7 60.1 %collective-permute-start.19 = (bf16[32,6144]{1,0:T(8,128)(2,1)S(1)}, bf16[32,6144]{1,0:T(8,128)(2,1)S(1)}, u32[]{:S(2)}, u32[]{:S(2)}) collective-permute-start(bf16[32,6144]{1,0:T(8,128)(2,1)S(1)} %pad_maximum_fusion.7), channel_id=1, source_target_pairs={{0,28},{4,24},{8,20},{12,16},{16,12},{20,8},{24,4},{28,0},{1,29},{... | collective-permute-start | bytes 1179656 | tf_op jit(solution)/shard_map/ppermute | solution.py:484
  150.4 36.9 %copy-start.2 = (bf16[32,6144]{1,0:T(8,128)(2,1)}, bf16[32,6144]{1,0:T(8,128)(2,1)S(1)}, u32[]{:S(2)}) copy-start(bf16[32,6144]{1,0:T(8,128)(2,1)S(1)} %collective-permute-done.15.refs_9_) | copy-start | bytes 1179652
  150.4 57.5 %collective-permute-start.4 = (bf16[8,128,128]{2,1,0:T(8,128)(2,1)S(1)}, bf16[8,128,128]{2,1,0:T(8,128)(2,1)S(1)}, u32[]{:S(2)}, u32[]{:S(2)}) collective-permute-start(bf16[8,128,128]{2,1,0:T(8,128)(2,1)S(1)} %get-tuple-element.54), channel_id=1, source_target_pairs={{0,4},{4,0},{8,12},{12,8},{16,20},{20,16},{24,28},{28,24},{1,5},{5... | collective-permute-start | bytes 786440 | tf_op jit(solution)/shard_map/ppermute | solution.py:398
  176.8 10.5 %copy-start.3 = (bf16[32,6144]{1,0:T(8,128)(2,1)}, bf16[32,6144]{1,0:T(8,128)(2,1)S(1)}, u32[]{:S(2)}) copy-start(bf16[32,6144]{1,0:T(8,128)(2,1)S(1)} %collective-permute-done.16.refs_10_) | copy-start | bytes 1179652
  176.8 31.1 %collective-permute-start.9 = (bf16[8,128,128]{2,1,0:T(8,128)(2,1)S(1)}, bf16[8,128,128]{2,1,0:T(8,128)(2,1)S(1)}, u32[]{:S(2)}, u32[]{:S(2)}) collective-permute-start(bf16[8,128,128]{2,1,0:T(8,128)(2,1)S(1)} %get-tuple-element.52), channel_id=1, source_target_pairs={{0,4},{4,0},{8,12},{12,8},{16,20},{20,16},{24,28},{28,24},{1,5},{5... | collective-permute-start | bytes 786440 | tf_op jit(solution)/shard_map/ppermute | solution.py:398
  187.3 20.5 %copy-start.4 = (bf16[32,6144]{1,0:T(8,128)(2,1)}, bf16[32,6144]{1,0:T(8,128)(2,1)S(1)}, u32[]{:S(2)}) copy-start(bf16[32,6144]{1,0:T(8,128)(2,1)S(1)} %collective-permute-done.17.refs_11_) | copy-start | bytes 1179652
  193.8 14.1 %copy-start.5 = (bf16[32,6144]{1,0:T(8,128)(2,1)}, bf16[32,6144]{1,0:T(8,128)(2,1)S(1)}, u32[]{:S(2)}) copy-start(bf16[32,6144]{1,0:T(8,128)(2,1)S(1)} %collective-permute-done.18.refs_12_) | copy-start | bytes 1179652
  207.8 0.8 copy-start.6
  207.8 0.9 copy-start.9
  207.8 0.9 copy-start.10
